TPU v7x, 256 devices: a whole 4x4x8 slice. The times are simulated.
256 devices in a mesh: cuts: 16 (over z_lo, y, core), col: 16 (over z_hi, x).
Axes of the slice: x: 4, y: 4, z: 8 (z_hi: 4, z_lo: 2; z = z_hi * 2 + z_lo), core: 2. Of those that a mesh axis runs over, the one named last changes fastest.
Arguments:
- data: bfloat16 [16, 64, 64, 1024], P('cuts', None, 'col'), may hold values from -12 to 12
- weights: float32 [16, 64], replicated, may hold values from 0.5 to 2
- mixing: float32 [64, 64], replicated, may hold values from -0.4 to 2.9
Outputs:
- factor: float32 [64, 64, 1024], P(None, 'col')
- updated: float32 [16, 64], P('cuts')
All inputs are finite; a program needn't handle non-finite values.
Results may differ from a plain program's by a relative error of at most 0.0029.
Values sent between devices are 32-bit elements; how exact they have to be, the bound alone decides.
A program may use at most 64 MiB of HBM per device.

v0:
```python
import jax
import jax.numpy as jnp
from jax import lax
from jax.sharding import PartitionSpec as P

GRID = 32
ITERS = 3


strength = 0.5
highest = lax.Precision.HIGHEST
low_edge = 1.0
high_edge = 1.0 + 12.0 * strength
centre = (high_edge + low_edge) / 2.0
spread = (high_edge - low_edge) / 2.0


def extended_2(cells, sides, width):
    for axis, dim in sides:
        count = lax.axis_size(axis)
        ends = count - 1
        head = lax.slice_in_dim(cells, 0, width, axis=dim)
        tail = lax.slice_in_dim(cells, cells.shape[dim] - width, cells.shape[dim], axis=dim)
        cells = jnp.concatenate(
            [
                lax.ppermute(tail, axis, [(i, (i + 1) % count) for i in range(ends)]),
                cells,
                lax.ppermute(head, axis, [((i + 1) % count, i) for i in range(ends)]),
            ],
            axis=dim,
        )
    return cells


def split_up(shard, dim, devices):
    before, after = (shard.shape[:dim], shard.shape[dim + 1 :])
    return jnp.moveaxis(shard.reshape(*before, devices, -1, *after), dim, 0)


def sent_and_summed(shard, axis, dim):
    tiles = split_up(shard, dim, lax.axis_size(axis))
    arrived = lax.all_to_all(tiles, axis, split_axis=0, concat_axis=0, tiled=True)
    return arrived.sum(axis=0)


def joined_along(tiles, dim):
    dims = list(tiles.shape[1:])
    dims[dim] *= tiles.shape[0]
    return jnp.moveaxis(tiles, 0, dim).reshape(dims)


def from_everyone(shard, axis):
    devices = lax.axis_size(axis)
    return lax.all_to_all(
        jnp.broadcast_to(shard[None], (devices, *shard.shape)), axis, 0, 0, tiled=True
    )


def gather_directly(shard, axis, dim):
    return joined_along(from_everyone(shard, axis), dim)


def taken_together(shard, axis):
    return from_everyone(shard, axis).sum(axis=0)


def packed_total(arrays, axis):
    line, at, done = (jnp.concatenate([a.reshape(-1) for a in arrays]), 0, [])
    running = taken_together(line, axis)
    for a in arrays:
        done.append(running[at : at + a.size].reshape(a.shape))
        at += a.size
    return tuple(done)


def operate(extended):
    channels, depth, cells = extended.shape
    edge = GRID
    interior = extended[:, 1:-1]
    column = jnp.arange(cells, dtype=jnp.int32) % edge
    has_left = (column > 0).astype(jnp.float32)
    has_right = (column < edge - 1).astype(jnp.float32)
    left_part = jnp.pad(interior, ((0, 0), (0, 0), (1, 0)))[:, :, :-1] * has_left
    right_part = jnp.pad(interior, ((0, 0), (0, 0), (0, 1)))[:, :, 1:] * has_right
    upper_part = jnp.pad(interior, ((0, 0), (0, 0), (edge, 0)))[:, :, :-edge]
    lower_part = jnp.pad(interior, ((0, 0), (0, 0), (0, edge)))[:, :, edge:]
    neighbours = extended[:, 2:] + extended[:, :-2]
    neighbours = neighbours + left_part + right_part + upper_part + lower_part
    return interior + strength * (6.0 * interior - neighbours)


def smooth_once(source):
    planes = source.shape[1]
    extended = extended_2(source, (("col", 1),), ITERS)
    first_plane = lax.axis_index("col") * planes - ITERS
    total_planes = planes * lax.axis_size("col")
    levels = first_plane + jnp.arange(planes + 2 * ITERS, dtype=jnp.int32)
    inside = ((levels >= 0) & (levels < total_planes)).astype(jnp.float32)[None, :, None]
    solution = jnp.zeros_like(source)
    residual = extended
    direction = extended / centre
    ratio = spread / centre
    for iteration in range(ITERS):
        margin = ITERS - iteration
        solution = solution + direction[:, margin : margin + planes]
        window = inside[:, iteration + 1 : iteration + 1 + planes + 2 * (margin - 1)]
        residual = (residual[:, 1:-1] - operate(direction)) * window
        ratio_next = 1.0 / (2.0 * centre / spread - ratio)
        direction = ratio_next * ratio * direction[:, 1:-1] + 2.0 * ratio_next / spread * residual
        ratio = ratio_next
    return solution + direction


def smooth(source):
    return smooth_once(source)


def per_device(data, weights, mixing):
    local_scans, ranks, planes, cells = data.shape
    mix_gram = jnp.dot(mixing.T, mixing, precision=highest)
    weight_gram = jnp.dot(weights.T, weights, precision=highest)
    lower_factor = jnp.linalg.cholesky(mix_gram * weight_gram)
    own_weights = lax.dynamic_slice_in_dim(
        weights, lax.axis_index("cuts") * local_scans, local_scans, 0
    )
    scaled = (mixing[None, :, :] * own_weights[:, None, :]).reshape(local_scans * ranks, ranks)
    coefficients = jax.scipy.linalg.cho_solve((lower_factor, True), scaled.T).T.astype(jnp.bfloat16)
    stacked = data.reshape(local_scans * ranks, planes * cells)
    portion = sent_and_summed(
        lax.dot_general(
            coefficients, stacked, (((0,), (0,)), ((), ())), preferred_element_type=jnp.float32
        ),
        "cuts",
        0,
    )
    smoothed = smooth(portion.reshape(-1, planes, cells))
    factor = gather_directly(smoothed, "cuts", 0)
    factor_flat = factor.reshape(ranks, planes * cells)
    factor_half = factor_flat.astype(jnp.bfloat16)
    factor_gram = jnp.dot(factor_flat, factor_flat.T, precision=highest)
    products = lax.dot_general(
        data.reshape(local_scans, ranks, planes * cells),
        factor_half,
        (((2,), (1,)), ((), ())),
        preferred_element_type=jnp.float32,
    )
    factor_gram, products = packed_total((factor_gram, products), "col")
    targets = jnp.sum(mixing[None, :, :] * products, axis=1)
    lower_next = jnp.linalg.cholesky(mix_gram * factor_gram)
    updated = jax.scipy.linalg.cho_solve((lower_next, True), targets.T).T
    return (factor, updated)


def solution(mesh):
    return jax.shard_map(
        per_device,
        mesh=mesh,
        in_specs=(P("cuts", None, "col", None), P(), P()),
        out_specs=(P(None, "col", None), P("cuts", None)),
        check_vma=False,
    )
```

profile of v0, /device:TPU:24, one launch (start us, length us, event | category | flops | bytes accessed | tf_op | source)
XLA Modules:
  0.0 120.8 jit_solution(15113444038105301408)
XLA Ops:
  0.7 1.1 fusion.60
  2.1 5.8 %cholesky.44 = f32[64,64]{1,0:T(8,128)S(1)} custom-call(f32[64,64]{1,0:T(8,128)S(1)} %fusion.43), custom_call_target="Cholesky" | custom-call | tf_op jit(solution)/shard_map/jit(cholesky)/cholesky | solution.py:122
  8.0 0.6 compare_reduce_fusion.1
  8.6 0.7 fusion.34
  9.3 4.9 %custom-call.16 = f32[1,64,64]{1,2,0:T(8,128)S(1)} custom-call(f32[1,64,64]{2,1,0:T(8,128)S(1)} %fusion.34), custom_call_target="InvertDiagBlocksLowerTriangular" | custom-call | tf_op jit(solution)/shard_map/jit(_cho_solve)/triangular_solve | solution.py:127
  14.2 1.0 fusion.41
  16.0 1.6 %copy.41 = f32[16,4,4096]{2,1,0:T(4,128)} copy(f32[16,4,4096]{2,0,1:T(8,128)S(1)} %fusion.45) | data formatting | bytes 2097152 | tf_op jit(solution)/shard_map/dot_general | solution.py:130
  17.7 6.1 %all-to-all-start = ((f32[16,4,4096]{2,1,0:T(4,128)}), f32[16,4,4096]{2,1,0:T(4,128)S(1)}, u32[]{:S(2)}, u32[]{:S(2)}) async-start(f32[16,4,4096]{2,1,0:T(4,128)} %copy.41), calls=%async_computation | async-start | bytes 2097152 | tf_op jit(solution)/shard_map/all_to_all | solution.py:42
  24.0 14.4 %all-to-all-done = f32[16,4,4096]{2,1,0:T(4,128)S(1)} async-done(((f32[16,4,4096]{2,1,0:T(4,128)}), f32[16,4,4096]{2,1,0:T(4,128)S(1)}, u32[]{:S(2)}, u32[]{:S(2)}) %all-to-all-start) | async-done | bytes 1048608 | tf_op jit(solution)/shard_map/all_to_all | solution.py:42
  38.7 3.4 %collective-permute-start = (f32[4,3,1024]{2,1,0:T(4,128)S(1)}, f32[4,3,1024]{2,1,0:T(4,128)S(1)}, u32[]{:S(2)}, u32[]{:S(2)}) collective-permute-start(f32[4,3,1024]{2,1,0:T(4,128)S(1)} %get-tuple-element.9), channel_id=1, source_target_pairs={{0,1},{1,2},{2,3},{3,4},{4,5},{5,6},{6,7},{7,8},{8,9},{9,10},{10,1... | collective-permute-start | bytes 147464 | tf_op jit(solution)/shard_map/ppermute | solution.py:26
  42.1 1.3 %collective-permute-start.1 = (f32[4,3,1024]{2,1,0:T(4,128)S(1)}, f32[4,3,1024]{2,1,0:T(4,128)S(1)}, u32[]{:S(2)}, u32[]{:S(2)}) collective-permute-start(f32[4,3,1024]{2,1,0:T(4,128)S(1)} %get-tuple-element.10), channel_id=1, source_target_pairs={{1,0},{2,1},{3,2},{4,3},{5,4},{6,5},{7,6},{8,7},{9,8},{10,9},{11,1... | collective-permute-start | bytes 147464 | tf_op jit(solution)/shard_map/ppermute | solution.py:28
  44.0 4.3 %collective-permute-done.1 = f32[4,3,1024]{2,1,0:T(4,128)S(1)} collective-permute-done((f32[4,3,1024]{2,1,0:T(4,128)S(1)}, f32[4,3,1024]{2,1,0:T(4,128)S(1)}, u32[]{:S(2)}, u32[]{:S(2)}) %collective-permute-start.1) | collective-permute-done | bytes 49184 | tf_op jit(solution)/shard_map/ppermute | solution.py:28
  49.1 1.2 %broadcast_in_dim.5 = f32[16,4,4,1024]{3,2,1,0:T(4,128)} broadcast(f32[4,4,1024]{2,1,0:T(4,128)S(1)} %fusion.33), dimensions={1,2,3} | broadcast | bytes 1114112 | tf_op jit(solution)/shard_map/broadcast_in_dim | solution.py:55
  50.3 5.4 %all-to-all-start.1 = ((f32[16,4,4,1024]{3,2,1,0:T(4,128)}), f32[16,4,4,1024]{3,2,1,0:T(4,128)S(1)}, u32[]{:S(2)}, u32[]{:S(2)}) async-start(f32[16,4,4,1024]{3,2,1,0:T(4,128)} %broadcast_in_dim.5), calls=%async_computation.1 | async-start | bytes 2097152 | tf_op jit(solution)/shard_map/all_to_all | solution.py:54
  55.9 14.5 %all-to-all-done.1 = f32[16,4,4,1024]{3,2,1,0:T(4,128)S(1)} async-done(((f32[16,4,4,1024]{3,2,1,0:T(4,128)}), f32[16,4,4,1024]{3,2,1,0:T(4,128)S(1)}, u32[]{:S(2)}, u32[]{:S(2)}) %all-to-all-start.1) | async-done | bytes 1048608 | tf_op jit(solution)/shard_map/all_to_all | solution.py:54
  71.9 1.0 fusion.61
  72.9 1.2 broadcast_in_dim.6
  74.1 13.8 %all-to-all-start.2 = ((f32[16,1,8192]{2,1,0:T(1,128)}), f32[16,1,8192]{2,1,0:T(1,128)S(1)}, u32[]{:S(2)}, u32[]{:S(2)}) async-start(f32[16,1,8192]{2,1,0:T(1,128)} %broadcast_in_dim.6), calls=%async_computation.2 | async-start | bytes 1048576 | tf_op jit(solution)/shard_map/all_to_all | solution.py:54
  87.9 18.3 %all-to-all-done.2 = f32[16,1,8192]{2,1,0:T(1,128)S(1)} async-done(((f32[16,1,8192]{2,1,0:T(1,128)}), f32[16,1,8192]{2,1,0:T(1,128)S(1)}, u32[]{:S(2)}, u32[]{:S(2)}) %all-to-all-start.2) | async-done | bytes 524320 | tf_op jit(solution)/shard_map/all_to_all | solution.py:54
  106.8 5.8 %cholesky.55 = f32[64,64]{1,0:T(8,128)S(1)} custom-call(f32[64,64]{1,0:T(8,128)S(1)} %fusion.39), custom_call_target="Cholesky" | custom-call | tf_op jit(solution)/shard_map/jit(cholesky)/cholesky | solution.py:149
  113.3 0.7 fusion.35
  114.0 4.9 %custom-call.17 = f32[1,64,64]{1,2,0:T(8,128)S(1)} custom-call(f32[1,64,64]{2,1,0:T(8,128)S(1)} %fusion.35), custom_call_target="InvertDiagBlocksLowerTriangular" | custom-call | tf_op jit(solution)/shard_map/jit(_cho_solve)/triangular_solve | solution.py:150
  119.2 0.7 fusion.36
  119.9 1.0 copy.58
  (51 shorter events, 6.2 us)
Async XLA Ops:
  0.6 1.1 copy-start
  0.6 14.7 %copy-start.1 = (bf16[1,64,4,1024]{3,2,1,0:T(4,128)(2,1)S(1)}, bf16[1,64,4,1024]{3,2,1,0:T(4,128)(2,1)}, u32[]{:S(2)}) copy-start(bf16[1,64,4,1024]{3,2,1,0:T(4,128)(2,1)} %param.4) | copy-start | bytes 1572868
  17.7 20.7 %all-to-all-start = ((f32[16,4,4096]{2,1,0:T(4,128)}), f32[16,4,4096]{2,1,0:T(4,128)S(1)}, u32[]{:S(2)}, u32[]{:S(2)}) async-start(f32[16,4,4096]{2,1,0:T(4,128)} %copy.41), calls=%async_computation | async-start | bytes 2097152 | tf_op jit(solution)/shard_map/all_to_all | solution.py:42
  38.7 5.3 %collective-permute-start = (f32[4,3,1024]{2,1,0:T(4,128)S(1)}, f32[4,3,1024]{2,1,0:T(4,128)S(1)}, u32[]{:S(2)}, u32[]{:S(2)}) collective-permute-start(f32[4,3,1024]{2,1,0:T(4,128)S(1)} %get-tuple-element.9), channel_id=1, source_target_pairs={{0,1},{1,2},{2,3},{3,4},{4,5},{5,6},{6,7},{7,8},{8,9},{9,10},{10,1... | collective-permute-start | bytes 147464 | tf_op jit(solution)/shard_map/ppermute | solution.py:26
  42.1 6.2 %collective-permute-start.1 = (f32[4,3,1024]{2,1,0:T(4,128)S(1)}, f32[4,3,1024]{2,1,0:T(4,128)S(1)}, u32[]{:S(2)}, u32[]{:S(2)}) collective-permute-start(f32[4,3,1024]{2,1,0:T(4,128)S(1)} %get-tuple-element.10), channel_id=1, source_target_pairs={{1,0},{2,1},{3,2},{4,3},{5,4},{6,5},{7,6},{8,7},{9,8},{10,9},{11,1... | collective-permute-start | bytes 147464 | tf_op jit(solution)/shard_map/ppermute | solution.py:28
  50.3 20.1 %all-to-all-start.1 = ((f32[16,4,4,1024]{3,2,1,0:T(4,128)}), f32[16,4,4,1024]{3,2,1,0:T(4,128)S(1)}, u32[]{:S(2)}, u32[]{:S(2)}) async-start(f32[16,4,4,1024]{3,2,1,0:T(4,128)} %broadcast_in_dim.5), calls=%async_computation.1 | async-start | bytes 2097152 | tf_op jit(solution)/shard_map/all_to_all | solution.py:54
  74.1 32.0 %all-to-all-start.2 = ((f32[16,1,8192]{2,1,0:T(1,128)}), f32[16,1,8192]{2,1,0:T(1,128)S(1)}, u32[]{:S(2)}, u32[]{:S(2)}) async-start(f32[16,1,8192]{2,1,0:T(1,128)} %broadcast_in_dim.6), calls=%async_computation.2 | async-start | bytes 1048576 | tf_op jit(solution)/shard_map/all_to_all | solution.py:54
  114.0 5.0 %copy-start.2 = (f32[64,64]{1,0:T(8,128)S(1)}, f32[64,64]{1,0:T(8,128)}, u32[]{:S(2)}) copy-start(f32[64,64]{1,0:T(8,128)} %param.6) | copy-start | bytes 49156
where the time goes:
time: 122 us; the launch traced here: 121 us
  waiting for transfers between devices  52.1 us (43%)
  starting transfers between devices  30 us (25%)
  other arithmetic  25.7 us (21%)
  local copies, waits for them, and re-layouts  7.37 us (6%)
  matrix products  4.83 us (4%)
    all_to_all x2, waiting for transfers between devices, from_everyone(): lax.all_to_all(jnp.broadcast_to(shard[None], (devices, *shard.shape)), ax...  32.8 us
    all_to_all x2, starting transfers between devices, from_everyone(): lax.all_to_all(jnp.broadcast_to(shard[None], (devices, *shard.shape)), ax...  19.2 us
    all_to_all x1, waiting for transfers between devices, sent_and_summed(): lax.all_to_all(tiles, axis, split_axis=0, concat_axis=0, tiled=True)  14.4 us
    another operation x3, other arithmetic, per_device(): lower_factor = jnp.linalg.cholesky(mix_gram * weight_gram)  6.52 us
    another operation x3, other arithmetic, per_device(): lower_next = jnp.linalg.cholesky(mix_gram * factor_gram)  6.52 us
    all_to_all x1, starting transfers between devices, sent_and_summed(): lax.all_to_all(tiles, axis, split_axis=0, concat_axis=0, tiled=True)  6.06 us
    another operation x2, other arithmetic, per_device(): updated = jax.scipy.linalg.cho_solve((lower_next, True), targets.T).T  5.55 us
    another operation x2, other arithmetic, per_device(): jax.scipy.linalg.cho_solve((lower_factor, True), scaled.T)  5.55 us
  transfers between devices with their start and end apart: 5, of which 5 were waited for; matrix products, arithmetic and copies ran while one was open for 0% of the time, Pallas kernels for 0%

commit v1 on v0

--- a/solution.py
+++ b/solution.py
@@ -126,15 +126,16 @@
     scaled = (mixing[None, :, :] * own_weights[:, None, :]).reshape(local_scans * ranks, ranks)
     coefficients = jax.scipy.linalg.cho_solve((lower_factor, True), scaled.T).T.astype(jnp.bfloat16)
     stacked = data.reshape(local_scans * ranks, planes * cells)
-    portion = sent_and_summed(
+    portion = lax.psum_scatter(
         lax.dot_general(
             coefficients, stacked, (((0,), (0,)), ((), ())), preferred_element_type=jnp.float32
         ),
         "cuts",
-        0,
+        scatter_dimension=0,
+        tiled=True,
     )
     smoothed = smooth(portion.reshape(-1, planes, cells))
-    factor = gather_directly(smoothed, "cuts", 0)
+    factor = lax.all_gather(smoothed, "cuts", axis=0, tiled=True)
     factor_flat = factor.reshape(ranks, planes * cells)
     factor_half = factor_flat.astype(jnp.bfloat16)
     factor_gram = jnp.dot(factor_flat, factor_flat.T, precision=highest)
@@ -144,8 +145,8 @@
         (((2,), (1,)), ((), ())),
         preferred_element_type=jnp.float32,
     )
-    factor_gram, products = packed_total((factor_gram, products), "col")
     targets = jnp.sum(mixing[None, :, :] * products, axis=1)
+    factor_gram, targets = lax.psum((factor_gram, targets), "col")
     lower_next = jnp.linalg.cholesky(mix_gram * factor_gram)
     updated = jax.scipy.linalg.cho_solve((lower_next, True), targets.T).T
     return (factor, updated)

time: 122 us -> 310 us (2.54)
  waiting for transfers between devices: 52.1 us -> 168 us
  blocking collectives: 0 us -> 82.2 us
  starting transfers between devices: 30 us -> 4.75 us
  between operations: 0.93 us -> 14.9 us
    unnamed x0 -> x3, waiting for transfers between devices: none -> 123 us
    psum x0 -> x1, blocking collectives: none -> 82.2 us  [per_device(): factor_gram, targets = lax.psum((factor_gram, targets), 'col')]
    all_to_all x3 -> x0, waiting for transfers between devices: 47.2 us -> none  [the longest x2 32.8 us: from_everyone(): lax.all_to_all(jnp.broadcast_to(shard[None], (devices, *shard.shape)), ax...]
    all_gather x0 -> x1, waiting for transfers between devices: none -> 40 us  [per_device(): factor = lax.all_gather(smoothed, 'cuts', axis=0, tiled=True)]
    all_to_all x3 -> x0, starting transfers between devices: 25.3 us -> none  [the longest x2 19.2 us: from_everyone(): lax.all_to_all(jnp.broadcast_to(shard[None], (devices, *shard.shape)), ax...]
    unnamed x10 -> x13, local copies, waits for them, and re-layouts: 1.93 us -> 5.28 us
  transfers between devices with their start and end apart: 5 -> 4, of which waited for: 5 -> 4; matrix products, arithmetic and copies ran while one was open for 0% -> 0% of each run, Pallas kernels for 0% -> 0%
where the time goes in v1:
time: 310 us; the launch traced here: 309 us
  waiting for transfers between devices  168 us (54%)
  blocking collectives  82.2 us (27%)
  other arithmetic  27 us (9%)
  between operations  14.9 us (5%)
  matrix products  6.25 us (2%)
  local copies, waits for them, and re-layouts  5.8 us (2%)
  starting transfers between devices  4.75 us (2%)
    unnamed x3, waiting for transfers between devices  123 us
    psum x1, blocking collectives, per_device(): factor_gram, targets = lax.psum((factor_gram, targets), 'col')  82.2 us
    all_gather x1, waiting for transfers between devices, per_device(): factor = lax.all_gather(smoothed, 'cuts', axis=0, tiled=True)  40 us
    another operation x3, other arithmetic, per_device(): lower_next = jnp.linalg.cholesky(mix_gram * factor_gram)  6.52 us
    another operation x3, other arithmetic, per_device(): lower_factor = jnp.linalg.cholesky(mix_gram * weight_gram)  6.52 us
  transfers between devices with their start and end apart: 4, of which 4 were waited for; matrix products, arithmetic and copies ran while one was open for 0% of the time, Pallas kernels for 0%

profile of v1, /device:TPU:24, one launch (start us, length us, event | category | flops | bytes accessed | tf_op | source)
XLA Modules:
  0.0 308.5 jit_solution(8941545026422105702)
XLA Ops:
  7.2 1.1 fusion.60
  8.7 5.8 %cholesky.44 = f32[64,64]{1,0:T(8,128)S(1)} custom-call(f32[64,64]{1,0:T(8,128)S(1)} %fusion.46), custom_call_target="Cholesky" | custom-call | tf_op jit(solution)/shard_map/jit(cholesky)/cholesky | solution.py:122
  15.2 0.7 fusion.37
  15.8 4.9 %custom-call.16 = f32[1,64,64]{1,2,0:T(8,128)S(1)} custom-call(f32[1,64,64]{2,1,0:T(8,128)S(1)} %fusion.37), custom_call_target="InvertDiagBlocksLowerTriangular" | custom-call | tf_op jit(solution)/shard_map/jit(_cho_solve)/triangular_solve | solution.py:127
  21.3 1.2 copy.38
  22.5 1.3 fusion.61
  23.9 0.7 copy-done.3
  26.0 122.8 %all-reduce.16.cloned.1.call-done = f32[64,4096]{1,0:T(8,128)} async-done(((f32[64,4096]{1,0:T(8,128)}), f32[64,4096]{1,0:T(8,128)}) %all-reduce.16.cloned.1.call-update) | async-done | bytes 1048592
  148.8 0.9 constant_dynamic-slice_fusion
  149.8 3.4 %collective-permute-start = (f32[4,3,1024]{2,1,0:T(4,128)S(1)}, f32[4,3,1024]{2,1,0:T(4,128)S(1)}, u32[]{:S(2)}, u32[]{:S(2)}) collective-permute-start(f32[4,3,1024]{2,1,0:T(4,128)S(1)} %get-tuple-element.15), channel_id=1, source_target_pairs={{0,1},{1,2},{2,3},{3,4},{4,5},{5,6},{6,7},{7,8},{8,9},{9,10},{10,1... | collective-permute-start | bytes 147464 | tf_op jit(solution)/shard_map/ppermute | solution.py:26
  153.2 1.3 collective-permute-start.1
  155.0 4.3 %collective-permute-done.1 = f32[4,3,1024]{2,1,0:T(4,128)S(1)} collective-permute-done((f32[4,3,1024]{2,1,0:T(4,128)S(1)}, f32[4,3,1024]{2,1,0:T(4,128)S(1)}, u32[]{:S(2)}, u32[]{:S(2)}) %collective-permute-start.1) | collective-permute-done | bytes 49184 | tf_op jit(solution)/shard_map/ppermute | solution.py:28
  159.9 0.9 fusion.36
  160.8 40.0 %all-gather.2.cloned.1.call-done = f32[64,4,1024]{2,1,0:T(4,128)} async-done(((f32[4,4,1024]{2,1,0:T(4,128)}), f32[64,4,1024]{2,1,0:T(4,128)}) %all-gather.2.cloned.1.call-update) | async-done | bytes 1048592 | tf_op jit(solution)/shard_map/all_gather | solution.py:138
  200.8 1.4 convert_element_type.73
  202.7 0.7 copy-done.1
  203.5 2.0 convolution_bitcast_fusion.1
  205.5 82.2 %all-reduce.13 = (f32[64,64]{0,1:T(8,128)S(1)}, f32[64]{0:T(128)S(1)}) all-reduce(f32[64,64]{0,1:T(8,128)S(1)} %convolution_bitcast_fusion.1, f32[64]{0:T(128)S(1)} %fusion.1), channel_id=1, replica_groups=mesh['cuts'=16,'col'=16] {'col'}, use_global_device_ids=true, to_apply=%region_3.5 | all-reduce | flops 4160 | bytes 33280 | tf_op jit(solution)/shard_map/psum | solution.py:149
  287.8 5.8 %cholesky.55 = f32[64,64]{1,0:T(8,128)S(1)} custom-call(f32[64,64]{1,0:T(8,128)S(1)} %fusion.42), custom_call_target="Cholesky" | custom-call | tf_op jit(solution)/shard_map/jit(cholesky)/cholesky | solution.py:150
  293.7 0.6 compare_reduce_fusion
  294.3 0.7 fusion.38
  295.0 4.9 %custom-call.17 = f32[1,64,64]{1,2,0:T(8,128)S(1)} custom-call(f32[1,64,64]{2,1,0:T(8,128)S(1)} %fusion.38), custom_call_target="InvertDiagBlocksLowerTriangular" | custom-call | tf_op jit(solution)/shard_map/jit(_cho_solve)/triangular_solve | solution.py:151
  300.0 0.7 fusion.39
  300.7 1.0 copy.44
  (40 shorter events, 4.4 us)
Async XLA Ops:
  7.2 1.1 copy-start
  7.2 141.6 %all-reduce.16.cloned.1.call-start = ((), (), s32[]{:S(2)}) async-start(), calls=%async_computation.1 | async-start | bytes 2097152
  15.2 5.6 %copy-start.2 = (f32[64,64]{1,0:T(8,128)S(1)}, f32[64,64]{1,0:T(8,128)}, u32[]{:S(2)}) copy-start(f32[64,64]{1,0:T(8,128)} %param.6) | copy-start | bytes 49156
  23.8 177.0 %all-gather.2.cloned.1.call-start = ((), (), s32[]{:S(2)}) async-start(), calls=%async_computation | async-start | bytes 1114112 | tf_op jit(solution)/shard_map/all_gather | solution.py:138
  23.8 0.7 copy-start.3
  149.8 5.3 %collective-permute-start = (f32[4,3,1024]{2,1,0:T(4,128)S(1)}, f32[4,3,1024]{2,1,0:T(4,128)S(1)}, u32[]{:S(2)}, u32[]{:S(2)}) collective-permute-start(f32[4,3,1024]{2,1,0:T(4,128)S(1)} %get-tuple-element.15), channel_id=1, source_target_pairs={{0,1},{1,2},{2,3},{3,4},{4,5},{5,6},{6,7},{7,8},{8,9},{9,10},{10,1... | collective-permute-start | bytes 147464 | tf_op jit(solution)/shard_map/ppermute | solution.py:26
  153.2 6.2 %collective-permute-start.1 = (f32[4,3,1024]{2,1,0:T(4,128)S(1)}, f32[4,3,1024]{2,1,0:T(4,128)S(1)}, u32[]{:S(2)}, u32[]{:S(2)}) collective-permute-start(f32[4,3,1024]{2,1,0:T(4,128)S(1)} %get-tuple-element.16), channel_id=1, source_target_pairs={{1,0},{2,1},{3,2},{4,3},{5,4},{6,5},{7,6},{8,7},{9,8},{10,9},{11,1... | collective-permute-start | bytes 147464 | tf_op jit(solution)/shard_map/ppermute | solution.py:28
  202.2 1.2 copy-start.1
Sparse Core Ops, SparseCore 0:
  23.9 124.8 all-reduce.15
  160.9 39.8 all-gather.1

commit v2 on v0

--- a/solution.py
+++ b/solution.py
@@ -144,8 +144,20 @@
         (((2,), (1,)), ((), ())),
         preferred_element_type=jnp.float32,
     )
-    factor_gram, products = packed_total((factor_gram, products), "col")
     targets = jnp.sum(mixing[None, :, :] * products, axis=1)
+    half = ranks // 2
+    row = lax.broadcasted_iota(jnp.int32, (half, half), 0)
+    col = lax.broadcasted_iota(jnp.int32, (half, half), 1)
+    top, off, low = (factor_gram[:half, :half], factor_gram[:half, half:], factor_gram[half:, half:])
+    folded = jnp.where(row >= col, top, low)
+    folded, off, low_diag, targets = packed_total(
+        (folded, off, jnp.sum(jnp.where(row == col, low, 0.0), axis=1), targets), "col"
+    )
+    top = jnp.where(row >= col, folded, folded.T)
+    low = jnp.where(row < col, folded, jnp.where(row > col, folded.T, low_diag[:, None]))
+    factor_gram = jnp.concatenate(
+        [jnp.concatenate([top, off], axis=1), jnp.concatenate([off.T, low], axis=1)], axis=0
+    )
     lower_next = jnp.linalg.cholesky(mix_gram * factor_gram)
     updated = jax.scipy.linalg.cho_solve((lower_next, True), targets.T).T
     return (factor, updated)

time: 122 us -> 116 us (0.951)
  waiting for transfers between devices: 52.1 us -> 44.7 us
  local copies, waits for them, and re-layouts: 7.37 us -> 8.9 us
    all_to_all x2, waiting for transfers between devices: 32.8 us -> 25.4 us  [from_everyone(): lax.all_to_all(jnp.broadcast_to(shard[None], (devices, *shard.shape)), ax...]
    unnamed x10 -> x14, local copies, waits for them, and re-layouts: 1.93 us -> 3.14 us
where the time goes in v2:
time: 116 us; the launch traced here: 115 us
  waiting for transfers between devices  44.7 us (39%)
  starting transfers between devices  30 us (26%)
  other arithmetic  25.6 us (22%)
  local copies, waits for them, and re-layouts  8.9 us (8%)
  matrix products  4.9 us (4%)
    all_to_all x2, waiting for transfers between devices, from_everyone(): lax.all_to_all(jnp.broadcast_to(shard[None], (devices, *shard.shape)), ax...  25.4 us
    all_to_all x2, starting transfers between devices, from_everyone(): lax.all_to_all(jnp.broadcast_to(shard[None], (devices, *shard.shape)), ax...  19.2 us
    all_to_all x1, waiting for transfers between devices, sent_and_summed(): lax.all_to_all(tiles, axis, split_axis=0, concat_axis=0, tiled=True)  14.4 us
    another operation x3, other arithmetic, per_device(): lower_factor = jnp.linalg.cholesky(mix_gram * weight_gram)  6.52 us
    another operation x3, other arithmetic, per_device(): lower_next = jnp.linalg.cholesky(mix_gram * factor_gram)  6.52 us
    all_to_all x1, starting transfers between devices, sent_and_summed(): lax.all_to_all(tiles, axis, split_axis=0, concat_axis=0, tiled=True)  6.06 us
    another operation x2, other arithmetic, per_device(): updated = jax.scipy.linalg.cho_solve((lower_next, True), targets.T).T  5.56 us
    another operation x2, other arithmetic, per_device(): jax.scipy.linalg.cho_solve((lower_factor, True), scaled.T)  5.55 us
  transfers between devices with their start and end apart: 5, of which 5 were waited for; matrix products, arithmetic and copies ran while one was open for 0% of the time, Pallas kernels for 0%

profile of v2, /device:TPU:24, one launch (start us, length us, event | category | flops | bytes accessed | tf_op | source)
XLA Modules:
  0.0 115.0 jit_solution(3218588735551453256)
XLA Ops:
  0.7 1.1 fusion.62
  2.1 5.8 %cholesky.44 = f32[64,64]{1,0:T(8,128)S(1)} custom-call(f32[64,64]{1,0:T(8,128)S(1)} %fusion.45), custom_call_target="Cholesky" | custom-call | tf_op jit(solution)/shard_map/jit(cholesky)/cholesky | solution.py:122
  8.0 0.6 compare_reduce_fusion.1
  8.6 0.7 fusion.36
  9.3 4.9 %custom-call.16 = f32[1,64,64]{1,2,0:T(8,128)S(1)} custom-call(f32[1,64,64]{2,1,0:T(8,128)S(1)} %fusion.36), custom_call_target="InvertDiagBlocksLowerTriangular" | custom-call | tf_op jit(solution)/shard_map/jit(_cho_solve)/triangular_solve | solution.py:127
  14.2 1.0 fusion.43
  16.0 1.6 %copy.52 = f32[16,4,4096]{2,1,0:T(4,128)} copy(f32[16,4,4096]{2,0,1:T(8,128)S(1)} %fusion.48) | data formatting | bytes 2097152 | tf_op jit(solution)/shard_map/dot_general | solution.py:130
  17.7 6.1 %all-to-all-start = ((f32[16,4,4096]{2,1,0:T(4,128)}), f32[16,4,4096]{2,1,0:T(4,128)S(1)}, u32[]{:S(2)}, u32[]{:S(2)}) async-start(f32[16,4,4096]{2,1,0:T(4,128)} %copy.52), calls=%async_computation | async-start | bytes 2097152 | tf_op jit(solution)/shard_map/all_to_all | solution.py:42
  24.0 14.4 %all-to-all-done = f32[16,4,4096]{2,1,0:T(4,128)S(1)} async-done(((f32[16,4,4096]{2,1,0:T(4,128)}), f32[16,4,4096]{2,1,0:T(4,128)S(1)}, u32[]{:S(2)}, u32[]{:S(2)}) %all-to-all-start) | async-done | bytes 1048608 | tf_op jit(solution)/shard_map/all_to_all | solution.py:42
  38.7 3.4 %collective-permute-start = (f32[4,3,1024]{2,1,0:T(4,128)S(1)}, f32[4,3,1024]{2,1,0:T(4,128)S(1)}, u32[]{:S(2)}, u32[]{:S(2)}) collective-permute-start(f32[4,3,1024]{2,1,0:T(4,128)S(1)} %get-tuple-element.9), channel_id=1, source_target_pairs={{0,1},{1,2},{2,3},{3,4},{4,5},{5,6},{6,7},{7,8},{8,9},{9,10},{10,1... | collective-permute-start | bytes 147464 | tf_op jit(solution)/shard_map/ppermute | solution.py:26
  42.1 1.3 %collective-permute-start.1 = (f32[4,3,1024]{2,1,0:T(4,128)S(1)}, f32[4,3,1024]{2,1,0:T(4,128)S(1)}, u32[]{:S(2)}, u32[]{:S(2)}) collective-permute-start(f32[4,3,1024]{2,1,0:T(4,128)S(1)} %get-tuple-element.10), channel_id=1, source_target_pairs={{1,0},{2,1},{3,2},{4,3},{5,4},{6,5},{7,6},{8,7},{9,8},{10,9},{11,1... | collective-permute-start | bytes 147464 | tf_op jit(solution)/shard_map/ppermute | solution.py:28
  44.0 4.3 %collective-permute-done.1 = f32[4,3,1024]{2,1,0:T(4,128)S(1)} collective-permute-done((f32[4,3,1024]{2,1,0:T(4,128)S(1)}, f32[4,3,1024]{2,1,0:T(4,128)S(1)}, u32[]{:S(2)}, u32[]{:S(2)}) %collective-permute-start.1) | collective-permute-done | bytes 49184 | tf_op jit(solution)/shard_map/ppermute | solution.py:28
  49.1 1.2 %broadcast_in_dim.13 = f32[16,4,4,1024]{3,2,1,0:T(4,128)} broadcast(f32[4,4,1024]{2,1,0:T(4,128)S(1)} %fusion.35), dimensions={1,2,3} | broadcast | bytes 1114112 | tf_op jit(solution)/shard_map/broadcast_in_dim | solution.py:55
  50.3 5.4 %all-to-all-start.1 = ((f32[16,4,4,1024]{3,2,1,0:T(4,128)}), f32[16,4,4,1024]{3,2,1,0:T(4,128)S(1)}, u32[]{:S(2)}, u32[]{:S(2)}) async-start(f32[16,4,4,1024]{3,2,1,0:T(4,128)} %broadcast_in_dim.13), calls=%async_computation.1 | async-start | bytes 2097152 | tf_op jit(solution)/shard_map/all_to_all | solution.py:54
  55.9 14.5 %all-to-all-done.1 = f32[16,4,4,1024]{3,2,1,0:T(4,128)S(1)} async-done(((f32[16,4,4,1024]{3,2,1,0:T(4,128)}), f32[16,4,4,1024]{3,2,1,0:T(4,128)S(1)}, u32[]{:S(2)}, u32[]{:S(2)}) %all-to-all-start.1) | async-done | bytes 1048608 | tf_op jit(solution)/shard_map/all_to_all | solution.py:54
  71.4 1.0 fusion.63
  73.8 0.7 broadcast_in_dim.15
  74.5 13.8 %all-to-all-start.2 = ((f32[16,1,2144]{2,1,0:T(1,128)}), f32[16,1,2144]{2,1,0:T(1,128)S(1)}, u32[]{:S(2)}, u32[]{:S(2)}) async-start(f32[16,1,2144]{2,1,0:T(1,128)} %broadcast_in_dim.15), calls=%async_computation.2 | async-start | bytes 278528 | tf_op jit(solution)/shard_map/all_to_all | solution.py:54
  88.3 10.9 %all-to-all-done.2 = f32[16,1,2144]{2,1,0:T(1,128)S(1)} async-done(((f32[16,1,2144]{2,1,0:T(1,128)}), f32[16,1,2144]{2,1,0:T(1,128)S(1)}, u32[]{:S(2)}, u32[]{:S(2)}) %all-to-all-start.2) | async-done | bytes 137248 | tf_op jit(solution)/shard_map/all_to_all | solution.py:54
  101.0 5.8 %cholesky.55 = f32[64,64]{1,0:T(8,128)S(1)} custom-call(f32[64,64]{1,0:T(8,128)S(1)} %fusion.41), custom_call_target="Cholesky" | custom-call | tf_op jit(solution)/shard_map/jit(cholesky)/cholesky | solution.py:161
  107.5 0.7 fusion.37
  108.2 4.9 %custom-call.17 = f32[1,64,64]{1,2,0:T(8,128)S(1)} custom-call(f32[1,64,64]{2,1,0:T(8,128)S(1)} %fusion.37), custom_call_target="InvertDiagBlocksLowerTriangular" | custom-call | tf_op jit(solution)/shard_map/jit(_cho_solve)/triangular_solve | solution.py:162
  113.3 0.7 fusion.38
  114.0 1.0 copy.74
  (60 shorter events, 8.2 us)
Async XLA Ops:
  0.6 1.1 copy-start
  0.6 14.7 %copy-start.1 = (bf16[1,64,4,1024]{3,2,1,0:T(4,128)(2,1)S(1)}, bf16[1,64,4,1024]{3,2,1,0:T(4,128)(2,1)}, u32[]{:S(2)}) copy-start(bf16[1,64,4,1024]{3,2,1,0:T(4,128)(2,1)} %param.4) | copy-start | bytes 1572868
  17.7 20.7 %all-to-all-start = ((f32[16,4,4096]{2,1,0:T(4,128)}), f32[16,4,4096]{2,1,0:T(4,128)S(1)}, u32[]{:S(2)}, u32[]{:S(2)}) async-start(f32[16,4,4096]{2,1,0:T(4,128)} %copy.52), calls=%async_computation | async-start | bytes 2097152 | tf_op jit(solution)/shard_map/all_to_all | solution.py:42
  38.7 5.3 %collective-permute-start = (f32[4,3,1024]{2,1,0:T(4,128)S(1)}, f32[4,3,1024]{2,1,0:T(4,128)S(1)}, u32[]{:S(2)}, u32[]{:S(2)}) collective-permute-start(f32[4,3,1024]{2,1,0:T(4,128)S(1)} %get-tuple-element.9), channel_id=1, source_target_pairs={{0,1},{1,2},{2,3},{3,4},{4,5},{5,6},{6,7},{7,8},{8,9},{9,10},{10,1... | collective-permute-start | bytes 147464 | tf_op jit(solution)/shard_map/ppermute | solution.py:26
  42.1 6.2 %collective-permute-start.1 = (f32[4,3,1024]{2,1,0:T(4,128)S(1)}, f32[4,3,1024]{2,1,0:T(4,128)S(1)}, u32[]{:S(2)}, u32[]{:S(2)}) collective-permute-start(f32[4,3,1024]{2,1,0:T(4,128)S(1)} %get-tuple-element.10), channel_id=1, source_target_pairs={{1,0},{2,1},{3,2},{4,3},{5,4},{6,5},{7,6},{8,7},{9,8},{10,9},{11,1... | collective-permute-start | bytes 147464 | tf_op jit(solution)/shard_map/ppermute | solution.py:28
  50.3 20.1 %all-to-all-start.1 = ((f32[16,4,4,1024]{3,2,1,0:T(4,128)}), f32[16,4,4,1024]{3,2,1,0:T(4,128)S(1)}, u32[]{:S(2)}, u32[]{:S(2)}) async-start(f32[16,4,4,1024]{3,2,1,0:T(4,128)} %broadcast_in_dim.13), calls=%async_computation.1 | async-start | bytes 2097152 | tf_op jit(solution)/shard_map/all_to_all | solution.py:54
  72.6 0.8 copy-start.2
  74.5 24.7 %all-to-all-start.2 = ((f32[16,1,2144]{2,1,0:T(1,128)}), f32[16,1,2144]{2,1,0:T(1,128)S(1)}, u32[]{:S(2)}, u32[]{:S(2)}) async-start(f32[16,1,2144]{2,1,0:T(1,128)} %broadcast_in_dim.15), calls=%async_computation.2 | async-start | bytes 278528 | tf_op jit(solution)/shard_map/all_to_all | solution.py:54
  99.3 0.6 copy-start.3
  100.1 0.7 slice-start
  107.5 5.6 %copy-start.4 = (f32[2144]{0:T(1024)S(1)}, f32[2144]{0:T(1024)}, u32[]{:S(2)}) copy-start(f32[2144]{0:T(1024)} %copy-done.3) | copy-start | bytes 25732

commit v3 on v2

--- a/solution.py
+++ b/solution.py
@@ -2,6 +2,7 @@
 import jax.numpy as jnp
 from jax import lax
 from jax.sharding import PartitionSpec as P
+from jax.experimental import pallas as pl
 
 GRID = 32
 ITERS = 3
@@ -115,16 +116,40 @@
     return smooth_once(source)
 
 
+def _eliminate(a_ref, o_ref):
+    a = a_ref[...]
+    n, w = a.shape
+    ri = lax.broadcasted_iota(jnp.int32, (n, w), 0)
+    ci = lax.broadcasted_iota(jnp.int32, (n, w), 1)
+    rc = lax.broadcasted_iota(jnp.int32, (n, 1), 0)
+
+    def step(j, a):
+        rowj = jnp.sum(jnp.where(ri == j, a, 0.0), axis=0, keepdims=True)
+        colj = jnp.sum(jnp.where(ci == j, a, 0.0), axis=1, keepdims=True)
+        pivot = jnp.sum(jnp.where(rc == j, colj, 0.0), axis=0, keepdims=True)
+        rown = rowj / pivot
+        return jnp.where(ri == j, rown, a - colj * rown)
+
+    o_ref[...] = lax.fori_loop(0, n, step, a)
+
+
+def spd_solve(m, b):
+    n, k = b.shape
+    width = max(128, (n + k + 127) // 128 * 128)
+    a = jnp.concatenate([m, b, jnp.zeros((n, width - n - k), m.dtype)], axis=1)
+    out = pl.pallas_call(_eliminate, out_shape=jax.ShapeDtypeStruct(a.shape, a.dtype))(a)
+    return out[:, n : n + k]
+
+
 def per_device(data, weights, mixing):
     local_scans, ranks, planes, cells = data.shape
     mix_gram = jnp.dot(mixing.T, mixing, precision=highest)
     weight_gram = jnp.dot(weights.T, weights, precision=highest)
-    lower_factor = jnp.linalg.cholesky(mix_gram * weight_gram)
     own_weights = lax.dynamic_slice_in_dim(
         weights, lax.axis_index("cuts") * local_scans, local_scans, 0
     )
     scaled = (mixing[None, :, :] * own_weights[:, None, :]).reshape(local_scans * ranks, ranks)
-    coefficients = jax.scipy.linalg.cho_solve((lower_factor, True), scaled.T).T.astype(jnp.bfloat16)
+    coefficients = spd_solve(mix_gram * weight_gram, scaled.T).T.astype(jnp.bfloat16)
     stacked = data.reshape(local_scans * ranks, planes * cells)
     portion = sent_and_summed(
         lax.dot_general(
@@ -158,8 +183,7 @@
     factor_gram = jnp.concatenate(
         [jnp.concatenate([top, off], axis=1), jnp.concatenate([off.T, low], axis=1)], axis=0
     )
-    lower_next = jnp.linalg.cholesky(mix_gram * factor_gram)
-    updated = jax.scipy.linalg.cho_solve((lower_next, True), targets.T).T
+    updated = spd_solve(mix_gram * factor_gram, targets.T).T
     return (factor, updated)
 
 

time: 116 us -> 110 us (0.948)
  other arithmetic: 25.6 us -> 2.96 us
  Pallas kernels: 0 us -> 16 us
  local copies, waits for them, and re-layouts: 8.9 us -> 12.7 us
  matrix products: 4.9 us -> 2.03 us
    another operation x10 -> x0, other arithmetic: 24.1 us -> none  [the longest x3 6.52 us: per_device(): lower_factor = jnp.linalg.cholesky(mix_gram * weight_gram)]
    pallas_call x0 -> x2, Pallas kernels: none -> 16 us  [spd_solve(): pl.pallas_call(_eliminate, out_shape=jax.ShapeDtypeStruct(a.shape, a.dtype))]
    slice x0 -> x2, local copies, waits for them, and re-layouts: none -> 2.29 us  [spd_solve(): return out[:, n:n + k]]
    another operation x4 -> x0, matrix products: 2.05 us -> none  [the longest x2 1.15 us: per_device(): jax.scipy.linalg.cho_solve((lower_factor, True), scaled.T)]
    concatenate x0 -> x2, other arithmetic: none -> 1.4 us  [spd_solve(): a = jnp.concatenate([m, b, jnp.zeros((n, width - n - k), m.dtype)], axis=1)]
    unnamed x14 -> x15, local copies, waits for them, and re-layouts: 3.14 us -> 3.54 us
where the time goes in v3:
time: 110 us; the launch traced here: 109 us
  waiting for transfers between devices  44.6 us (41%)
  starting transfers between devices  30.1 us (27%)
  Pallas kernels  16 us (15%)
  local copies, waits for them, and re-layouts  12.7 us (12%)
  other arithmetic  2.96 us (3%)
  matrix products  2.03 us (2%)
    all_to_all x2, waiting for transfers between devices, from_everyone(): lax.all_to_all(jnp.broadcast_to(shard[None], (devices, *shard.shape)), ax...  25.3 us
    all_to_all x2, starting transfers between devices, from_everyone(): lax.all_to_all(jnp.broadcast_to(shard[None], (devices, *shard.shape)), ax...  19.4 us
    pallas_call x2, Pallas kernels, spd_solve(): pl.pallas_call(_eliminate, out_shape=jax.ShapeDtypeStruct(a.shape, a.dtype))  16 us
    all_to_all x1, waiting for transfers between devices, sent_and_summed(): lax.all_to_all(tiles, axis, split_axis=0, concat_axis=0, tiled=True)  14.4 us
    all_to_all x1, starting transfers between devices, sent_and_summed(): lax.all_to_all(tiles, axis, split_axis=0, concat_axis=0, tiled=True)  6.06 us
    ppermute x1, waiting for transfers between devices, extended_2(): lax.ppermute(head, axis, [((i + 1) % count, i) for i in range(ends)])  4.27 us
    unnamed x15, local copies, waits for them, and re-layouts  3.54 us
    ppermute x1, starting transfers between devices, extended_2(): lax.ppermute(tail, axis, [(i, (i + 1) % count) for i in range(ends)])  3.4 us
  transfers between devices with their start and end apart: 5, of which 5 were waited for; matrix products, arithmetic and copies ran while one was open for 0% of the time, Pallas kernels for 0%

profile of v3, /device:TPU:24, one launch (start us, length us, event | category | flops | bytes accessed | tf_op | source)
XLA Modules:
  0.0 109.3 jit_solution(15739586420226950279)
XLA Ops:
  0.7 0.9 copy.38
  2.2 0.7 pad_maximum_fusion.1.a_ref
  2.9 8.0 %shard_map.50 = f32[64,128]{1,0:T(8,128)} custom-call(f32[64,128]{1,0:T(8,128)} %pad_maximum_fusion.1.a_ref), custom_call_target="tpu_custom_call" | custom-call | tf_op jit(solution)/shard_map/pallas_call | solution.py:140
  10.9 0.8 slice.343
  11.7 1.4 %reshape.107 = bf16[64,4096,1]{1,0,2:T(8,128)(2,1)S(1)} reshape(bf16[1,64,4,1024]{3,2,1,0:T(4,128)(2,1)} %param.3) | data formatting | bytes 1048576 | tf_op jit(solution)/shard_map/reshape | solution.py:153
  13.4 1.6 %copy.40 = f32[16,4,4096]{2,1,0:T(4,128)} copy(f32[16,4,4096]{2,0,1:T(8,128)S(1)} %fusion.37) | data formatting | bytes 2097152 | tf_op jit(solution)/shard_map/dot_general | solution.py:155
  15.0 6.1 %all-to-all-start = ((f32[16,4,4096]{2,1,0:T(4,128)}), f32[16,4,4096]{2,1,0:T(4,128)S(1)}, u32[]{:S(2)}, u32[]{:S(2)}) async-start(f32[16,4,4096]{2,1,0:T(4,128)} %copy.40), calls=%async_computation | async-start | bytes 2097152 | tf_op jit(solution)/shard_map/all_to_all | solution.py:43
  21.3 14.4 %all-to-all-done = f32[16,4,4096]{2,1,0:T(4,128)S(1)} async-done(((f32[16,4,4096]{2,1,0:T(4,128)}), f32[16,4,4096]{2,1,0:T(4,128)S(1)}, u32[]{:S(2)}, u32[]{:S(2)}) %all-to-all-start) | async-done | bytes 1048608 | tf_op jit(solution)/shard_map/all_to_all | solution.py:43
  36.0 3.4 %collective-permute-start = (f32[4,3,1024]{2,1,0:T(4,128)S(1)}, f32[4,3,1024]{2,1,0:T(4,128)S(1)}, u32[]{:S(2)}, u32[]{:S(2)}) collective-permute-start(f32[4,3,1024]{2,1,0:T(4,128)S(1)} %get-tuple-element.8), channel_id=1, source_target_pairs={{0,1},{1,2},{2,3},{3,4},{4,5},{5,6},{6,7},{7,8},{8,9},{9,10},{10,1... | collective-permute-start | bytes 147464 | tf_op jit(solution)/shard_map/ppermute | solution.py:27
  39.4 1.3 %collective-permute-start.1 = (f32[4,3,1024]{2,1,0:T(4,128)S(1)}, f32[4,3,1024]{2,1,0:T(4,128)S(1)}, u32[]{:S(2)}, u32[]{:S(2)}) collective-permute-start(f32[4,3,1024]{2,1,0:T(4,128)S(1)} %get-tuple-element.9), channel_id=1, source_target_pairs={{1,0},{2,1},{3,2},{4,3},{5,4},{6,5},{7,6},{8,7},{9,8},{10,9},{11,1... | collective-permute-start | bytes 147464 | tf_op jit(solution)/shard_map/ppermute | solution.py:29
  40.7 0.6 collective-permute-done
  41.3 4.3 %collective-permute-done.1 = f32[4,3,1024]{2,1,0:T(4,128)S(1)} collective-permute-done((f32[4,3,1024]{2,1,0:T(4,128)S(1)}, f32[4,3,1024]{2,1,0:T(4,128)S(1)}, u32[]{:S(2)}, u32[]{:S(2)}) %collective-permute-start.1) | collective-permute-done | bytes 49184 | tf_op jit(solution)/shard_map/ppermute | solution.py:29
  46.4 1.2 %broadcast_in_dim.14 = f32[16,4,4,1024]{3,2,1,0:T(4,128)} broadcast(f32[4,4,1024]{2,1,0:T(4,128)S(1)} %fusion.35), dimensions={1,2,3} | broadcast | bytes 1114112 | tf_op jit(solution)/shard_map/broadcast_in_dim | solution.py:56
  47.6 5.6 %all-to-all-start.1 = ((f32[16,4,4,1024]{3,2,1,0:T(4,128)}), f32[16,4,4,1024]{3,2,1,0:T(4,128)S(1)}, u32[]{:S(2)}, u32[]{:S(2)}) async-start(f32[16,4,4,1024]{3,2,1,0:T(4,128)} %broadcast_in_dim.14), calls=%async_computation.1 | async-start | bytes 2097152 | tf_op jit(solution)/shard_map/all_to_all | solution.py:55
  53.4 14.5 %all-to-all-done.1 = f32[16,4,4,1024]{3,2,1,0:T(4,128)S(1)} async-done(((f32[16,4,4,1024]{3,2,1,0:T(4,128)}), f32[16,4,4,1024]{3,2,1,0:T(4,128)S(1)}, u32[]{:S(2)}, u32[]{:S(2)}) %all-to-all-start.1) | async-done | bytes 1048608 | tf_op jit(solution)/shard_map/all_to_all | solution.py:55
  67.9 0.6 copy.55
  68.5 1.0 fusion.53
  70.9 0.7 broadcast_in_dim.17
  71.6 13.8 %all-to-all-start.2 = ((f32[16,1,2144]{2,1,0:T(1,128)}), f32[16,1,2144]{2,1,0:T(1,128)S(1)}, u32[]{:S(2)}, u32[]{:S(2)}) async-start(f32[16,1,2144]{2,1,0:T(1,128)} %broadcast_in_dim.17), calls=%async_computation.2 | async-start | bytes 278528 | tf_op jit(solution)/shard_map/all_to_all | solution.py:55
  85.5 10.8 %all-to-all-done.2 = f32[16,1,2144]{2,1,0:T(1,128)S(1)} async-done(((f32[16,1,2144]{2,1,0:T(1,128)}), f32[16,1,2144]{2,1,0:T(1,128)S(1)}, u32[]{:S(2)}, u32[]{:S(2)}) %all-to-all-start.2) | async-done | bytes 137248 | tf_op jit(solution)/shard_map/all_to_all | solution.py:55
  98.2 0.7 maximum_maximum_fusion.a_ref
  98.9 8.0 %shard_map.51 = f32[64,128]{1,0:T(8,128)} custom-call(f32[64,128]{1,0:T(8,128)} %maximum_maximum_fusion.a_ref), custom_call_target="tpu_custom_call" | custom-call | tf_op jit(solution)/shard_map/pallas_call | solution.py:140
  106.9 1.5 %slice_reduce_fusion = f32[64]{0:T(128)} fusion(f32[64,128]{1,0:T(8,128)} %shard_map.51), kind=kLoop, calls=%fused_computation.58 | loop fusion | bytes 512 | tf_op jit(solution)/shard_map/slice | solution.py:141
  108.3 1.0 copy.61
  (54 shorter events, 5.5 us)
Async XLA Ops:
  0.6 1.2 %copy-start = (f32[16,64]{1,0:T(8,128)S(1)}, f32[16,64]{1,0:T(8,128)}, u32[]{:S(2)}) copy-start(f32[16,64]{1,0:T(8,128)} %param.4) | copy-start | bytes 12292
  0.6 0.9 copy-start.2
  15.0 20.7 %all-to-all-start = ((f32[16,4,4096]{2,1,0:T(4,128)}), f32[16,4,4096]{2,1,0:T(4,128)S(1)}, u32[]{:S(2)}, u32[]{:S(2)}) async-start(f32[16,4,4096]{2,1,0:T(4,128)} %copy.40), calls=%async_computation | async-start | bytes 2097152 | tf_op jit(solution)/shard_map/all_to_all | solution.py:43
  36.0 5.3 %collective-permute-start = (f32[4,3,1024]{2,1,0:T(4,128)S(1)}, f32[4,3,1024]{2,1,0:T(4,128)S(1)}, u32[]{:S(2)}, u32[]{:S(2)}) collective-permute-start(f32[4,3,1024]{2,1,0:T(4,128)S(1)} %get-tuple-element.8), channel_id=1, source_target_pairs={{0,1},{1,2},{2,3},{3,4},{4,5},{5,6},{6,7},{7,8},{8,9},{9,10},{10,1... | collective-permute-start | bytes 147464 | tf_op jit(solution)/shard_map/ppermute | solution.py:27
  39.4 6.2 %collective-permute-start.1 = (f32[4,3,1024]{2,1,0:T(4,128)S(1)}, f32[4,3,1024]{2,1,0:T(4,128)S(1)}, u32[]{:S(2)}, u32[]{:S(2)}) collective-permute-start(f32[4,3,1024]{2,1,0:T(4,128)S(1)} %get-tuple-element.9), channel_id=1, source_target_pairs={{1,0},{2,1},{3,2},{4,3},{5,4},{6,5},{7,6},{8,7},{9,8},{10,9},{11,1... | collective-permute-start | bytes 147464 | tf_op jit(solution)/shard_map/ppermute | solution.py:29
  47.6 5.6 %copy-start.1 = (bf16[1,64,4,1024]{3,2,1,0:T(4,128)(2,1)S(1)}, bf16[1,64,4,1024]{3,2,1,0:T(4,128)(2,1)}, u32[]{:S(2)}) copy-start(bf16[1,64,4,1024]{3,2,1,0:T(4,128)(2,1)} %param.3) | copy-start | bytes 1572868
  47.6 20.3 %all-to-all-start.1 = ((f32[16,4,4,1024]{3,2,1,0:T(4,128)}), f32[16,4,4,1024]{3,2,1,0:T(4,128)S(1)}, u32[]{:S(2)}, u32[]{:S(2)}) async-start(f32[16,4,4,1024]{3,2,1,0:T(4,128)} %broadcast_in_dim.14), calls=%async_computation.1 | async-start | bytes 2097152 | tf_op jit(solution)/shard_map/all_to_all | solution.py:55
  71.6 24.7 %all-to-all-start.2 = ((f32[16,1,2144]{2,1,0:T(1,128)}), f32[16,1,2144]{2,1,0:T(1,128)S(1)}, u32[]{:S(2)}, u32[]{:S(2)}) async-start(f32[16,1,2144]{2,1,0:T(1,128)} %broadcast_in_dim.17), calls=%async_computation.2 | async-start | bytes 278528 | tf_op jit(solution)/shard_map/all_to_all | solution.py:55
  96.4 0.6 copy-start.3
  97.4 0.7 slice-start

commit v4 on v2

--- a/solution.py
+++ b/solution.py
@@ -2,6 +2,7 @@
 import jax.numpy as jnp
 from jax import lax
 from jax.sharding import PartitionSpec as P
+from jax.experimental import pallas as pl
 
 GRID = 32
 ITERS = 3
@@ -115,20 +116,45 @@
     return smooth_once(source)
 
 
+def _eliminate(m_ref, b_ref, o_ref):
+    m = m_ref[...]
+    b = b_ref[...]
+    n = m.shape[0]
+    ri = lax.broadcasted_iota(jnp.int32, m.shape, 0)
+    ci = lax.broadcasted_iota(jnp.int32, m.shape, 1)
+    rb = lax.broadcasted_iota(jnp.int32, b.shape, 0)
+
+    def step(j, carry):
+        m, b = carry
+        colj = jnp.sum(jnp.where(ci == j, m, 0.0), axis=1, keepdims=True)
+        pivot = jnp.sum(jnp.where(ri[:, :1] == j, colj, 0.0), axis=0, keepdims=True)
+        rowm = jnp.sum(jnp.where(ri == j, m, 0.0), axis=0, keepdims=True) / pivot
+        rowb = jnp.sum(jnp.where(rb == j, b, 0.0), axis=0, keepdims=True) / pivot
+        m = jnp.where(ri == j, rowm, m - colj * rowm)
+        b = jnp.where(rb == j, rowb, b - colj * rowb)
+        return m, b
+
+    o_ref[...] = lax.fori_loop(0, n, step, (m, b), unroll=8)[1]
+
+
+def spd_solve(m, b):
+    return pl.pallas_call(_eliminate, out_shape=jax.ShapeDtypeStruct(b.shape, b.dtype))(m, b)
+
+
 def per_device(data, weights, mixing):
     local_scans, ranks, planes, cells = data.shape
     mix_gram = jnp.dot(mixing.T, mixing, precision=highest)
     weight_gram = jnp.dot(weights.T, weights, precision=highest)
-    lower_factor = jnp.linalg.cholesky(mix_gram * weight_gram)
     own_weights = lax.dynamic_slice_in_dim(
         weights, lax.axis_index("cuts") * local_scans, local_scans, 0
     )
-    scaled = (mixing[None, :, :] * own_weights[:, None, :]).reshape(local_scans * ranks, ranks)
-    coefficients = jax.scipy.linalg.cho_solve((lower_factor, True), scaled.T).T.astype(jnp.bfloat16)
+    scaled = (mixing.T[None, :, :] * own_weights[:, :, None]).transpose(1, 0, 2)
+    coefficients = spd_solve(mix_gram * weight_gram, scaled.reshape(ranks, local_scans * ranks))
+    coefficients = coefficients.astype(jnp.bfloat16)
     stacked = data.reshape(local_scans * ranks, planes * cells)
     portion = sent_and_summed(
         lax.dot_general(
-            coefficients, stacked, (((0,), (0,)), ((), ())), preferred_element_type=jnp.float32
+            coefficients, stacked, (((1,), (0,)), ((), ())), preferred_element_type=jnp.float32
         ),
         "cuts",
         0,
@@ -158,8 +184,7 @@
     factor_gram = jnp.concatenate(
         [jnp.concatenate([top, off], axis=1), jnp.concatenate([off.T, low], axis=1)], axis=0
     )
-    lower_next = jnp.linalg.cholesky(mix_gram * factor_gram)
-    updated = jax.scipy.linalg.cho_solve((lower_next, True), targets.T).T
+    updated = spd_solve(mix_gram * factor_gram, targets.T).T
     return (factor, updated)
 
 

time: 116 us -> 111 us (0.957)
  other arithmetic: 25.6 us -> 4.93 us
  Pallas kernels: 0 us -> 15.9 us
  matrix products: 4.9 us -> 2.64 us
  local copies, waits for them, and re-layouts: 8.9 us -> 10.4 us
    another operation x10 -> x0, other arithmetic: 24.1 us -> none  [the longest x3 6.52 us: per_device(): lower_factor = jnp.linalg.cholesky(mix_gram * weight_gram)]
    pallas_call x0 -> x2, Pallas kernels: none -> 15.9 us  [spd_solve(): pl.pallas_call(_eliminate, out_shape=jax.ShapeDtypeStruct(b.shape, b.dtype))]
    another operation x4 -> x0, matrix products: 2.05 us -> none  [the longest x2 1.15 us: per_device(): jax.scipy.linalg.cho_solve((lower_factor, True), scaled.T)]
    pallas_call x0 -> x1, other arithmetic: none -> 1.38 us  [spd_solve(): pl.pallas_call(_eliminate, out_shape=jax.ShapeDtypeStruct(b.shape, b.dtype))]
    mul x1 -> x2, other arithmetic: 0.08 us -> 1.38 us  [the longest x1 0.7 us: per_device(): updated = spd_solve(mix_gram * factor_gram, targets.T).T]
    unnamed x14 -> x15, local copies, waits for them, and re-layouts: 3.14 us -> 3.54 us
where the time goes in v4:
time: 111 us; the launch traced here: 110 us
  waiting for transfers between devices  44.7 us (40%)
  starting transfers between devices  30.1 us (27%)
  Pallas kernels  15.9 us (14%)
  local copies, waits for them, and re-layouts  10.4 us (9%)
  other arithmetic  4.93 us (4%)
  matrix products  2.64 us (2%)
    all_to_all x2, waiting for transfers between devices, from_everyone(): lax.all_to_all(jnp.broadcast_to(shard[None], (devices, *shard.shape)), ax...  25.4 us
    all_to_all x2, starting transfers between devices, from_everyone(): lax.all_to_all(jnp.broadcast_to(shard[None], (devices, *shard.shape)), ax...  19.4 us
    pallas_call x2, Pallas kernels, spd_solve(): pl.pallas_call(_eliminate, out_shape=jax.ShapeDtypeStruct(b.shape, b.dtype))  15.9 us
    all_to_all x1, waiting for transfers between devices, sent_and_summed(): lax.all_to_all(tiles, axis, split_axis=0, concat_axis=0, tiled=True)  14.4 us
    all_to_all x1, starting transfers between devices, sent_and_summed(): lax.all_to_all(tiles, axis, split_axis=0, concat_axis=0, tiled=True)  6.06 us
    ppermute x1, waiting for transfers between devices, extended_2(): lax.ppermute(head, axis, [((i + 1) % count, i) for i in range(ends)])  4.27 us
    unnamed x15, local copies, waits for them, and re-layouts  3.54 us
    ppermute x1, starting transfers between devices, extended_2(): lax.ppermute(tail, axis, [(i, (i + 1) % count) for i in range(ends)])  3.4 us
  transfers between devices with their start and end apart: 5, of which 5 were waited for; matrix products, arithmetic and copies ran while one was open for 0% of the time, Pallas kernels for 0%

profile of v4, /device:TPU:24, one launch (start us, length us, event | category | flops | bytes accessed | tf_op | source)
XLA Modules:
  0.0 109.5 jit_solution(2890625415680459144)
XLA Ops:
  0.7 0.9 copy.38
  1.8 0.9 convolution_multiply_fusion.m_ref
  2.7 0.7 multiply_bitcast_fusion.b_ref
  3.4 8.0 %shard_map.50 = f32[64,64]{1,0:T(8,128)} custom-call(f32[64,64]{1,0:T(8,128)} %convolution_multiply_fusion.m_ref, f32[64,64]{1,0:T(8,128)} %multiply_bitcast_fusion.b_ref), custom_call_target="tpu_custom_call" | custom-call | tf_op jit(solution)/shard_map/pallas_call | solution.py:141
  11.3 0.8 convert_element_type.69
  12.1 1.4 %reshape.106 = bf16[64,4096,1]{1,0,2:T(8,128)(2,1)S(1)} reshape(bf16[1,64,4,1024]{3,2,1,0:T(4,128)(2,1)} %param.3) | data formatting | bytes 1048576 | tf_op jit(solution)/shard_map/reshape | solution.py:154
  13.8 1.6 %copy.40 = f32[16,4,4096]{2,1,0:T(4,128)} copy(f32[16,4,4096]{2,0,1:T(8,128)S(1)} %fusion.37) | data formatting | bytes 2097152 | tf_op jit(solution)/shard_map/dot_general | solution.py:156
  15.4 6.1 %all-to-all-start = ((f32[16,4,4096]{2,1,0:T(4,128)}), f32[16,4,4096]{2,1,0:T(4,128)S(1)}, u32[]{:S(2)}, u32[]{:S(2)}) async-start(f32[16,4,4096]{2,1,0:T(4,128)} %copy.40), calls=%async_computation | async-start | bytes 2097152 | tf_op jit(solution)/shard_map/all_to_all | solution.py:43
  21.7 14.4 %all-to-all-done = f32[16,4,4096]{2,1,0:T(4,128)S(1)} async-done(((f32[16,4,4096]{2,1,0:T(4,128)}), f32[16,4,4096]{2,1,0:T(4,128)S(1)}, u32[]{:S(2)}, u32[]{:S(2)}) %all-to-all-start) | async-done | bytes 1048608 | tf_op jit(solution)/shard_map/all_to_all | solution.py:43
  36.4 3.4 %collective-permute-start = (f32[4,3,1024]{2,1,0:T(4,128)S(1)}, f32[4,3,1024]{2,1,0:T(4,128)S(1)}, u32[]{:S(2)}, u32[]{:S(2)}) collective-permute-start(f32[4,3,1024]{2,1,0:T(4,128)S(1)} %get-tuple-element.8), channel_id=1, source_target_pairs={{0,1},{1,2},{2,3},{3,4},{4,5},{5,6},{6,7},{7,8},{8,9},{9,10},{10,1... | collective-permute-start | bytes 147464 | tf_op jit(solution)/shard_map/ppermute | solution.py:27
  39.8 1.3 %collective-permute-start.1 = (f32[4,3,1024]{2,1,0:T(4,128)S(1)}, f32[4,3,1024]{2,1,0:T(4,128)S(1)}, u32[]{:S(2)}, u32[]{:S(2)}) collective-permute-start(f32[4,3,1024]{2,1,0:T(4,128)S(1)} %get-tuple-element.9), channel_id=1, source_target_pairs={{1,0},{2,1},{3,2},{4,3},{5,4},{6,5},{7,6},{8,7},{9,8},{10,9},{11,1... | collective-permute-start | bytes 147464 | tf_op jit(solution)/shard_map/ppermute | solution.py:29
  41.7 4.3 %collective-permute-done.1 = f32[4,3,1024]{2,1,0:T(4,128)S(1)} collective-permute-done((f32[4,3,1024]{2,1,0:T(4,128)S(1)}, f32[4,3,1024]{2,1,0:T(4,128)S(1)}, u32[]{:S(2)}, u32[]{:S(2)}) %collective-permute-start.1) | collective-permute-done | bytes 49184 | tf_op jit(solution)/shard_map/ppermute | solution.py:29
  46.8 1.2 %broadcast_in_dim.12 = f32[16,4,4,1024]{3,2,1,0:T(4,128)} broadcast(f32[4,4,1024]{2,1,0:T(4,128)S(1)} %fusion.35), dimensions={1,2,3} | broadcast | bytes 1114112 | tf_op jit(solution)/shard_map/broadcast_in_dim | solution.py:56
  48.0 5.6 %all-to-all-start.1 = ((f32[16,4,4,1024]{3,2,1,0:T(4,128)}), f32[16,4,4,1024]{3,2,1,0:T(4,128)S(1)}, u32[]{:S(2)}, u32[]{:S(2)}) async-start(f32[16,4,4,1024]{3,2,1,0:T(4,128)} %broadcast_in_dim.12), calls=%async_computation.1 | async-start | bytes 2097152 | tf_op jit(solution)/shard_map/all_to_all | solution.py:55
  53.8 14.5 %all-to-all-done.1 = f32[16,4,4,1024]{3,2,1,0:T(4,128)S(1)} async-done(((f32[16,4,4,1024]{3,2,1,0:T(4,128)}), f32[16,4,4,1024]{3,2,1,0:T(4,128)S(1)}, u32[]{:S(2)}, u32[]{:S(2)}) %all-to-all-start.1) | async-done | bytes 1048608 | tf_op jit(solution)/shard_map/all_to_all | solution.py:55
  68.9 1.0 fusion.53
  71.3 0.7 broadcast_in_dim.14
  72.0 13.8 %all-to-all-start.2 = ((f32[16,1,2144]{2,1,0:T(1,128)}), f32[16,1,2144]{2,1,0:T(1,128)S(1)}, u32[]{:S(2)}, u32[]{:S(2)}) async-start(f32[16,1,2144]{2,1,0:T(1,128)} %broadcast_in_dim.14), calls=%async_computation.2 | async-start | bytes 278528 | tf_op jit(solution)/shard_map/all_to_all | solution.py:55
  85.8 10.9 %all-to-all-done.2 = f32[16,1,2144]{2,1,0:T(1,128)S(1)} async-done(((f32[16,1,2144]{2,1,0:T(1,128)}), f32[16,1,2144]{2,1,0:T(1,128)S(1)}, u32[]{:S(2)}, u32[]{:S(2)}) %all-to-all-start.2) | async-done | bytes 137248 | tf_op jit(solution)/shard_map/all_to_all | solution.py:55
  97.8 0.7 copy.47.b_ref
  98.5 0.7 maximum_multiply_fusion.m_ref
  99.2 8.0 %shard_map.51 = f32[64,1]{1,0:T(8,128)} custom-call(f32[64,64]{1,0:T(8,128)} %maximum_multiply_fusion.m_ref, f32[64,1]{1,0:T(8,128)} %copy.47.b_ref), custom_call_target="tpu_custom_call" | custom-call | tf_op jit(solution)/shard_map/pallas_call | solution.py:141
  107.2 1.4 %reduce.3 = f32[64]{0:T(128)} reduce(f32[64,1]{1,0:T(8,128)} %shard_map.51, f32[]{:T(128)} %constant.93), dimensions={1}, to_apply=%pallas_call.7.reduce_sub_computation | reduce | bytes 516 | tf_op jit(solution)/shard_map/pallas_call | solution.py:141
  108.6 1.0 copy.61
  (50 shorter events, 5.6 us)
Async XLA Ops:
  0.6 1.2 %copy-start = (f32[16,64]{1,0:T(8,128)S(1)}, f32[16,64]{1,0:T(8,128)}, u32[]{:S(2)}) copy-start(f32[16,64]{1,0:T(8,128)} %param.4) | copy-start | bytes 12292
  0.6 0.9 copy-start.2
  15.4 20.7 %all-to-all-start = ((f32[16,4,4096]{2,1,0:T(4,128)}), f32[16,4,4096]{2,1,0:T(4,128)S(1)}, u32[]{:S(2)}, u32[]{:S(2)}) async-start(f32[16,4,4096]{2,1,0:T(4,128)} %copy.40), calls=%async_computation | async-start | bytes 2097152 | tf_op jit(solution)/shard_map/all_to_all | solution.py:43
  36.4 5.3 %collective-permute-start = (f32[4,3,1024]{2,1,0:T(4,128)S(1)}, f32[4,3,1024]{2,1,0:T(4,128)S(1)}, u32[]{:S(2)}, u32[]{:S(2)}) collective-permute-start(f32[4,3,1024]{2,1,0:T(4,128)S(1)} %get-tuple-element.8), channel_id=1, source_target_pairs={{0,1},{1,2},{2,3},{3,4},{4,5},{5,6},{6,7},{7,8},{8,9},{9,10},{10,1... | collective-permute-start | bytes 147464 | tf_op jit(solution)/shard_map/ppermute | solution.py:27
  39.8 6.2 %collective-permute-start.1 = (f32[4,3,1024]{2,1,0:T(4,128)S(1)}, f32[4,3,1024]{2,1,0:T(4,128)S(1)}, u32[]{:S(2)}, u32[]{:S(2)}) collective-permute-start(f32[4,3,1024]{2,1,0:T(4,128)S(1)} %get-tuple-element.9), channel_id=1, source_target_pairs={{1,0},{2,1},{3,2},{4,3},{5,4},{6,5},{7,6},{8,7},{9,8},{10,9},{11,1... | collective-permute-start | bytes 147464 | tf_op jit(solution)/shard_map/ppermute | solution.py:29
  48.0 5.6 %copy-start.1 = (bf16[1,64,4,1024]{3,2,1,0:T(4,128)(2,1)S(1)}, bf16[1,64,4,1024]{3,2,1,0:T(4,128)(2,1)}, u32[]{:S(2)}) copy-start(bf16[1,64,4,1024]{3,2,1,0:T(4,128)(2,1)} %param.3) | copy-start | bytes 1572868
  48.0 20.3 %all-to-all-start.1 = ((f32[16,4,4,1024]{3,2,1,0:T(4,128)}), f32[16,4,4,1024]{3,2,1,0:T(4,128)S(1)}, u32[]{:S(2)}, u32[]{:S(2)}) async-start(f32[16,4,4,1024]{3,2,1,0:T(4,128)} %broadcast_in_dim.12), calls=%async_computation.1 | async-start | bytes 2097152 | tf_op jit(solution)/shard_map/all_to_all | solution.py:55
  72.0 24.7 %all-to-all-start.2 = ((f32[16,1,2144]{2,1,0:T(1,128)}), f32[16,1,2144]{2,1,0:T(1,128)S(1)}, u32[]{:S(2)}, u32[]{:S(2)}) async-start(f32[16,1,2144]{2,1,0:T(1,128)} %broadcast_in_dim.14), calls=%async_computation.2 | async-start | bytes 278528 | tf_op jit(solution)/shard_map/all_to_all | solution.py:55
  96.8 0.6 copy-start.3
  97.8 0.7 slice-start

commit v5 on v4

--- a/solution.py
+++ b/solution.py
@@ -1,8 +1,12 @@
+import functools
 import jax
 import jax.numpy as jnp
 from jax import lax
 from jax.sharding import PartitionSpec as P
 from jax.experimental import pallas as pl
+from jax.experimental.pallas import tpu as pltpu
+
+MESH = pl.DeviceIdType.MESH
 
 GRID = 32
 ITERS = 3
@@ -33,6 +37,70 @@
     return cells
 
 
+def _exchange_kernel(axis, other, n, whole, x_ref, o_ref, send_sem, recv_sem, own_sem):
+    me = lax.axis_index(axis)
+    fixed = lax.axis_index(other)
+
+    def where(peer):
+        return (peer, fixed) if axis == "cuts" else (fixed, peer)
+
+    def part(peer):
+        return x_ref if whole else x_ref.at[peer]
+
+    barrier = pltpu.get_barrier_semaphore()
+    for d in range(1, n):
+        pl.semaphore_signal(
+            barrier, inc=1, device_id=where(lax.rem(me + d, n)), device_id_type=MESH
+        )
+    pl.semaphore_wait(barrier, n - 1)
+    own = pltpu.make_async_copy(part(me), o_ref.at[me], own_sem)
+    own.start()
+    copies = []
+    for d in range(1, n):
+        peer = lax.rem(me + d, n)
+        copy = pltpu.make_async_remote_copy(
+            src_ref=part(peer),
+            dst_ref=o_ref.at[me],
+            send_sem=send_sem.at[peer],
+            recv_sem=recv_sem.at[me],
+            device_id=where(peer),
+            device_id_type=MESH,
+        )
+        copy.start()
+        copies.append(copy)
+    for copy in copies:
+        copy.wait_send()
+    for d in range(1, n):
+        source = lax.rem(me + n - d, n)
+        pltpu.make_async_remote_copy(
+            src_ref=part(source),
+            dst_ref=o_ref.at[source],
+            send_sem=send_sem.at[source],
+            recv_sem=recv_sem.at[source],
+            device_id=where(source),
+            device_id_type=MESH,
+        ).wait_recv()
+    own.wait()
+
+
+def exchange(x, axis, key, whole=False):
+    other = "col" if axis == "cuts" else "cuts"
+    n = lax.axis_size(axis)
+    shape = (n, *x.shape) if whole else x.shape
+    return pl.pallas_call(
+        functools.partial(_exchange_kernel, axis, other, n, whole),
+        out_shape=jax.ShapeDtypeStruct(shape, x.dtype),
+        in_specs=[pl.BlockSpec(memory_space=pltpu.VMEM)],
+        out_specs=pl.BlockSpec(memory_space=pltpu.VMEM),
+        scratch_shapes=[
+            pltpu.SemaphoreType.DMA((n,)),
+            pltpu.SemaphoreType.DMA((n,)),
+            pltpu.SemaphoreType.DMA,
+        ],
+        compiler_params=pltpu.CompilerParams(collective_id=key, has_side_effects=True),
+    )(x)
+
+
 def split_up(shard, dim, devices):
     before, after = (shard.shape[:dim], shard.shape[dim + 1 :])
     return jnp.moveaxis(shard.reshape(*before, devices, -1, *after), dim, 0)
@@ -40,7 +108,7 @@
 
 def sent_and_summed(shard, axis, dim):
     tiles = split_up(shard, dim, lax.axis_size(axis))
-    arrived = lax.all_to_all(tiles, axis, split_axis=0, concat_axis=0, tiled=True)
+    arrived = exchange(tiles, axis, 0)
     return arrived.sum(axis=0)
 
 
@@ -51,10 +119,7 @@
 
 
 def from_everyone(shard, axis):
-    devices = lax.axis_size(axis)
-    return lax.all_to_all(
-        jnp.broadcast_to(shard[None], (devices, *shard.shape)), axis, 0, 0, tiled=True
-    )
+    return exchange(shard, axis, 1 if axis == "cuts" else 2, whole=True)
 
 
 def gather_directly(shard, axis, dim):

time: 111 us -> 112 us (level)
  Pallas kernels: 15.9 us -> 78.9 us
  waiting for transfers between devices: 44.7 us -> 5.15 us
  starting transfers between devices: 30.1 us -> 4.69 us
  other arithmetic: 4.93 us -> 8.98 us
    pallas_call x0 -> x3, Pallas kernels: none -> 63.1 us  [exchange(): pl.pallas_call(functools.partial(_exchange_kernel, axis, other, n, whole)...]
    all_to_all x3 -> x0, waiting for transfers between devices: 39.9 us -> none  [the longest x2 25.4 us: from_everyone(): lax.all_to_all(jnp.broadcast_to(shard[None], (devices, *shard.shape)), ax...]
    all_to_all x3 -> x0, starting transfers between devices: 25.4 us -> none  [the longest x2 19.4 us: from_everyone(): lax.all_to_all(jnp.broadcast_to(shard[None], (devices, *shard.shape)), ax...]
    broadcast_in_dim x2 -> x0, local copies, waits for them, and re-layouts: 1.96 us -> none  [from_everyone(): jnp.broadcast_to(shard[None], (devices, *shard.shape))]
    convert_element_type x1, other arithmetic: 0.23 us -> 1.52 us  [per_device(): factor_half = factor_flat.astype(jnp.bfloat16)]
    reduce_sum x1, other arithmetic: 0.16 us -> 1.45 us  [sent_and_summed(): return arrived.sum(axis=0)]
    unnamed x15 -> x17, local copies, waits for them, and re-layouts: 3.54 us -> 3.56 us
  transfers between devices with their start and end apart: 5 -> 2, of which waited for: 5 -> 2; matrix products, arithmetic and copies ran while one was open for 0% -> 0% of each run, Pallas kernels for 0% -> 0%
where the time goes in v5:
time: 112 us; the launch traced here: 111 us
  Pallas kernels  78.9 us (70%)
  local copies, waits for them, and re-layouts  9.67 us (9%)
  other arithmetic  8.98 us (8%)
  waiting for transfers between devices  5.15 us (5%)
  starting transfers between devices  4.69 us (4%)
  matrix products  2.64 us (2%)
    pallas_call x3, Pallas kernels, exchange(): pl.pallas_call(functools.partial(_exchange_kernel, axis, other, n, whole)...  63.1 us
    pallas_call x2, Pallas kernels, spd_solve(): pl.pallas_call(_eliminate, out_shape=jax.ShapeDtypeStruct(b.shape, b.dtype))  15.9 us
    ppermute x1, waiting for transfers between devices, extended_2(): lax.ppermute(head, axis, [((i + 1) % count, i) for i in range(ends)])  4.67 us
    unnamed x17, local copies, waits for them, and re-layouts  3.56 us
    ppermute x1, starting transfers between devices, extended_2(): lax.ppermute(tail, axis, [(i, (i + 1) % count) for i in range(ends)])  3.4 us
  transfers between devices with their start and end apart: 2, of which 2 were waited for; matrix products, arithmetic and copies ran while one was open for 0% of the time, Pallas kernels for 0%

profile of v5, /device:TPU:24, one launch (start us, length us, event | category | flops | bytes accessed | tf_op | source)
XLA Modules:
  0.0 111.0 jit_solution(18050347013897377796)
XLA Ops:
  0.7 0.9 copy.13
  1.8 0.9 convolution_multiply_fusion.m_ref
  2.7 0.7 multiply_bitcast_fusion.b_ref
  3.4 7.9 %shard_map.50 = f32[64,64]{1,0:T(8,128)} custom-call(f32[64,64]{1,0:T(8,128)} %convolution_multiply_fusion.m_ref, f32[64,64]{1,0:T(8,128)} %multiply_bitcast_fusion.b_ref), custom_call_target="tpu_custom_call" | custom-call | tf_op jit(solution)/shard_map/pallas_call | solution.py:206
  11.3 0.8 convert_element_type.69
  12.1 1.4 %reshape.99 = bf16[64,4096,1]{1,0,2:T(8,128)(2,1)S(1)} reshape(bf16[1,64,4,1024]{3,2,1,0:T(4,128)(2,1)} %param.3) | data formatting | bytes 1048576 | tf_op jit(solution)/shard_map/reshape | solution.py:219
  13.8 1.6 %copy.15.x_ref = f32[16,4,4096]{2,1,0:T(4,128)} copy(f32[16,4,4096]{2,0,1:T(8,128)S(1)} %fusion.37) | data formatting | bytes 2097152 | tf_op jit(solution)/shard_map/dot_general | solution.py:221
  15.4 20.7 %shard_map.51 = f32[16,4,4096]{2,1,0:T(4,128)} custom-call(f32[16,4,4096]{2,1,0:T(4,128)} %copy.15.x_ref), custom_call_target="tpu_custom_call" | custom-call | tf_op jit(solution)/shard_map/pallas_call | solution.py:90
  36.1 1.4 %reduce_sum.36 = f32[4,4096]{1,0:T(4,128)S(1)} reduce(f32[16,4,4096]{2,1,0:T(4,128)} %shard_map.51, f32[]{:T(128)} %constant.25.clone.1), dimensions={0}, to_apply=%region_0.0 | reduce | flops 245760 | bytes 1114116 | tf_op jit(solution)/shard_map/reduce_sum | solution.py:112
  37.6 3.4 %collective-permute-start = (f32[4,3,1024]{2,1,0:T(4,128)S(1)}, f32[4,3,1024]{2,1,0:T(4,128)S(1)}, u32[]{:S(2)}, u32[]{:S(2)}) collective-permute-start(f32[4,3,1024]{2,1,0:T(4,128)S(1)} %get-tuple-element.8), channel_id=1, source_target_pairs={{0,1},{1,2},{2,3},{3,4},{4,5},{5,6},{6,7},{7,8},{8,9},{9,10},{10,1... | collective-permute-start | bytes 147464 | tf_op jit(solution)/shard_map/ppermute | solution.py:31
  41.1 1.3 %collective-permute-start.1 = (f32[4,3,1024]{2,1,0:T(4,128)S(1)}, f32[4,3,1024]{2,1,0:T(4,128)S(1)}, u32[]{:S(2)}, u32[]{:S(2)}) collective-permute-start(f32[4,3,1024]{2,1,0:T(4,128)S(1)} %get-tuple-element.9), channel_id=1, source_target_pairs={{1,0},{2,1},{3,2},{4,3},{5,4},{6,5},{7,6},{8,7},{9,8},{10,9},{11,1... | collective-permute-start | bytes 147464 | tf_op jit(solution)/shard_map/ppermute | solution.py:33
  43.2 4.7 %collective-permute-done.1 = f32[4,3,1024]{2,1,0:T(4,128)S(1)} collective-permute-done((f32[4,3,1024]{2,1,0:T(4,128)S(1)}, f32[4,3,1024]{2,1,0:T(4,128)S(1)}, u32[]{:S(2)}, u32[]{:S(2)}) %collective-permute-start.1) | collective-permute-done | bytes 49184 | tf_op jit(solution)/shard_map/ppermute | solution.py:33
  48.5 0.8 fusion.35.x_ref
  49.4 20.0 %shard_map.52 = f32[16,4,4,1024]{3,2,1,0:T(4,128)} custom-call(f32[4,4,1024]{2,1,0:T(4,128)} %fusion.35.x_ref), custom_call_target="tpu_custom_call" | custom-call | tf_op jit(solution)/shard_map/pallas_call | solution.py:90
  69.4 1.5 %convert_element_type.73 = bf16[16,4,4,1024]{3,2,1,0:T(4,128)(2,1)S(1)} convert(f32[16,4,4,1024]{3,2,1,0:T(4,128)} %shard_map.52) | non-fusion elementwise | flops 262144 | bytes 1572864 | tf_op jit(solution)/shard_map/convert_element_type | solution.py:230
  71.5 1.0 fusion.53
  73.6 0.7 concatenate.16.x_ref
  74.2 22.4 %shard_map.53 = f32[16,2144]{1,0:T(8,128)} custom-call(f32[2144]{0:T(1024)} %concatenate.16.x_ref), custom_call_target="tpu_custom_call" | custom-call | tf_op jit(solution)/shard_map/pallas_call | solution.py:90
  96.6 0.9 reduce_sum.39
  98.5 0.7 copy.21.b_ref
  100.0 0.7 maximum_multiply_fusion.m_ref
  100.7 7.9 %shard_map.54 = f32[64,1]{1,0:T(8,128)} custom-call(f32[64,64]{1,0:T(8,128)} %maximum_multiply_fusion.m_ref, f32[64,1]{1,0:T(8,128)} %copy.21.b_ref), custom_call_target="tpu_custom_call" | custom-call | tf_op jit(solution)/shard_map/pallas_call | solution.py:206
  108.6 1.4 %reduce.2 = f32[64]{0:T(128)} reduce(f32[64,1]{1,0:T(8,128)} %shard_map.54, f32[]{:T(128)} %constant.93), dimensions={1}, to_apply=%pallas_call.19.reduce_sub_computation | reduce | bytes 516 | tf_op jit(solution)/shard_map/pallas_call | solution.py:206
  110.0 1.0 copy.30
  (47 shorter events, 5.4 us)
Async XLA Ops:
  0.6 1.2 %copy-start = (f32[16,64]{1,0:T(8,128)S(1)}, f32[16,64]{1,0:T(8,128)}, u32[]{:S(2)}) copy-start(f32[16,64]{1,0:T(8,128)} %param.4) | copy-start | bytes 12292
  0.6 0.9 copy-start.3
  36.1 6.5 %copy-start.2 = (bf16[1,64,4,1024]{3,2,1,0:T(4,128)(2,1)S(1)}, bf16[1,64,4,1024]{3,2,1,0:T(4,128)(2,1)}, u32[]{:S(2)}) copy-start(bf16[1,64,4,1024]{3,2,1,0:T(4,128)(2,1)} %param.3) | copy-start | bytes 1572868
  37.6 5.6 %collective-permute-start = (f32[4,3,1024]{2,1,0:T(4,128)S(1)}, f32[4,3,1024]{2,1,0:T(4,128)S(1)}, u32[]{:S(2)}, u32[]{:S(2)}) collective-permute-start(f32[4,3,1024]{2,1,0:T(4,128)S(1)} %get-tuple-element.8), channel_id=1, source_target_pairs={{0,1},{1,2},{2,3},{3,4},{4,5},{5,6},{6,7},{7,8},{8,9},{9,10},{10,1... | collective-permute-start | bytes 147464 | tf_op jit(solution)/shard_map/ppermute | solution.py:31
  41.1 6.9 %collective-permute-start.1 = (f32[4,3,1024]{2,1,0:T(4,128)S(1)}, f32[4,3,1024]{2,1,0:T(4,128)S(1)}, u32[]{:S(2)}, u32[]{:S(2)}) collective-permute-start(f32[4,3,1024]{2,1,0:T(4,128)S(1)} %get-tuple-element.9), channel_id=1, source_target_pairs={{1,0},{2,1},{3,2},{4,3},{5,4},{6,5},{7,6},{8,7},{9,8},{10,9},{11,1... | collective-permute-start | bytes 147464 | tf_op jit(solution)/shard_map/ppermute | solution.py:33
  69.4 1.5 %copy-start.1 = (f32[16,4,4,1024]{3,2,1,0:T(4,128)S(1)}, f32[16,4,4,1024]{3,2,1,0:T(4,128)}, u32[]{:S(2)}) copy-start(f32[16,4,4,1024]{3,2,1,0:T(4,128)} %shard_map.52) | copy-start | bytes 3145732
  97.6 0.6 copy-start.4
  99.2 0.7 slice-start

commit v6 on v5

--- a/solution.py
+++ b/solution.py
@@ -189,17 +189,28 @@
     ci = lax.broadcasted_iota(jnp.int32, m.shape, 1)
     rb = lax.broadcasted_iota(jnp.int32, b.shape, 0)
 
+    def pick_row(x, rows, p):
+        return jnp.sum(jnp.where(rows == p, x, 0.0), axis=0, keepdims=True)
+
+    def pick_col(x, p):
+        return jnp.sum(jnp.where(ci[: x.shape[0]] == p, x, 0.0), axis=1, keepdims=True)
+
     def step(j, carry):
         m, b = carry
-        colj = jnp.sum(jnp.where(ci == j, m, 0.0), axis=1, keepdims=True)
-        pivot = jnp.sum(jnp.where(ri[:, :1] == j, colj, 0.0), axis=0, keepdims=True)
-        rowm = jnp.sum(jnp.where(ri == j, m, 0.0), axis=0, keepdims=True) / pivot
-        rowb = jnp.sum(jnp.where(rb == j, b, 0.0), axis=0, keepdims=True) / pivot
-        m = jnp.where(ri == j, rowm, m - colj * rowm)
-        b = jnp.where(rb == j, rowb, b - colj * rowb)
+        p, q = 2 * j, 2 * j + 1
+        c0, c1 = pick_col(m, p), pick_col(m, q)
+        r0, r1 = pick_row(m, ri, p), pick_row(m, ri, q)
+        s0, s1 = pick_row(b, rb, p), pick_row(b, rb, q)
+        a, e = pick_col(r0, p), pick_col(r0, q)
+        c, d = pick_col(r1, p), pick_col(r1, q)
+        scale = 1.0 / (a * d - e * c)
+        n0, n1 = (d * r0 - e * r1) * scale, (a * r1 - c * r0) * scale
+        t0, t1 = (d * s0 - e * s1) * scale, (a * s1 - c * s0) * scale
+        m = jnp.where(ri == p, n0, jnp.where(ri == q, n1, m - c0 * n0 - c1 * n1))
+        b = jnp.where(rb == p, t0, jnp.where(rb == q, t1, b - c0 * t0 - c1 * t1))
         return m, b
 
-    o_ref[...] = lax.fori_loop(0, n, step, (m, b), unroll=8)[1]
+    o_ref[...] = lax.fori_loop(0, n // 2, step, (m, b), unroll=4)[1]
 
 
 def spd_solve(m, b):

time: 112 us -> 107 us (0.955)
  Pallas kernels: 78.9 us -> 73.8 us
    pallas_call x2, Pallas kernels: 15.9 us -> 10.7 us  [spd_solve(): pl.pallas_call(_eliminate, out_shape=jax.ShapeDtypeStruct(b.shape, b.dtype))]
where the time goes in v6:
time: 107 us; the launch traced here: 106 us
  Pallas kernels  73.8 us (69%)
  local copies, waits for them, and re-layouts  9.67 us (9%)
  other arithmetic  8.98 us (8%)
  waiting for transfers between devices  5.15 us (5%)
  starting transfers between devices  4.69 us (4%)
  matrix products  2.64 us (2%)
    pallas_call x3, Pallas kernels, exchange(): pl.pallas_call(functools.partial(_exchange_kernel, axis, other, n, whole)...  63 us
    pallas_call x2, Pallas kernels, spd_solve(): pl.pallas_call(_eliminate, out_shape=jax.ShapeDtypeStruct(b.shape, b.dtype))  10.7 us
    ppermute x1, waiting for transfers between devices, extended_2(): lax.ppermute(head, axis, [((i + 1) % count, i) for i in range(ends)])  4.67 us
    unnamed x17, local copies, waits for them, and re-layouts  3.56 us
    ppermute x1, starting transfers between devices, extended_2(): lax.ppermute(tail, axis, [(i, (i + 1) % count) for i in range(ends)])  3.4 us
  transfers between devices with their start and end apart: 2, of which 2 were waited for; matrix products, arithmetic and copies ran while one was open for 0% of the time, Pallas kernels for 0%

profile of v6, /device:TPU:24, one launch (start us, length us, event | category | flops | bytes accessed | tf_op | source)
XLA Modules:
  0.0 105.8 jit_solution(2524457368127005821)
XLA Ops:
  0.7 0.9 copy.13
  1.8 0.9 convolution_multiply_fusion.m_ref
  2.7 0.7 multiply_bitcast_fusion.b_ref
  3.4 5.4 %shard_map.50 = f32[64,64]{1,0:T(8,128)} custom-call(f32[64,64]{1,0:T(8,128)} %convolution_multiply_fusion.m_ref, f32[64,64]{1,0:T(8,128)} %multiply_bitcast_fusion.b_ref), custom_call_target="tpu_custom_call" | custom-call | tf_op jit(solution)/shard_map/pallas_call | solution.py:217
  8.7 0.8 convert_element_type.69
  9.5 1.4 %reshape.99 = bf16[64,4096,1]{1,0,2:T(8,128)(2,1)S(1)} reshape(bf16[1,64,4,1024]{3,2,1,0:T(4,128)(2,1)} %param.3) | data formatting | bytes 1048576 | tf_op jit(solution)/shard_map/reshape | solution.py:230
  11.2 1.6 %copy.15.x_ref = f32[16,4,4096]{2,1,0:T(4,128)} copy(f32[16,4,4096]{2,0,1:T(8,128)S(1)} %fusion.37) | data formatting | bytes 2097152 | tf_op jit(solution)/shard_map/dot_general | solution.py:232
  12.8 20.7 %shard_map.51 = f32[16,4,4096]{2,1,0:T(4,128)} custom-call(f32[16,4,4096]{2,1,0:T(4,128)} %copy.15.x_ref), custom_call_target="tpu_custom_call" | custom-call | tf_op jit(solution)/shard_map/pallas_call | solution.py:90
  33.5 1.4 %reduce_sum.36 = f32[4,4096]{1,0:T(4,128)S(1)} reduce(f32[16,4,4096]{2,1,0:T(4,128)} %shard_map.51, f32[]{:T(128)} %constant.25.clone.1), dimensions={0}, to_apply=%region_0.0 | reduce | flops 245760 | bytes 1114116 | tf_op jit(solution)/shard_map/reduce_sum | solution.py:112
  35.1 3.4 %collective-permute-start = (f32[4,3,1024]{2,1,0:T(4,128)S(1)}, f32[4,3,1024]{2,1,0:T(4,128)S(1)}, u32[]{:S(2)}, u32[]{:S(2)}) collective-permute-start(f32[4,3,1024]{2,1,0:T(4,128)S(1)} %get-tuple-element.8), channel_id=1, source_target_pairs={{0,1},{1,2},{2,3},{3,4},{4,5},{5,6},{6,7},{7,8},{8,9},{9,10},{10,1... | collective-permute-start | bytes 147464 | tf_op jit(solution)/shard_map/ppermute | solution.py:31
  38.5 1.3 %collective-permute-start.1 = (f32[4,3,1024]{2,1,0:T(4,128)S(1)}, f32[4,3,1024]{2,1,0:T(4,128)S(1)}, u32[]{:S(2)}, u32[]{:S(2)}) collective-permute-start(f32[4,3,1024]{2,1,0:T(4,128)S(1)} %get-tuple-element.9), channel_id=1, source_target_pairs={{1,0},{2,1},{3,2},{4,3},{5,4},{6,5},{7,6},{8,7},{9,8},{10,9},{11,1... | collective-permute-start | bytes 147464 | tf_op jit(solution)/shard_map/ppermute | solution.py:33
  40.7 4.7 %collective-permute-done.1 = f32[4,3,1024]{2,1,0:T(4,128)S(1)} collective-permute-done((f32[4,3,1024]{2,1,0:T(4,128)S(1)}, f32[4,3,1024]{2,1,0:T(4,128)S(1)}, u32[]{:S(2)}, u32[]{:S(2)}) %collective-permute-start.1) | collective-permute-done | bytes 49184 | tf_op jit(solution)/shard_map/ppermute | solution.py:33
  45.9 0.8 fusion.35.x_ref
  46.8 20.0 %shard_map.52 = f32[16,4,4,1024]{3,2,1,0:T(4,128)} custom-call(f32[4,4,1024]{2,1,0:T(4,128)} %fusion.35.x_ref), custom_call_target="tpu_custom_call" | custom-call | tf_op jit(solution)/shard_map/pallas_call | solution.py:90
  66.8 1.5 %convert_element_type.73 = bf16[16,4,4,1024]{3,2,1,0:T(4,128)(2,1)S(1)} convert(f32[16,4,4,1024]{3,2,1,0:T(4,128)} %shard_map.52) | non-fusion elementwise | flops 262144 | bytes 1572864 | tf_op jit(solution)/shard_map/convert_element_type | solution.py:241
  69.0 1.0 fusion.53
  71.0 0.7 concatenate.16.x_ref
  71.7 22.4 %shard_map.53 = f32[16,2144]{1,0:T(8,128)} custom-call(f32[2144]{0:T(1024)} %concatenate.16.x_ref), custom_call_target="tpu_custom_call" | custom-call | tf_op jit(solution)/shard_map/pallas_call | solution.py:90
  94.1 0.9 reduce_sum.39
  96.0 0.7 copy.21.b_ref
  97.4 0.7 maximum_multiply_fusion.m_ref
  98.1 5.4 %shard_map.54 = f32[64,1]{1,0:T(8,128)} custom-call(f32[64,64]{1,0:T(8,128)} %maximum_multiply_fusion.m_ref, f32[64,1]{1,0:T(8,128)} %copy.21.b_ref), custom_call_target="tpu_custom_call" | custom-call | tf_op jit(solution)/shard_map/pallas_call | solution.py:217
  103.5 1.4 %reduce.2 = f32[64]{0:T(128)} reduce(f32[64,1]{1,0:T(8,128)} %shard_map.54, f32[]{:T(128)} %constant.93), dimensions={1}, to_apply=%pallas_call.19.reduce_sub_computation | reduce | bytes 516 | tf_op jit(solution)/shard_map/pallas_call | solution.py:217
  104.9 1.0 copy.30
  (47 shorter events, 5.4 us)
Async XLA Ops:
  0.6 1.2 %copy-start = (f32[16,64]{1,0:T(8,128)S(1)}, f32[16,64]{1,0:T(8,128)}, u32[]{:S(2)}) copy-start(f32[16,64]{1,0:T(8,128)} %param.4) | copy-start | bytes 12292
  0.6 0.9 copy-start.3
  33.5 6.5 %copy-start.2 = (bf16[1,64,4,1024]{3,2,1,0:T(4,128)(2,1)S(1)}, bf16[1,64,4,1024]{3,2,1,0:T(4,128)(2,1)}, u32[]{:S(2)}) copy-start(bf16[1,64,4,1024]{3,2,1,0:T(4,128)(2,1)} %param.3) | copy-start | bytes 1572868
  35.1 5.6 %collective-permute-start = (f32[4,3,1024]{2,1,0:T(4,128)S(1)}, f32[4,3,1024]{2,1,0:T(4,128)S(1)}, u32[]{:S(2)}, u32[]{:S(2)}) collective-permute-start(f32[4,3,1024]{2,1,0:T(4,128)S(1)} %get-tuple-element.8), channel_id=1, source_target_pairs={{0,1},{1,2},{2,3},{3,4},{4,5},{5,6},{6,7},{7,8},{8,9},{9,10},{10,1... | collective-permute-start | bytes 147464 | tf_op jit(solution)/shard_map/ppermute | solution.py:31
  38.5 6.9 %collective-permute-start.1 = (f32[4,3,1024]{2,1,0:T(4,128)S(1)}, f32[4,3,1024]{2,1,0:T(4,128)S(1)}, u32[]{:S(2)}, u32[]{:S(2)}) collective-permute-start(f32[4,3,1024]{2,1,0:T(4,128)S(1)} %get-tuple-element.9), channel_id=1, source_target_pairs={{1,0},{2,1},{3,2},{4,3},{5,4},{6,5},{7,6},{8,7},{9,8},{10,9},{11,1... | collective-permute-start | bytes 147464 | tf_op jit(solution)/shard_map/ppermute | solution.py:33
  66.8 1.5 %copy-start.1 = (f32[16,4,4,1024]{3,2,1,0:T(4,128)S(1)}, f32[16,4,4,1024]{3,2,1,0:T(4,128)}, u32[]{:S(2)}) copy-start(f32[16,4,4,1024]{3,2,1,0:T(4,128)} %shard_map.52) | copy-start | bytes 3145732
  95.0 0.6 copy-start.4
  96.7 0.7 slice-start

commit v7 on v6

--- a/solution.py
+++ b/solution.py
@@ -101,6 +101,85 @@
     )(x)
 
 
+def _halo_kernel(n, head_ref, tail_ref, below_ref, above_ref, send_sem, recv_sem):
+    me = lax.axis_index("col")
+    fixed = lax.axis_index("cuts")
+    has_left = (me + n - 1) // n
+    has_right = 1 - me // (n - 1)
+    left, right = (fixed, me - has_left), (fixed, me + has_right)
+
+    def to_left():
+        return pltpu.make_async_remote_copy(
+            src_ref=head_ref, dst_ref=above_ref, send_sem=send_sem.at[0],
+            recv_sem=recv_sem.at[1], device_id=left, device_id_type=MESH,
+        )
+
+    def to_right():
+        return pltpu.make_async_remote_copy(
+            src_ref=tail_ref, dst_ref=below_ref, send_sem=send_sem.at[1],
+            recv_sem=recv_sem.at[0], device_id=right, device_id_type=MESH,
+        )
+
+    barrier = pltpu.get_barrier_semaphore()
+
+    @pl.when(me > 0)
+    def _():
+        pl.semaphore_signal(barrier, inc=1, device_id=left, device_id_type=MESH)
+
+    @pl.when(me < n - 1)
+    def _():
+        pl.semaphore_signal(barrier, inc=1, device_id=right, device_id_type=MESH)
+
+    pl.semaphore_wait(barrier, has_left + has_right)
+
+    @pl.when(me == 0)
+    def _():
+        below_ref[...] = jnp.zeros_like(below_ref)
+
+    @pl.when(me == n - 1)
+    def _():
+        above_ref[...] = jnp.zeros_like(above_ref)
+
+    @pl.when(me > 0)
+    def _():
+        to_left().start()
+
+    @pl.when(me < n - 1)
+    def _():
+        to_right().start()
+
+    @pl.when(me > 0)
+    def _():
+        to_left().wait_send()
+        pltpu.make_async_remote_copy(
+            src_ref=tail_ref, dst_ref=below_ref, send_sem=send_sem.at[1],
+            recv_sem=recv_sem.at[0], device_id=left, device_id_type=MESH,
+        ).wait_recv()
+
+    @pl.when(me < n - 1)
+    def _():
+        to_right().wait_send()
+        pltpu.make_async_remote_copy(
+            src_ref=head_ref, dst_ref=above_ref, send_sem=send_sem.at[0],
+            recv_sem=recv_sem.at[1], device_id=right, device_id_type=MESH,
+        ).wait_recv()
+
+
+def with_halo(cells, width):
+    n = lax.axis_size("col")
+    head = lax.slice_in_dim(cells, 0, width, axis=1)
+    tail = lax.slice_in_dim(cells, cells.shape[1] - width, cells.shape[1], axis=1)
+    below, above = pl.pallas_call(
+        functools.partial(_halo_kernel, n),
+        out_shape=(jax.ShapeDtypeStruct(head.shape, head.dtype),) * 2,
+        in_specs=[pl.BlockSpec(memory_space=pltpu.VMEM)] * 2,
+        out_specs=(pl.BlockSpec(memory_space=pltpu.VMEM),) * 2,
+        scratch_shapes=[pltpu.SemaphoreType.DMA((2,)), pltpu.SemaphoreType.DMA((2,))],
+        compiler_params=pltpu.CompilerParams(collective_id=3, has_side_effects=True),
+    )(head, tail)
+    return jnp.concatenate([below, cells, above], axis=1)
+
+
 def split_up(shard, dim, devices):
     before, after = (shard.shape[:dim], shard.shape[dim + 1 :])
     return jnp.moveaxis(shard.reshape(*before, devices, -1, *after), dim, 0)
@@ -157,7 +236,7 @@
 
 def smooth_once(source):
     planes = source.shape[1]
-    extended = extended_2(source, (("col", 1),), ITERS)
+    extended = with_halo(source, ITERS)
     first_plane = lax.axis_index("col") * planes - ITERS
     total_planes = planes * lax.axis_size("col")
     levels = first_plane + jnp.arange(planes + 2 * ITERS, dtype=jnp.int32)

time: 107 us -> 103 us (0.963)
  waiting for transfers between devices: 5.15 us -> 0 us
  starting transfers between devices: 4.69 us -> 0 us
  Pallas kernels: 73.8 us -> 77.5 us
  local copies, waits for them, and re-layouts: 9.67 us -> 11.9 us
    pallas_call x0 -> x1, Pallas kernels: none -> 7.19 us  [with_halo(): pl.pallas_call(functools.partial(_halo_kernel, n), out_shape=(jax.ShapeDt...]
    ppermute x2 -> x0, waiting for transfers between devices: 5.15 us -> none  [the longest x1 4.67 us: extended_2(): lax.ppermute(head, axis, [((i + 1) % count, i) for i in range(ends)])]
    ppermute x2 -> x0, starting transfers between devices: 4.69 us -> none  [the longest x1 3.4 us: extended_2(): lax.ppermute(tail, axis, [(i, (i + 1) % count) for i in range(ends)])]
    pallas_call x3, Pallas kernels: 63 us -> 59.5 us  [exchange(): pl.pallas_call(functools.partial(_exchange_kernel, axis, other, n, whole)...]
    unnamed x17 -> x15, local copies, waits for them, and re-layouts: 3.56 us -> 5.74 us
    convert_element_type x1, other arithmetic: 1.52 us -> 0.23 us  [per_device(): factor_half = factor_flat.astype(jnp.bfloat16)]
  transfers between devices with their start and end apart: 2 -> 0, of which waited for: 2 -> 0; matrix products, arithmetic and copies ran while one was open for 0% -> 0% of each run, Pallas kernels for 0% -> 0%
where the time goes in v7:
time: 103 us; the launch traced here: 101 us
  Pallas kernels  77.5 us (75%)
  local copies, waits for them, and re-layouts  11.9 us (12%)
  other arithmetic  8.53 us (8%)
  matrix products  2.63 us (3%)
    pallas_call x3, Pallas kernels, exchange(): pl.pallas_call(functools.partial(_exchange_kernel, axis, other, n, whole)...  59.5 us
    pallas_call x2, Pallas kernels, spd_solve(): pl.pallas_call(_eliminate, out_shape=jax.ShapeDtypeStruct(b.shape, b.dtype))  10.7 us
    pallas_call x1, Pallas kernels, with_halo(): pl.pallas_call(functools.partial(_halo_kernel, n), out_shape=(jax.ShapeDt...  7.19 us
    unnamed x15, local copies, waits for them, and re-layouts  5.74 us

profile of v7, /device:TPU:24, one launch (start us, length us, event | category | flops | bytes accessed | tf_op | source)
XLA Modules:
  0.0 101.3 jit_solution(1826709509873969511)
XLA Ops:
  0.6 0.7 copy-done
  1.3 0.8 copy.13
  3.2 0.9 convolution_multiply_fusion.m_ref
  4.0 5.4 %shard_map.50 = f32[64,64]{1,0:T(8,128)} custom-call(f32[64,64]{1,0:T(8,128)} %convolution_multiply_fusion.m_ref, f32[64,64]{1,0:T(8,128)} %multiply_bitcast_fusion.b_ref), custom_call_target="tpu_custom_call" | custom-call | tf_op jit(solution)/shard_map/pallas_call | solution.py:296
  9.4 0.8 convert_element_type.69
  10.2 1.4 %reshape.99 = bf16[64,4096,1]{1,0,2:T(8,128)(2,1)S(1)} reshape(bf16[1,64,4,1024]{3,2,1,0:T(4,128)(2,1)} %param.3) | data formatting | bytes 1048576 | tf_op jit(solution)/shard_map/reshape | solution.py:309
  11.9 1.6 %copy.15.x_ref = f32[16,4,4096]{2,1,0:T(4,128)} copy(f32[16,4,4096]{2,0,1:T(8,128)S(1)} %fusion.37) | data formatting | bytes 2097152 | tf_op jit(solution)/shard_map/dot_general | solution.py:311
  13.5 20.7 %shard_map.51 = f32[16,4,4096]{2,1,0:T(4,128)} custom-call(f32[16,4,4096]{2,1,0:T(4,128)} %copy.15.x_ref), custom_call_target="tpu_custom_call" | custom-call | tf_op jit(solution)/shard_map/pallas_call | solution.py:90
  34.2 1.4 %reduce_sum.36 = f32[4,4096]{1,0:T(4,128)S(1)} reduce(f32[16,4,4096]{2,1,0:T(4,128)} %shard_map.51, f32[]{:T(128)} %constant.25.clone.1), dimensions={0}, to_apply=%region_0.0 | reduce | flops 245760 | bytes 1114116 | tf_op jit(solution)/shard_map/reduce_sum | solution.py:191
  36.3 7.2 %shard_map.52 = (f32[4,3,1024]{2,1,0:T(4,128)}, f32[4,3,1024]{2,1,0:T(4,128)}) custom-call(f32[4,3,1024]{2,1,0:T(4,128)} %get-tuple-element.13.head_ref, f32[4,3,1024]{2,1,0:T(4,128)} %get-tuple-element.12.tail_ref), custom_call_target="tpu_custom_call" | custom-call | tf_op jit(solution)/shard_map/pallas_call | solution.py:172
  43.5 1.0 pad_maximum_fusion
  45.3 0.8 fusion.35.x_ref
  46.1 20.0 %shard_map.53 = f32[16,4,4,1024]{3,2,1,0:T(4,128)} custom-call(f32[4,4,1024]{2,1,0:T(4,128)} %fusion.35.x_ref), custom_call_target="tpu_custom_call" | custom-call | tf_op jit(solution)/shard_map/pallas_call | solution.py:90
  66.1 1.8 %copy.24 = f32[8,8,4,1024]{3,1,2,0:T(8,128)S(1)} copy(f32[8,8,4,1024]{3,2,1,0:T(4,128)} %bitcast.45) | data formatting | bytes 2097152
  68.0 1.0 fusion.53
  69.8 0.9 copy-done.2
  71.3 0.7 concatenate.16.x_ref
  72.0 18.8 %shard_map.54 = f32[16,2144]{1,0:T(8,128)} custom-call(f32[2144]{0:T(1024)} %concatenate.16.x_ref), custom_call_target="tpu_custom_call" | custom-call | tf_op jit(solution)/shard_map/pallas_call | solution.py:90
  90.8 0.9 reduce_sum.39
  92.1 0.7 maximum_multiply_fusion.m_ref
  92.9 0.7 copy.21.b_ref
  93.6 5.4 %shard_map.55 = f32[64,1]{1,0:T(8,128)} custom-call(f32[64,64]{1,0:T(8,128)} %maximum_multiply_fusion.m_ref, f32[64,1]{1,0:T(8,128)} %copy.21.b_ref), custom_call_target="tpu_custom_call" | custom-call | tf_op jit(solution)/shard_map/pallas_call | solution.py:296
  99.0 1.4 %reduce.2 = f32[64]{0:T(128)} reduce(f32[64,1]{1,0:T(8,128)} %shard_map.55, f32[]{:T(128)} %constant.93), dimensions={1}, to_apply=%pallas_call.27.reduce_sub_computation | reduce | bytes 516 | tf_op jit(solution)/shard_map/pallas_call | solution.py:296
  100.4 1.0 copy.30
  (41 shorter events, 4.6 us)
Async XLA Ops:
  0.6 0.7 copy-start
  2.2 0.8 copy-start.3
  68.0 1.4 %copy-start.1 = (f32[16,4,4,1024]{3,2,1,0:T(4,128)S(1)}, f32[16,4,4,1024]{3,2,1,0:T(4,128)}, u32[]{:S(2)}) copy-start(f32[16,4,4,1024]{3,2,1,0:T(4,128)} %shard_map.53) | copy-start | bytes 3145732
  69.6 1.0 %copy-start.2 = (bf16[1,64,4,1024]{3,2,1,0:T(4,128)(2,1)S(1)}, bf16[1,64,4,1024]{3,2,1,0:T(4,128)(2,1)}, u32[]{:S(2)}) copy-start(bf16[1,64,4,1024]{3,2,1,0:T(4,128)(2,1)} %param.3) | copy-start | bytes 1572868

commit v8 on v7

--- a/solution.py
+++ b/solution.py
@@ -37,41 +37,44 @@
     return cells
 
 
-def _exchange_kernel(axis, other, n, whole, x_ref, o_ref, send_sem, recv_sem, own_sem):
+def _exchange_kernel(axis, other, size, stride, whole, x_ref, o_ref, send_sem, recv_sem, own_sem):
     me = lax.axis_index(axis)
     fixed = lax.axis_index(other)
-
-    def where(peer):
+    pos = (me // stride) % size
+    base = me - pos * stride
+
+    def where(peer_pos):
+        peer = base + peer_pos * stride
         return (peer, fixed) if axis == "cuts" else (fixed, peer)
 
-    def part(peer):
-        return x_ref if whole else x_ref.at[peer]
+    def part(peer_pos):
+        return x_ref if whole else x_ref.at[peer_pos]
 
     barrier = pltpu.get_barrier_semaphore()
-    for d in range(1, n):
+    for d in range(1, size):
         pl.semaphore_signal(
-            barrier, inc=1, device_id=where(lax.rem(me + d, n)), device_id_type=MESH
-        )
-    pl.semaphore_wait(barrier, n - 1)
-    own = pltpu.make_async_copy(part(me), o_ref.at[me], own_sem)
+            barrier, inc=1, device_id=where((pos + d) % size), device_id_type=MESH
+        )
+    pl.semaphore_wait(barrier, size - 1)
+    own = pltpu.make_async_copy(part(pos), o_ref.at[pos], own_sem)
     own.start()
     copies = []
-    for d in range(1, n):
-        peer = lax.rem(me + d, n)
+    for d in range(1, size):
+        peer_pos = (pos + d) % size
         copy = pltpu.make_async_remote_copy(
-            src_ref=part(peer),
-            dst_ref=o_ref.at[me],
-            send_sem=send_sem.at[peer],
-            recv_sem=recv_sem.at[me],
-            device_id=where(peer),
+            src_ref=part(peer_pos),
+            dst_ref=o_ref.at[pos],
+            send_sem=send_sem.at[peer_pos],
+            recv_sem=recv_sem.at[pos],
+            device_id=where(peer_pos),
             device_id_type=MESH,
         )
         copy.start()
         copies.append(copy)
     for copy in copies:
         copy.wait_send()
-    for d in range(1, n):
-        source = lax.rem(me + n - d, n)
+    for d in range(1, size):
+        source = (pos + size - d) % size
         pltpu.make_async_remote_copy(
             src_ref=part(source),
             dst_ref=o_ref.at[source],
@@ -83,18 +86,18 @@
     own.wait()
 
 
-def exchange(x, axis, key, whole=False):
+def exchange(x, axis, key, whole=False, size=None, stride=1):
     other = "col" if axis == "cuts" else "cuts"
-    n = lax.axis_size(axis)
-    shape = (n, *x.shape) if whole else x.shape
+    size = size or lax.axis_size(axis)
+    shape = (size, *x.shape) if whole else x.shape
     return pl.pallas_call(
-        functools.partial(_exchange_kernel, axis, other, n, whole),
+        functools.partial(_exchange_kernel, axis, other, size, stride, whole),
         out_shape=jax.ShapeDtypeStruct(shape, x.dtype),
         in_specs=[pl.BlockSpec(memory_space=pltpu.VMEM)],
         out_specs=pl.BlockSpec(memory_space=pltpu.VMEM),
         scratch_shapes=[
-            pltpu.SemaphoreType.DMA((n,)),
-            pltpu.SemaphoreType.DMA((n,)),
+            pltpu.SemaphoreType.DMA((size,)),
+            pltpu.SemaphoreType.DMA((size,)),
             pltpu.SemaphoreType.DMA,
         ],
         compiler_params=pltpu.CompilerParams(collective_id=key, has_side_effects=True),
@@ -307,15 +310,18 @@
     coefficients = spd_solve(mix_gram * weight_gram, scaled.reshape(ranks, local_scans * ranks))
     coefficients = coefficients.astype(jnp.bfloat16)
     stacked = data.reshape(local_scans * ranks, planes * cells)
-    portion = sent_and_summed(
-        lax.dot_general(
-            coefficients, stacked, (((1,), (0,)), ((), ())), preferred_element_type=jnp.float32
-        ),
-        "cuts",
-        0,
-    )
+    partial = lax.dot_general(
+        coefficients, stacked, (((1,), (0,)), ((), ())), preferred_element_type=jnp.float32
+    )
+    cores = 2
+    chips = lax.axis_size("cuts") // cores
+    paired = exchange(partial.reshape(cores, chips, -1, planes * cells), "cuts", 0, size=cores)
+    paired = paired.sum(axis=0)
+    portion = exchange(paired, "cuts", 4, size=chips, stride=cores).sum(axis=0)
     smoothed = smooth(portion.reshape(-1, planes, cells))
-    factor = gather_directly(smoothed, "cuts", 0)
+    half_factor = exchange(smoothed, "cuts", 1, whole=True, size=chips, stride=cores)
+    factor = exchange(half_factor, "cuts", 5, whole=True, size=cores)
+    factor = factor.reshape(ranks, planes, cells)
     factor_flat = factor.reshape(ranks, planes * cells)
     factor_half = factor_flat.astype(jnp.bfloat16)
     factor_gram = jnp.dot(factor_flat, factor_flat.T, precision=highest)

time: 103 us -> 94.8 us (0.920)
  Pallas kernels: 77.5 us -> 68.3 us
  other arithmetic: 8.53 us -> 10.7 us
  local copies, waits for them, and re-layouts: 11.9 us -> 10.2 us
    pallas_call x3 -> x5, Pallas kernels: 59.5 us -> 50.7 us  [exchange(): pl.pallas_call(functools.partial(_exchange_kernel, axis, other, size, str...]
    reduce_sum x1 -> x2, other arithmetic: 1.39 us -> 3.54 us  [the longest x1 2.4 us: per_device(): paired = paired.sum(axis=0)]
    dot_general x1 -> x0, local copies, waits for them, and re-layouts: 1.65 us -> none  [per_device(): lax.dot_general(coefficients, stacked, (((1,), (0,)), ((), ())), preferre...]
where the time goes in v8:
time: 94.8 us; the launch traced here: 93.6 us
  Pallas kernels  68.3 us (72%)
  other arithmetic  10.7 us (11%)
  local copies, waits for them, and re-layouts  10.2 us (11%)
  matrix products  3.61 us (4%)
    pallas_call x5, Pallas kernels, exchange(): pl.pallas_call(functools.partial(_exchange_kernel, axis, other, size, str...  50.7 us
    pallas_call x2, Pallas kernels, spd_solve(): pl.pallas_call(_eliminate, out_shape=jax.ShapeDtypeStruct(b.shape, b.dtype))  10.7 us
    pallas_call x1, Pallas kernels, with_halo(): pl.pallas_call(functools.partial(_halo_kernel, n), out_shape=(jax.ShapeDt...  6.78 us
    unnamed x15, local copies, waits for them, and re-layouts  5.74 us
    reduce_sum x1, other arithmetic, per_device(): paired = paired.sum(axis=0)  2.4 us

profile of v8, /device:TPU:24, one launch (start us, length us, event | category | flops | bytes accessed | tf_op | source)
XLA Modules:
  0.0 93.6 jit_solution(12546977083591789480)
XLA Ops:
  1.3 0.8 copy.13
  3.2 0.9 convolution_multiply_fusion.m_ref
  4.0 5.4 %shard_map.50 = f32[64,64]{1,0:T(8,128)} custom-call(f32[64,64]{1,0:T(8,128)} %convolution_multiply_fusion.m_ref, f32[64,64]{1,0:T(8,128)} %multiply_bitcast_fusion.b_ref), custom_call_target="tpu_custom_call" | custom-call | tf_op jit(solution)/shard_map/pallas_call | solution.py:299
  9.4 0.8 convert_element_type.69
  10.2 1.4 %reshape.99 = bf16[64,4096,1,1]{1,0,2,3:T(8,128)(2,1)S(1)} reshape(bf16[1,64,4,1024]{3,2,1,0:T(4,128)(2,1)} %param.3) | data formatting | bytes 1048576 | tf_op jit(solution)/shard_map/reshape | solution.py:312
  11.6 1.3 %fusion.2.x_ref = f32[2,8,4,4096]{3,2,1,0:T(4,128)} fusion(bf16[2,8,4,64]{3,2,1,0:T(4,128)(2,1)S(1)} %bitcast.56, bf16[64,4096,1,1]{1,0,2,3:T(8,128)(2,1)S(1)} %reshape.99), kind=kOutput, calls=%fused_computation.4 | convolution fusion | flops 33554432 | bytes 1581056 | tf_op jit(solution)/shard_map/dot_general | solution.py:313
  12.8 4.2 %shard_map.51 = f32[2,8,4,4096]{3,2,1,0:T(4,128)} custom-call(f32[2,8,4,4096]{3,2,1,0:T(4,128)} %fusion.2.x_ref), custom_call_target="tpu_custom_call" | custom-call | tf_op jit(solution)/shard_map/pallas_call | solution.py:93
  17.0 2.4 %reduce_sum.45.x_ref = f32[8,4,4096]{2,1,0:T(4,128)} reduce(f32[2,8,4,4096]{3,2,1,0:T(4,128)} %shard_map.51, f32[]{:T(128)} %constant.25.clone.1), dimensions={0}, to_apply=%region_0.0 | reduce | flops 131072 | bytes 1572868 | tf_op jit(solution)/shard_map/reduce_sum | solution.py:319
  19.4 13.8 %shard_map.52 = f32[8,4,4096]{2,1,0:T(4,128)} custom-call(f32[8,4,4096]{2,1,0:T(4,128)} %reduce_sum.45.x_ref), custom_call_target="tpu_custom_call" | custom-call | tf_op jit(solution)/shard_map/pallas_call | solution.py:93
  33.3 1.1 %reduce_sum.46 = f32[4,4096]{1,0:T(4,128)S(1)} reduce(f32[8,4,4096]{2,1,0:T(4,128)} %shard_map.52, f32[]{:T(128)} %constant.25.clone.1), dimensions={0}, to_apply=%region_1.0 | reduce | flops 114688 | bytes 589828 | tf_op jit(solution)/shard_map/reduce_sum | solution.py:320
  35.2 6.8 %shard_map.53 = (f32[4,3,1024]{2,1,0:T(4,128)}, f32[4,3,1024]{2,1,0:T(4,128)}) custom-call(f32[4,3,1024]{2,1,0:T(4,128)} %get-tuple-element.13.head_ref, f32[4,3,1024]{2,1,0:T(4,128)} %get-tuple-element.12.tail_ref), custom_call_target="tpu_custom_call" | custom-call | tf_op jit(solution)/shard_map/pallas_call | solution.py:175
  42.0 1.0 %pad_maximum_fusion = (f32[4,10,1024]{2,1,0:T(8,128)S(1)}, f32[4,10,1024]{2,1,0:T(8,128)S(1)}) fusion(f32[4,3,1024]{2,1,0:T(4,128)} %get-tuple-element.5, f32[4,4,1024]{2,1,0:T(4,128)S(1)} %reshape.93, f32[4,3,1024]{2,1,0:T(4,128)} %get-tuple-element.4), kind=kLoop, calls=%fused_computation.6 | loop fusion | flops 122880 | bytes 491520 | tf_op jit(solution)/shard_map/concatenate | solution.py:183
  43.7 0.8 fusion.37.x_ref
  44.5 11.1 %shard_map.54.x_ref = f32[8,4,4,1024]{3,2,1,0:T(4,128)} custom-call(f32[4,4,1024]{2,1,0:T(4,128)} %fusion.37.x_ref), custom_call_target="tpu_custom_call" | custom-call | tf_op jit(solution)/shard_map/pallas_call | solution.py:93
  55.7 4.2 %shard_map.55 = f32[2,8,4,4,1024]{4,3,2,1,0:T(4,128)} custom-call(f32[8,4,4,1024]{3,2,1,0:T(4,128)} %shard_map.54.x_ref), custom_call_target="tpu_custom_call" | custom-call | tf_op jit(solution)/shard_map/pallas_call | solution.py:93
  59.8 1.8 %copy.27 = f32[8,8,4,1024]{3,1,2,0:T(8,128)S(1)} copy(f32[8,8,4,1024]{3,2,1,0:T(4,128)} %bitcast.48) | data formatting | bytes 2097152
  61.7 1.0 %fusion.53 = f32[64,64]{0,1:T(8,128)S(1)} fusion(f32[64,4096]{1,0:T(8,128)S(1)} %bitcast.50), kind=kOutput, calls=%fused_computation.90 | convolution fusion | flops 201326592 | bytes 1064960 | tf_op jit(solution)/shard_map/dot_general | solution.py:327
  63.5 0.9 copy-done.2
  65.6 17.4 %shard_map.56 = f32[16,2144]{1,0:T(8,128)} custom-call(f32[2144]{0:T(1024)} %concatenate.16.x_ref), custom_call_target="tpu_custom_call" | custom-call | tf_op jit(solution)/shard_map/pallas_call | solution.py:93
  83.1 0.9 reduce_sum.49
  84.4 0.7 maximum_multiply_fusion.m_ref
  85.9 5.4 %shard_map.57 = f32[64,1]{1,0:T(8,128)} custom-call(f32[64,64]{1,0:T(8,128)} %maximum_multiply_fusion.m_ref, f32[64,1]{1,0:T(8,128)} %copy.21.b_ref), custom_call_target="tpu_custom_call" | custom-call | tf_op jit(solution)/shard_map/pallas_call | solution.py:299
  91.2 1.4 %reduce.2 = f32[64]{0:T(128)} reduce(f32[64,1]{1,0:T(8,128)} %shard_map.57, f32[]{:T(128)} %constant.93), dimensions={1}, to_apply=%pallas_call.35.reduce_sub_computation | reduce | bytes 516 | tf_op jit(solution)/shard_map/pallas_call | solution.py:299
  92.6 1.0 %copy.31 = f32[64,4,1024]{2,1,0:T(4,128)} copy(f32[64,4,1024]{2,1,0:T(4,128)S(1)} %bitcast.49) | data formatting | bytes 2097152
  (43 shorter events, 6.4 us)
Async XLA Ops:
  0.6 0.7 copy-start
  2.2 0.8 copy-start.3
  61.7 1.4 %copy-start.1 = (f32[2,8,4,4,1024]{4,3,2,1,0:T(4,128)S(1)}, f32[2,8,4,4,1024]{4,3,2,1,0:T(4,128)}, u32[]{:S(2)}) copy-start(f32[2,8,4,4,1024]{4,3,2,1,0:T(4,128)} %shard_map.55) | copy-start | bytes 3145732
  63.3 1.0 %copy-start.2 = (bf16[1,64,4,1024]{3,2,1,0:T(4,128)(2,1)S(1)}, bf16[1,64,4,1024]{3,2,1,0:T(4,128)(2,1)}, u32[]{:S(2)}) copy-start(bf16[1,64,4,1024]{3,2,1,0:T(4,128)(2,1)} %param.3) | copy-start | bytes 1572868

commit v9 on v8

--- a/solution.py
+++ b/solution.py
@@ -37,7 +37,11 @@
     return cells
 
 
-def _exchange_kernel(axis, other, size, stride, whole, x_ref, o_ref, send_sem, recv_sem, own_sem):
+def _exchange_kernel(axis, other, size, stride, whole, summed, x_ref, o_ref, *scratch):
+    if summed:
+        send_sem, recv_sem, own_sem, got = scratch
+    else:
+        (send_sem, recv_sem, own_sem), got = scratch, o_ref
     me = lax.axis_index(axis)
     fixed = lax.axis_index(other)
     pos = (me // stride) % size
@@ -56,14 +60,14 @@
             barrier, inc=1, device_id=where((pos + d) % size), device_id_type=MESH
         )
     pl.semaphore_wait(barrier, size - 1)
-    own = pltpu.make_async_copy(part(pos), o_ref.at[pos], own_sem)
+    own = pltpu.make_async_copy(part(pos), got.at[pos], own_sem)
     own.start()
     copies = []
     for d in range(1, size):
         peer_pos = (pos + d) % size
         copy = pltpu.make_async_remote_copy(
             src_ref=part(peer_pos),
-            dst_ref=o_ref.at[pos],
+            dst_ref=got.at[pos],
             send_sem=send_sem.at[peer_pos],
             recv_sem=recv_sem.at[pos],
             device_id=where(peer_pos),
@@ -77,29 +81,38 @@
         source = (pos + size - d) % size
         pltpu.make_async_remote_copy(
             src_ref=part(source),
-            dst_ref=o_ref.at[source],
+            dst_ref=got.at[source],
             send_sem=send_sem.at[source],
             recv_sem=recv_sem.at[source],
             device_id=where(source),
             device_id_type=MESH,
         ).wait_recv()
     own.wait()
-
-
-def exchange(x, axis, key, whole=False, size=None, stride=1):
+    if summed:
+        total = got[0]
+        for slot in range(1, size):
+            total = total + got[slot]
+        o_ref[...] = total
+
+
+def exchange(x, axis, key, whole=False, size=None, stride=1, summed=False):
     other = "col" if axis == "cuts" else "cuts"
     size = size or lax.axis_size(axis)
     shape = (size, *x.shape) if whole else x.shape
+    scratch = [
+        pltpu.SemaphoreType.DMA((size,)),
+        pltpu.SemaphoreType.DMA((size,)),
+        pltpu.SemaphoreType.DMA,
+    ]
+    if summed:
+        scratch.append(pltpu.VMEM(shape, x.dtype))
+        shape = shape[1:]
     return pl.pallas_call(
-        functools.partial(_exchange_kernel, axis, other, size, stride, whole),
+        functools.partial(_exchange_kernel, axis, other, size, stride, whole, summed),
         out_shape=jax.ShapeDtypeStruct(shape, x.dtype),
         in_specs=[pl.BlockSpec(memory_space=pltpu.VMEM)],
         out_specs=pl.BlockSpec(memory_space=pltpu.VMEM),
-        scratch_shapes=[
-            pltpu.SemaphoreType.DMA((size,)),
-            pltpu.SemaphoreType.DMA((size,)),
-            pltpu.SemaphoreType.DMA,
-        ],
+        scratch_shapes=scratch,
         compiler_params=pltpu.CompilerParams(collective_id=key, has_side_effects=True),
     )(x)
 
@@ -309,27 +322,25 @@
     scaled = (mixing.T[None, :, :] * own_weights[:, :, None]).transpose(1, 0, 2)
     coefficients = spd_solve(mix_gram * weight_gram, scaled.reshape(ranks, local_scans * ranks))
     coefficients = coefficients.astype(jnp.bfloat16)
-    stacked = data.reshape(local_scans * ranks, planes * cells)
     partial = lax.dot_general(
-        coefficients, stacked, (((1,), (0,)), ((), ())), preferred_element_type=jnp.float32
+        coefficients, data.reshape(-1, planes, cells), (((1,), (0,)), ((), ())), preferred_element_type=jnp.float32
     )
     cores = 2
     chips = lax.axis_size("cuts") // cores
-    paired = exchange(partial.reshape(cores, chips, -1, planes * cells), "cuts", 0, size=cores)
-    paired = paired.sum(axis=0)
-    portion = exchange(paired, "cuts", 4, size=chips, stride=cores).sum(axis=0)
+    paired = exchange(
+        partial.reshape(cores, chips, -1, planes, cells), "cuts", 0, size=cores, summed=True
+    )
+    portion = exchange(paired, "cuts", 4, size=chips, stride=cores, summed=True)
     smoothed = smooth(portion.reshape(-1, planes, cells))
     half_factor = exchange(smoothed, "cuts", 1, whole=True, size=chips, stride=cores)
     factor = exchange(half_factor, "cuts", 5, whole=True, size=cores)
     factor = factor.reshape(ranks, planes, cells)
-    factor_flat = factor.reshape(ranks, planes * cells)
-    factor_half = factor_flat.astype(jnp.bfloat16)
-    factor_gram = jnp.dot(factor_flat, factor_flat.T, precision=highest)
+    factor_half = factor.astype(jnp.bfloat16)
+    factor_gram = lax.dot_general(
+        factor, factor, (((1, 2), (1, 2)), ((), ())), precision=highest
+    )
     products = lax.dot_general(
-        data.reshape(local_scans, ranks, planes * cells),
-        factor_half,
-        (((2,), (1,)), ((), ())),
-        preferred_element_type=jnp.float32,
+        data, factor_half, (((2, 3), (1, 2)), ((), ())), preferred_element_type=jnp.float32
     )
     targets = jnp.sum(mixing[None, :, :] * products, axis=1)
     half = ranks // 2

time: 94.8 us -> 91.4 us (0.964)
  other arithmetic: 10.7 us -> 7.13 us
  matrix products: 3.61 us -> 5.92 us
  local copies, waits for them, and re-layouts: 10.2 us -> 8.35 us
    reduce_sum x2 -> x0, other arithmetic: 3.54 us -> none  [the longest x1 2.4 us: per_device(): paired = paired.sum(axis=0)]
    unnamed x15 -> x14, local copies, waits for them, and re-layouts: 5.74 us -> 2.78 us
    dot_general x3, matrix products: 2.53 us -> 4.83 us  [the longest x1 3.68 us: per_device(): lax.dot_general(factor, factor, (((1, 2), (1, 2)), ((), ())), precision=h...]
    dot_general x0 -> x1, local copies, waits for them, and re-layouts: none -> 1.68 us  [per_device(): lax.dot_general(coefficients, data.reshape(-1, planes, cells), (((1,), (0...]
    reshape x2 -> x0, local copies, waits for them, and re-layouts: 1.48 us -> none  [the longest x1 1.41 us: per_device(): stacked = data.reshape(local_scans * ranks, planes * cells)]
where the time goes in v9:
time: 91.4 us; the launch traced here: 90.4 us
  Pallas kernels  68.1 us (75%)
  local copies, waits for them, and re-layouts  8.35 us (9%)
  other arithmetic  7.13 us (8%)
  matrix products  5.92 us (6%)
    pallas_call x5, Pallas kernels, exchange(): pl.pallas_call(functools.partial(_exchange_kernel, axis, other, size, str...  50.6 us
    pallas_call x2, Pallas kernels, spd_solve(): pl.pallas_call(_eliminate, out_shape=jax.ShapeDtypeStruct(b.shape, b.dtype))  10.7 us
    pallas_call x1, Pallas kernels, with_halo(): pl.pallas_call(functools.partial(_halo_kernel, n), out_shape=(jax.ShapeDt...  6.8 us
    dot_general x1, matrix products, per_device(): lax.dot_general(factor, factor, (((1, 2), (1, 2)), ((), ())), precision=h...  3.68 us
    unnamed x14, local copies, waits for them, and re-layouts  2.78 us

profile of v9, /device:TPU:24, one launch (start us, length us, event | category | flops | bytes accessed | tf_op | source)
XLA Modules:
  0.0 90.4 jit_solution(17969710395119324936)
XLA Ops:
  0.7 0.7 copy-done.4
  1.4 0.8 copy.18
  2.2 0.7 multiply_bitcast_fusion.b_ref
  3.2 0.9 convolution_multiply_fusion.m_ref
  4.1 5.4 %shard_map.50 = f32[64,64]{1,0:T(8,128)} custom-call(f32[64,64]{1,0:T(8,128)} %convolution_multiply_fusion.m_ref, f32[64,64]{1,0:T(8,128)} %multiply_bitcast_fusion.b_ref), custom_call_target="tpu_custom_call" | custom-call | tf_op jit(solution)/shard_map/pallas_call | solution.py:312
  9.5 0.8 convert_element_type.69
  10.7 1.7 %copy.21.x_ref = f32[2,8,4,4,1024]{4,3,2,1,0:T(4,128)} copy(f32[2,8,4,4,1024]{4,2,3,1,0:T(4,128)S(1)} %fusion.3) | data formatting | bytes 2097152 | tf_op jit(solution)/shard_map/dot_general | solution.py:325
  12.4 4.1 %shard_map.51.x_ref = f32[8,4,4,1024]{3,2,1,0:T(4,128)} custom-call(f32[2,8,4,4,1024]{4,3,2,1,0:T(4,128)} %copy.21.x_ref), custom_call_target="tpu_custom_call" | custom-call | tf_op jit(solution)/shard_map/pallas_call | solution.py:110
  16.5 13.8 %shard_map.52 = f32[4,4,1024]{2,1,0:T(4,128)} custom-call(f32[8,4,4,1024]{3,2,1,0:T(4,128)} %shard_map.51.x_ref), custom_call_target="tpu_custom_call" | custom-call | tf_op jit(solution)/shard_map/pallas_call | solution.py:110
  30.3 1.6 %fusion.52 = (f32[4,3,1024]{2,1,0:T(4,128)}, f32[4,3,1024]{2,1,0:T(4,128)}) fusion(f32[4,4,1024]{2,1,0:T(4,128)} %shard_map.52), kind=kLoop, calls=%fused_computation.90 | loop fusion | bytes 196608 | tf_op jit(solution)/shard_map/slice | solution.py:187
  31.9 6.8 %shard_map.53 = (f32[4,3,1024]{2,1,0:T(4,128)}, f32[4,3,1024]{2,1,0:T(4,128)}) custom-call(f32[4,3,1024]{2,1,0:T(4,128)} %get-tuple-element.13.head_ref, f32[4,3,1024]{2,1,0:T(4,128)} %get-tuple-element.12.tail_ref), custom_call_target="tpu_custom_call" | custom-call | tf_op jit(solution)/shard_map/pallas_call | solution.py:188
  38.7 1.0 %pad_maximum_fusion = (f32[4,10,1024]{2,1,0:T(8,128)S(1)}, f32[4,10,1024]{2,1,0:T(8,128)S(1)}) fusion(f32[4,3,1024]{2,1,0:T(4,128)} %get-tuple-element.5, f32[4,4,1024]{2,1,0:T(4,128)S(1)} %copy-done.2, f32[4,3,1024]{2,1,0:T(4,128)} %get-tuple-element.4), kind=kLoop, calls=%fused_computation.10 | loop fusion | flops 122880 | bytes 491520 | tf_op jit(solution)/shard_map/concatenate | solution.py:196
  40.5 0.8 fusion.40.x_ref
  41.3 11.1 %shard_map.54.x_ref = f32[8,4,4,1024]{3,2,1,0:T(4,128)} custom-call(f32[4,4,1024]{2,1,0:T(4,128)} %fusion.40.x_ref), custom_call_target="tpu_custom_call" | custom-call | tf_op jit(solution)/shard_map/pallas_call | solution.py:110
  52.4 4.1 %shard_map.55 = f32[2,8,4,4,1024]{4,3,2,1,0:T(4,128)} custom-call(f32[8,4,4,1024]{3,2,1,0:T(4,128)} %shard_map.54.x_ref), custom_call_target="tpu_custom_call" | custom-call | tf_op jit(solution)/shard_map/pallas_call | solution.py:110
  56.6 3.7 %convolution_bitcast_fusion.1 = f32[64,64]{0,1:T(8,128)S(1)} fusion(f32[64,4,1024]{2,1,0:T(4,128)} %bitcast.46), kind=kOutput, calls=%fused_computation.2 | convolution fusion | flops 201326592 | bytes 1064960 | tf_op jit(solution)/shard_map/dot_general | solution.py:339
  61.7 0.7 concatenate.16.x_ref
  62.4 17.4 %shard_map.56 = f32[16,2144]{1,0:T(8,128)} custom-call(f32[2144]{0:T(1024)} %concatenate.16.x_ref), custom_call_target="tpu_custom_call" | custom-call | tf_op jit(solution)/shard_map/pallas_call | solution.py:110
  79.8 0.9 %reduce_sum.29 = f32[2144]{0:T(1024)S(1)} reduce(f32[16,2144]{1,0:T(8,128)} %shard_map.56, f32[]{:T(128)} %constant.56.clone.1), dimensions={0}, to_apply=%region_2.3 | reduce | flops 32160 | bytes 145796 | tf_op jit(solution)/shard_map/reduce_sum | solution.py:225
  81.2 0.7 maximum_multiply_fusion.m_ref
  81.9 0.7 copy.31.b_ref
  82.6 5.4 %shard_map.57 = f32[64,1]{1,0:T(8,128)} custom-call(f32[64,64]{1,0:T(8,128)} %maximum_multiply_fusion.m_ref, f32[64,1]{1,0:T(8,128)} %copy.31.b_ref), custom_call_target="tpu_custom_call" | custom-call | tf_op jit(solution)/shard_map/pallas_call | solution.py:312
  88.0 1.4 %reduce.2 = f32[64]{0:T(128)} reduce(f32[64,1]{1,0:T(8,128)} %shard_map.57, f32[]{:T(128)} %constant.93), dimensions={1}, to_apply=%pallas_call.35.reduce_sub_computation | reduce | bytes 516 | tf_op jit(solution)/shard_map/pallas_call | solution.py:312
  89.4 1.0 %copy.51 = f32[64,4,1024]{2,1,0:T(4,128)} copy(f32[64,4,1024]{2,1,0:T(4,128)S(1)} %bitcast.47) | data formatting | bytes 2097152
  (39 shorter events, 3.4 us)
Async XLA Ops:
  0.6 9.6 %copy-start = (bf16[1,64,4,1024]{3,2,1,0:T(4,128)(2,1)S(1)}, bf16[1,64,4,1024]{3,2,1,0:T(4,128)(2,1)}, u32[]{:S(2)}) copy-start(bf16[1,64,4,1024]{3,2,1,0:T(4,128)(2,1)} %param.3) | copy-start | bytes 1572868
  0.6 0.8 copy-start.4
  2.2 0.8 copy-start.3
  31.9 6.8 %copy-start.2 = (f32[4,4,1024]{2,1,0:T(4,128)S(1)}, f32[4,4,1024]{2,1,0:T(4,128)}, u32[]{:S(2)}) copy-start(f32[4,4,1024]{2,1,0:T(4,128)} %shard_map.52) | copy-start | bytes 196612
  56.6 4.1 %copy-start.1 = (f32[2,8,4,4,1024]{4,3,2,1,0:T(4,128)S(1)}, f32[2,8,4,4,1024]{4,3,2,1,0:T(4,128)}, u32[]{:S(2)}) copy-start(f32[2,8,4,4,1024]{4,3,2,1,0:T(4,128)} %shard_map.55) | copy-start | bytes 3145732

commit v10 on v9

--- a/solution.py
+++ b/solution.py
@@ -95,7 +95,7 @@
         o_ref[...] = total
 
 
-def exchange(x, axis, key, whole=False, size=None, stride=1, summed=False):
+def exchange(x, axis, key, whole=False, size=None, stride=1, summed=False, space=None):
     other = "col" if axis == "cuts" else "cuts"
     size = size or lax.axis_size(axis)
     shape = (size, *x.shape) if whole else x.shape
@@ -111,7 +111,7 @@
         functools.partial(_exchange_kernel, axis, other, size, stride, whole, summed),
         out_shape=jax.ShapeDtypeStruct(shape, x.dtype),
         in_specs=[pl.BlockSpec(memory_space=pltpu.VMEM)],
-        out_specs=pl.BlockSpec(memory_space=pltpu.VMEM),
+        out_specs=pl.BlockSpec(memory_space=space or pltpu.VMEM),
         scratch_shapes=scratch,
         compiler_params=pltpu.CompilerParams(collective_id=key, has_side_effects=True),
     )(x)
@@ -305,11 +305,16 @@
         b = jnp.where(rb == p, t0, jnp.where(rb == q, t1, b - c0 * t0 - c1 * t1))
         return m, b
 
-    o_ref[...] = lax.fori_loop(0, n // 2, step, (m, b), unroll=4)[1]
+    x = lax.fori_loop(0, n // 2, step, (m, b), unroll=4)[1]
+    if o_ref.shape == b.shape:
+        o_ref[...] = x
+    else:
+        o_ref[...] = jnp.sum(jnp.where(ri == ci, x, 0.0), axis=0, keepdims=True)
 
 
 def spd_solve(m, b):
-    return pl.pallas_call(_eliminate, out_shape=jax.ShapeDtypeStruct(b.shape, b.dtype))(m, b)
+    shape = (1, b.shape[0]) if b.shape[1] == 1 else b.shape
+    return pl.pallas_call(_eliminate, out_shape=jax.ShapeDtypeStruct(shape, b.dtype))(m, b)
 
 
 def per_device(data, weights, mixing):
@@ -333,7 +338,7 @@
     portion = exchange(paired, "cuts", 4, size=chips, stride=cores, summed=True)
     smoothed = smooth(portion.reshape(-1, planes, cells))
     half_factor = exchange(smoothed, "cuts", 1, whole=True, size=chips, stride=cores)
-    factor = exchange(half_factor, "cuts", 5, whole=True, size=cores)
+    factor = exchange(half_factor, "cuts", 5, whole=True, size=cores, space=pl.ANY)
     factor = factor.reshape(ranks, planes, cells)
     factor_half = factor.astype(jnp.bfloat16)
     factor_gram = lax.dot_general(
@@ -356,7 +361,7 @@
     factor_gram = jnp.concatenate(
         [jnp.concatenate([top, off], axis=1), jnp.concatenate([off.T, low], axis=1)], axis=0
     )
-    updated = spd_solve(mix_gram * factor_gram, targets.T).T
+    updated = spd_solve(mix_gram * factor_gram, targets.T)
     return (factor, updated)
 
 

time: 91.4 us -> 89.1 us (0.975)
  other arithmetic: 7.13 us -> 5.74 us
    pallas_call x1 -> x0, other arithmetic: 1.38 us -> none  [spd_solve(): pl.pallas_call(_eliminate, out_shape=jax.ShapeDtypeStruct(b.shape, b.dtype))]
where the time goes in v10:
time: 89.1 us; the launch traced here: 88.1 us
  Pallas kernels  67.3 us (76%)
  local copies, waits for them, and re-layouts  8.35 us (9%)
  matrix products  5.92 us (7%)
  other arithmetic  5.74 us (6%)
    pallas_call x5, Pallas kernels, exchange(): pl.pallas_call(functools.partial(_exchange_kernel, axis, other, size, str...  49.7 us
    pallas_call x2, Pallas kernels, spd_solve(): pl.pallas_call(_eliminate, out_shape=jax.ShapeDtypeStruct(shape, b.dtype))  10.7 us
    pallas_call x1, Pallas kernels, with_halo(): pl.pallas_call(functools.partial(_halo_kernel, n), out_shape=(jax.ShapeDt...  6.81 us
    dot_general x1, matrix products, per_device(): lax.dot_general(factor, factor, (((1, 2), (1, 2)), ((), ())), precision=h...  3.67 us
    unnamed x14, local copies, waits for them, and re-layouts  2.77 us

profile of v10, /device:TPU:24, one launch (start us, length us, event | category | flops | bytes accessed | tf_op | source)
XLA Modules:
  0.0 88.1 jit_solution(10921471169852685433)
XLA Ops:
  0.7 0.7 copy-done.4
  1.4 0.8 copy.18
  2.2 0.7 multiply_bitcast_fusion.b_ref
  3.2 0.9 convolution_multiply_fusion.m_ref
  4.1 5.4 %shard_map.50 = f32[64,64]{1,0:T(8,128)} custom-call(f32[64,64]{1,0:T(8,128)} %convolution_multiply_fusion.m_ref, f32[64,64]{1,0:T(8,128)} %multiply_bitcast_fusion.b_ref), custom_call_target="tpu_custom_call" | custom-call | tf_op jit(solution)/shard_map/pallas_call | solution.py:317
  9.5 0.8 convert_element_type.69
  10.7 1.7 %copy.21.x_ref = f32[2,8,4,4,1024]{4,3,2,1,0:T(4,128)} copy(f32[2,8,4,4,1024]{4,2,3,1,0:T(4,128)S(1)} %fusion.3) | data formatting | bytes 2097152 | tf_op jit(solution)/shard_map/dot_general | solution.py:330
  12.4 4.1 %shard_map.51.x_ref = f32[8,4,4,1024]{3,2,1,0:T(4,128)} custom-call(f32[2,8,4,4,1024]{4,3,2,1,0:T(4,128)} %copy.21.x_ref), custom_call_target="tpu_custom_call" | custom-call | tf_op jit(solution)/shard_map/pallas_call | solution.py:110
  16.5 13.8 %shard_map.52 = f32[4,4,1024]{2,1,0:T(4,128)} custom-call(f32[8,4,4,1024]{3,2,1,0:T(4,128)} %shard_map.51.x_ref), custom_call_target="tpu_custom_call" | custom-call | tf_op jit(solution)/shard_map/pallas_call | solution.py:110
  30.3 1.6 %fusion.52 = (f32[4,3,1024]{2,1,0:T(4,128)}, f32[4,3,1024]{2,1,0:T(4,128)}) fusion(f32[4,4,1024]{2,1,0:T(4,128)} %shard_map.52), kind=kLoop, calls=%fused_computation.90 | loop fusion | bytes 196608 | tf_op jit(solution)/shard_map/slice | solution.py:187
  31.9 6.8 %shard_map.53 = (f32[4,3,1024]{2,1,0:T(4,128)}, f32[4,3,1024]{2,1,0:T(4,128)}) custom-call(f32[4,3,1024]{2,1,0:T(4,128)} %get-tuple-element.13.head_ref, f32[4,3,1024]{2,1,0:T(4,128)} %get-tuple-element.12.tail_ref), custom_call_target="tpu_custom_call" | custom-call | tf_op jit(solution)/shard_map/pallas_call | solution.py:188
  38.7 1.0 %pad_maximum_fusion = (f32[4,10,1024]{2,1,0:T(8,128)S(1)}, f32[4,10,1024]{2,1,0:T(8,128)S(1)}) fusion(f32[4,3,1024]{2,1,0:T(4,128)} %get-tuple-element.5, f32[4,4,1024]{2,1,0:T(4,128)S(1)} %copy-done.2, f32[4,3,1024]{2,1,0:T(4,128)} %get-tuple-element.4), kind=kLoop, calls=%fused_computation.10 | loop fusion | flops 122880 | bytes 491520 | tf_op jit(solution)/shard_map/concatenate | solution.py:196
  40.5 0.8 fusion.40.x_ref
  41.3 11.1 %shard_map.54.x_ref = f32[8,4,4,1024]{3,2,1,0:T(4,128)} custom-call(f32[4,4,1024]{2,1,0:T(4,128)} %fusion.40.x_ref), custom_call_target="tpu_custom_call" | custom-call | tf_op jit(solution)/shard_map/pallas_call | solution.py:110
  52.4 3.3 %shard_map.55 = f32[2,8,4,4,1024]{4,3,2,1,0:T(4,128)} custom-call(f32[8,4,4,1024]{3,2,1,0:T(4,128)} %shard_map.54.x_ref), custom_call_target="tpu_custom_call" | custom-call | tf_op jit(solution)/shard_map/pallas_call | solution.py:110
  55.7 3.7 %convolution_bitcast_fusion.1 = f32[64,64]{0,1:T(8,128)S(1)} fusion(f32[64,4,1024]{2,1,0:T(4,128)} %bitcast.45), kind=kOutput, calls=%fused_computation.2 | convolution fusion | flops 201326592 | bytes 1064960 | tf_op jit(solution)/shard_map/dot_general | solution.py:344
  60.0 0.7 fusion.1
  60.8 0.7 concatenate.16.x_ref
  61.5 17.4 %shard_map.56 = f32[16,2144]{1,0:T(8,128)} custom-call(f32[2144]{0:T(1024)} %concatenate.16.x_ref), custom_call_target="tpu_custom_call" | custom-call | tf_op jit(solution)/shard_map/pallas_call | solution.py:110
  79.0 0.9 %reduce_sum.29 = f32[2144]{0:T(1024)S(1)} reduce(f32[16,2144]{1,0:T(8,128)} %shard_map.56, f32[]{:T(128)} %constant.56.clone.1), dimensions={0}, to_apply=%region_2.3 | reduce | flops 32160 | bytes 145796 | tf_op jit(solution)/shard_map/reduce_sum | solution.py:225
  80.3 0.7 maximum_multiply_fusion.m_ref
  81.1 0.7 copy.31.b_ref
  81.8 5.4 %shard_map.57 = f32[1,64]{1,0:T(1,128)} custom-call(f32[64,64]{1,0:T(8,128)} %maximum_multiply_fusion.m_ref, f32[64,1]{1,0:T(8,128)} %copy.31.b_ref), custom_call_target="tpu_custom_call" | custom-call | tf_op jit(solution)/shard_map/pallas_call | solution.py:317
  87.1 1.0 %copy.51 = f32[64,4,1024]{2,1,0:T(4,128)} copy(f32[64,4,1024]{2,1,0:T(4,128)S(1)} %bitcast.46) | data formatting | bytes 2097152
  (38 shorter events, 2.7 us)
Async XLA Ops:
  0.6 9.6 %copy-start = (bf16[1,64,4,1024]{3,2,1,0:T(4,128)(2,1)S(1)}, bf16[1,64,4,1024]{3,2,1,0:T(4,128)(2,1)}, u32[]{:S(2)}) copy-start(bf16[1,64,4,1024]{3,2,1,0:T(4,128)(2,1)} %param.3) | copy-start | bytes 1572868
  0.6 0.8 copy-start.4
  2.2 0.8 copy-start.3
  31.9 6.8 %copy-start.2 = (f32[4,4,1024]{2,1,0:T(4,128)S(1)}, f32[4,4,1024]{2,1,0:T(4,128)}, u32[]{:S(2)}) copy-start(f32[4,4,1024]{2,1,0:T(4,128)} %shard_map.52) | copy-start | bytes 196612
  55.7 4.1 %copy-start.1 = (f32[2,8,4,4,1024]{4,3,2,1,0:T(4,128)S(1)}, f32[2,8,4,4,1024]{4,3,2,1,0:T(4,128)}, u32[]{:S(2)}) copy-start(f32[2,8,4,4,1024]{4,3,2,1,0:T(4,128)} %shard_map.55) | copy-start | bytes 3145732

commit v11 on v10

--- a/solution.py
+++ b/solution.py
@@ -307,14 +307,16 @@
 
     x = lax.fori_loop(0, n // 2, step, (m, b), unroll=4)[1]
     if o_ref.shape == b.shape:
-        o_ref[...] = x
+        o_ref[...] = x.astype(o_ref.dtype)
     else:
         o_ref[...] = jnp.sum(jnp.where(ri == ci, x, 0.0), axis=0, keepdims=True)
 
 
-def spd_solve(m, b):
+def spd_solve(m, b, dtype=None):
     shape = (1, b.shape[0]) if b.shape[1] == 1 else b.shape
-    return pl.pallas_call(_eliminate, out_shape=jax.ShapeDtypeStruct(shape, b.dtype))(m, b)
+    return pl.pallas_call(
+        _eliminate, out_shape=jax.ShapeDtypeStruct(shape, dtype or b.dtype)
+    )(m, b)
 
 
 def per_device(data, weights, mixing):
@@ -325,8 +327,9 @@
         weights, lax.axis_index("cuts") * local_scans, local_scans, 0
     )
     scaled = (mixing.T[None, :, :] * own_weights[:, :, None]).transpose(1, 0, 2)
-    coefficients = spd_solve(mix_gram * weight_gram, scaled.reshape(ranks, local_scans * ranks))
-    coefficients = coefficients.astype(jnp.bfloat16)
+    coefficients = spd_solve(
+        mix_gram * weight_gram, scaled.reshape(ranks, local_scans * ranks), jnp.bfloat16
+    )
     partial = lax.dot_general(
         coefficients, data.reshape(-1, planes, cells), (((1,), (0,)), ((), ())), preferred_element_type=jnp.float32
     )
@@ -342,7 +345,7 @@
     factor = factor.reshape(ranks, planes, cells)
     factor_half = factor.astype(jnp.bfloat16)
     factor_gram = lax.dot_general(
-        factor, factor, (((1, 2), (1, 2)), ((), ())), precision=highest
+        factor, factor, (((1, 2), (1, 2)), ((), ())), precision=lax.Precision.HIGH
     )
     products = lax.dot_general(
         data, factor_half, (((2, 3), (1, 2)), ((), ())), preferred_element_type=jnp.float32

time: 89.1 us -> 88.6 us (level)
  no operation moved by 1% of the time
where the time goes in v11:
time: 88.6 us; the launch traced here: 87.7 us
  Pallas kernels  67.2 us (76%)
  local copies, waits for them, and re-layouts  8.35 us (9%)
  matrix products  6.26 us (7%)
  other arithmetic  5 us (6%)
    pallas_call x5, Pallas kernels, exchange(): pl.pallas_call(functools.partial(_exchange_kernel, axis, other, size, str...  49.7 us
    pallas_call x2, Pallas kernels, spd_solve(): pl.pallas_call(_eliminate, out_shape=jax.ShapeDtypeStruct(shape, dtype or...  10.7 us
    pallas_call x1, Pallas kernels, with_halo(): pl.pallas_call(functools.partial(_halo_kernel, n), out_shape=(jax.ShapeDt...  6.81 us
    dot_general x1, matrix products, per_device(): lax.dot_general(factor, factor, (((1, 2), (1, 2)), ((), ())), precision=l...  3.3 us
    unnamed x14, local copies, waits for them, and re-layouts  2.77 us

profile of v11, /device:TPU:24, one launch (start us, length us, event | category | flops | bytes accessed | tf_op | source)
XLA Modules:
  0.0 87.7 jit_solution(14217660161566466946)
XLA Ops:
  0.7 0.7 copy-done.4
  1.4 0.8 copy.18
  2.2 0.7 multiply_bitcast_fusion.b_ref
  3.2 0.9 convolution_multiply_fusion.m_ref
  4.1 5.4 %shard_map.50 = bf16[64,64]{1,0:T(8,128)(2,1)} custom-call(f32[64,64]{1,0:T(8,128)} %convolution_multiply_fusion.m_ref, f32[64,64]{1,0:T(8,128)} %multiply_bitcast_fusion.b_ref), custom_call_target="tpu_custom_call" | custom-call | tf_op jit(solution)/shard_map/pallas_call | solution.py:317
  9.5 1.2 %fusion.3 = f32[2,8,4,4,1024]{4,2,3,1,0:T(4,128)S(1)} fusion(bf16[2,8,4,64,1]{3,2,4,1,0:T(4,128)(2,1)} %bitcast.49, bf16[64,4,1024,1,1]{2,1,0,4,3:T(4,128)(2,1)S(1)} %bitcast.43), kind=kOutput, calls=%fused_computation.6 | convolution fusion | flops 33554432 | bytes 1581056 | tf_op jit(solution)/shard_map/dot_general | solution.py:333
  10.7 1.7 %copy.21.x_ref = f32[2,8,4,4,1024]{4,3,2,1,0:T(4,128)} copy(f32[2,8,4,4,1024]{4,2,3,1,0:T(4,128)S(1)} %fusion.3) | data formatting | bytes 2097152 | tf_op jit(solution)/shard_map/dot_general | solution.py:333
  12.3 4.1 %shard_map.51.x_ref = f32[8,4,4,1024]{3,2,1,0:T(4,128)} custom-call(f32[2,8,4,4,1024]{4,3,2,1,0:T(4,128)} %copy.21.x_ref), custom_call_target="tpu_custom_call" | custom-call | tf_op jit(solution)/shard_map/pallas_call | solution.py:110
  16.4 13.9 %shard_map.52 = f32[4,4,1024]{2,1,0:T(4,128)} custom-call(f32[8,4,4,1024]{3,2,1,0:T(4,128)} %shard_map.51.x_ref), custom_call_target="tpu_custom_call" | custom-call | tf_op jit(solution)/shard_map/pallas_call | solution.py:110
  30.3 1.6 %fusion.52 = (f32[4,3,1024]{2,1,0:T(4,128)}, f32[4,3,1024]{2,1,0:T(4,128)}) fusion(f32[4,4,1024]{2,1,0:T(4,128)} %shard_map.52), kind=kLoop, calls=%fused_computation.90 | loop fusion | bytes 196608 | tf_op jit(solution)/shard_map/slice | solution.py:187
  31.9 6.8 %shard_map.53 = (f32[4,3,1024]{2,1,0:T(4,128)}, f32[4,3,1024]{2,1,0:T(4,128)}) custom-call(f32[4,3,1024]{2,1,0:T(4,128)} %get-tuple-element.13.head_ref, f32[4,3,1024]{2,1,0:T(4,128)} %get-tuple-element.12.tail_ref), custom_call_target="tpu_custom_call" | custom-call | tf_op jit(solution)/shard_map/pallas_call | solution.py:188
  38.7 1.0 %pad_maximum_fusion = (f32[4,10,1024]{2,1,0:T(8,128)S(1)}, f32[4,10,1024]{2,1,0:T(8,128)S(1)}) fusion(f32[4,3,1024]{2,1,0:T(4,128)} %get-tuple-element.5, f32[4,4,1024]{2,1,0:T(4,128)S(1)} %copy-done.2, f32[4,3,1024]{2,1,0:T(4,128)} %get-tuple-element.4), kind=kLoop, calls=%fused_computation.10 | loop fusion | flops 122880 | bytes 491520 | tf_op jit(solution)/shard_map/concatenate | solution.py:196
  40.4 0.8 fusion.40.x_ref
  41.3 11.1 %shard_map.54.x_ref = f32[8,4,4,1024]{3,2,1,0:T(4,128)} custom-call(f32[4,4,1024]{2,1,0:T(4,128)} %fusion.40.x_ref), custom_call_target="tpu_custom_call" | custom-call | tf_op jit(solution)/shard_map/pallas_call | solution.py:110
  52.4 3.3 %shard_map.55 = f32[2,8,4,4,1024]{4,3,2,1,0:T(4,128)} custom-call(f32[8,4,4,1024]{3,2,1,0:T(4,128)} %shard_map.54.x_ref), custom_call_target="tpu_custom_call" | custom-call | tf_op jit(solution)/shard_map/pallas_call | solution.py:110
  55.6 3.3 %convolution_bitcast_fusion.1 = f32[64,64]{0,1:T(8,128)S(1)} fusion(f32[64,4,1024]{2,1,0:T(4,128)} %bitcast.45), kind=kOutput, calls=%fused_computation.2 | convolution fusion | flops 100663296 | bytes 1064960 | tf_op jit(solution)/shard_map/dot_general | solution.py:347
  59.6 0.7 fusion.1
  60.4 0.7 concatenate.16.x_ref
  61.1 17.4 %shard_map.56 = f32[16,2144]{1,0:T(8,128)} custom-call(f32[2144]{0:T(1024)} %concatenate.16.x_ref), custom_call_target="tpu_custom_call" | custom-call | tf_op jit(solution)/shard_map/pallas_call | solution.py:110
  78.5 0.9 %reduce_sum.29 = f32[2144]{0:T(1024)S(1)} reduce(f32[16,2144]{1,0:T(8,128)} %shard_map.56, f32[]{:T(128)} %constant.56.clone.1), dimensions={0}, to_apply=%region_2.3 | reduce | flops 32160 | bytes 145796 | tf_op jit(solution)/shard_map/reduce_sum | solution.py:225
  79.9 0.7 maximum_multiply_fusion.m_ref
  80.6 0.7 copy.31.b_ref
  81.4 5.4 %shard_map.57 = f32[1,64]{1,0:T(1,128)} custom-call(f32[64,64]{1,0:T(8,128)} %maximum_multiply_fusion.m_ref, f32[64,1]{1,0:T(8,128)} %copy.31.b_ref), custom_call_target="tpu_custom_call" | custom-call | tf_op jit(solution)/shard_map/pallas_call | solution.py:317
  86.7 1.0 %copy.51 = f32[64,4,1024]{2,1,0:T(4,128)} copy(f32[64,4,1024]{2,1,0:T(4,128)S(1)} %bitcast.46) | data formatting | bytes 2097152
  (37 shorter events, 2.3 us)
Async XLA Ops:
  0.6 8.8 %copy-start = (bf16[1,64,4,1024]{3,2,1,0:T(4,128)(2,1)S(1)}, bf16[1,64,4,1024]{3,2,1,0:T(4,128)(2,1)}, u32[]{:S(2)}) copy-start(bf16[1,64,4,1024]{3,2,1,0:T(4,128)(2,1)} %param.3) | copy-start | bytes 1572868
  0.6 0.8 copy-start.4
  2.2 0.8 copy-start.3
  31.9 6.8 %copy-start.2 = (f32[4,4,1024]{2,1,0:T(4,128)S(1)}, f32[4,4,1024]{2,1,0:T(4,128)}, u32[]{:S(2)}) copy-start(f32[4,4,1024]{2,1,0:T(4,128)} %shard_map.52) | copy-start | bytes 196612
  55.6 3.7 %copy-start.1 = (f32[2,8,4,4,1024]{4,3,2,1,0:T(4,128)S(1)}, f32[2,8,4,4,1024]{4,3,2,1,0:T(4,128)}, u32[]{:S(2)}) copy-start(f32[2,8,4,4,1024]{4,3,2,1,0:T(4,128)} %shard_map.55) | copy-start | bytes 3145732

commit v12 on v11

--- a/solution.py
+++ b/solution.py
@@ -222,7 +222,7 @@
 
 
 def taken_together(shard, axis):
-    return from_everyone(shard, axis).sum(axis=0)
+    return exchange(shard, axis, 2, whole=True, summed=True)
 
 
 def packed_total(arrays, axis):

time: 88.6 us -> 89.1 us (level)
  local copies, waits for them, and re-layouts: 8.35 us -> 9.72 us
  other arithmetic: 5 us -> 4.05 us
    slice x2 -> x3, local copies, waits for them, and re-layouts: 0.01 us -> 1.36 us  [packed_total(): done.append(running[at:at + a.size].reshape(a.shape))]
    reduce_sum x1 -> x0, other arithmetic: 0.93 us -> none  [taken_together(): return from_everyone(shard, axis).sum(axis=0)]
    unnamed x14 -> x16, local copies, waits for them, and re-layouts: 2.77 us -> 2.78 us
where the time goes in v12:
time: 89.1 us; the launch traced here: 88.1 us
  Pallas kernels  67.2 us (75%)
  local copies, waits for them, and re-layouts  9.72 us (11%)
  matrix products  6.26 us (7%)
  other arithmetic  4.05 us (5%)
    pallas_call x5, Pallas kernels, exchange(): pl.pallas_call(functools.partial(_exchange_kernel, axis, other, size, str...  49.7 us
    pallas_call x2, Pallas kernels, spd_solve(): pl.pallas_call(_eliminate, out_shape=jax.ShapeDtypeStruct(shape, dtype or...  10.7 us
    pallas_call x1, Pallas kernels, with_halo(): pl.pallas_call(functools.partial(_halo_kernel, n), out_shape=(jax.ShapeDt...  6.81 us
    dot_general x1, matrix products, per_device(): lax.dot_general(factor, factor, (((1, 2), (1, 2)), ((), ())), precision=l...  3.3 us
    unnamed x16, local copies, waits for them, and re-layouts  2.78 us

profile of v12, /device:TPU:24, one launch (start us, length us, event | category | flops | bytes accessed | tf_op | source)
XLA Modules:
  0.0 88.1 jit_solution(13549979630204265665)
XLA Ops:
  0.7 0.7 copy-done.5
  1.4 0.8 copy.18
  2.2 0.7 multiply_bitcast_fusion.b_ref
  3.2 0.9 convolution_multiply_fusion.m_ref
  4.1 5.4 %shard_map.50 = bf16[64,64]{1,0:T(8,128)(2,1)} custom-call(f32[64,64]{1,0:T(8,128)} %convolution_multiply_fusion.m_ref, f32[64,64]{1,0:T(8,128)} %multiply_bitcast_fusion.b_ref), custom_call_target="tpu_custom_call" | custom-call | tf_op jit(solution)/shard_map/pallas_call | solution.py:317
  9.5 1.2 %fusion.3 = f32[2,8,4,4,1024]{4,2,3,1,0:T(4,128)S(1)} fusion(bf16[2,8,4,64,1]{3,2,4,1,0:T(4,128)(2,1)} %bitcast.49, bf16[64,4,1024,1,1]{2,1,0,4,3:T(4,128)(2,1)S(1)} %bitcast.43), kind=kOutput, calls=%fused_computation.6 | convolution fusion | flops 33554432 | bytes 1581056 | tf_op jit(solution)/shard_map/dot_general | solution.py:333
  10.7 1.7 %copy.21.x_ref = f32[2,8,4,4,1024]{4,3,2,1,0:T(4,128)} copy(f32[2,8,4,4,1024]{4,2,3,1,0:T(4,128)S(1)} %fusion.3) | data formatting | bytes 2097152 | tf_op jit(solution)/shard_map/dot_general | solution.py:333
  12.3 4.1 %shard_map.51.x_ref = f32[8,4,4,1024]{3,2,1,0:T(4,128)} custom-call(f32[2,8,4,4,1024]{4,3,2,1,0:T(4,128)} %copy.21.x_ref), custom_call_target="tpu_custom_call" | custom-call | tf_op jit(solution)/shard_map/pallas_call | solution.py:110
  16.4 13.9 %shard_map.52 = f32[4,4,1024]{2,1,0:T(4,128)} custom-call(f32[8,4,4,1024]{3,2,1,0:T(4,128)} %shard_map.51.x_ref), custom_call_target="tpu_custom_call" | custom-call | tf_op jit(solution)/shard_map/pallas_call | solution.py:110
  30.3 1.6 %fusion.52 = (f32[4,3,1024]{2,1,0:T(4,128)}, f32[4,3,1024]{2,1,0:T(4,128)}) fusion(f32[4,4,1024]{2,1,0:T(4,128)} %shard_map.52), kind=kLoop, calls=%fused_computation.90 | loop fusion | bytes 196608 | tf_op jit(solution)/shard_map/slice | solution.py:187
  31.9 6.8 %shard_map.53 = (f32[4,3,1024]{2,1,0:T(4,128)}, f32[4,3,1024]{2,1,0:T(4,128)}) custom-call(f32[4,3,1024]{2,1,0:T(4,128)} %get-tuple-element.13.head_ref, f32[4,3,1024]{2,1,0:T(4,128)} %get-tuple-element.12.tail_ref), custom_call_target="tpu_custom_call" | custom-call | tf_op jit(solution)/shard_map/pallas_call | solution.py:188
  38.7 0.9 %pad_maximum_fusion = (f32[4,10,1024]{2,1,0:T(8,128)S(1)}, f32[4,10,1024]{2,1,0:T(8,128)S(1)}) fusion(f32[4,3,1024]{2,1,0:T(4,128)} %get-tuple-element.5, f32[4,4,1024]{2,1,0:T(4,128)S(1)} %copy-done.2, f32[4,3,1024]{2,1,0:T(4,128)} %get-tuple-element.4), kind=kLoop, calls=%fused_computation.10 | loop fusion | flops 122880 | bytes 491520 | tf_op jit(solution)/shard_map/concatenate | solution.py:196
  40.4 0.8 fusion.40.x_ref
  41.3 11.1 %shard_map.54.x_ref = f32[8,4,4,1024]{3,2,1,0:T(4,128)} custom-call(f32[4,4,1024]{2,1,0:T(4,128)} %fusion.40.x_ref), custom_call_target="tpu_custom_call" | custom-call | tf_op jit(solution)/shard_map/pallas_call | solution.py:110
  52.4 3.3 %shard_map.55 = f32[2,8,4,4,1024]{4,3,2,1,0:T(4,128)} custom-call(f32[8,4,4,1024]{3,2,1,0:T(4,128)} %shard_map.54.x_ref), custom_call_target="tpu_custom_call" | custom-call | tf_op jit(solution)/shard_map/pallas_call | solution.py:110
  55.7 3.3 %convolution_bitcast_fusion.1 = f32[64,64]{0,1:T(8,128)S(1)} fusion(f32[64,4,1024]{2,1,0:T(4,128)} %bitcast.45), kind=kOutput, calls=%fused_computation.2 | convolution fusion | flops 100663296 | bytes 1064960 | tf_op jit(solution)/shard_map/dot_general | solution.py:347
  59.6 0.7 fusion.1
  60.4 0.7 concatenate.16.x_ref
  61.1 17.4 %shard_map.56 = f32[2144]{0:T(1024)} custom-call(f32[2144]{0:T(1024)} %concatenate.16.x_ref), custom_call_target="tpu_custom_call" | custom-call | tf_op jit(solution)/shard_map/pallas_call | solution.py:110
  78.5 0.7 fusion.54
  80.3 0.7 maximum_multiply_fusion.m_ref
  81.0 0.7 copy.31.b_ref
  81.8 5.4 %shard_map.57 = f32[1,64]{1,0:T(1,128)} custom-call(f32[64,64]{1,0:T(8,128)} %maximum_multiply_fusion.m_ref, f32[64,1]{1,0:T(8,128)} %copy.31.b_ref), custom_call_target="tpu_custom_call" | custom-call | tf_op jit(solution)/shard_map/pallas_call | solution.py:317
  87.1 1.0 %copy.51 = f32[64,4,1024]{2,1,0:T(4,128)} copy(f32[64,4,1024]{2,1,0:T(4,128)S(1)} %bitcast.46) | data formatting | bytes 2097152
  (39 shorter events, 2.9 us)
Async XLA Ops:
  0.6 8.8 %copy-start = (bf16[1,64,4,1024]{3,2,1,0:T(4,128)(2,1)S(1)}, bf16[1,64,4,1024]{3,2,1,0:T(4,128)(2,1)}, u32[]{:S(2)}) copy-start(bf16[1,64,4,1024]{3,2,1,0:T(4,128)(2,1)} %param.3) | copy-start | bytes 1572868
  0.6 0.8 copy-start.5
  2.2 0.8 copy-start.3
  31.9 6.8 %copy-start.2 = (f32[4,4,1024]{2,1,0:T(4,128)S(1)}, f32[4,4,1024]{2,1,0:T(4,128)}, u32[]{:S(2)}) copy-start(f32[4,4,1024]{2,1,0:T(4,128)} %shard_map.52) | copy-start | bytes 196612
  55.7 3.7 %copy-start.1 = (f32[2,8,4,4,1024]{4,3,2,1,0:T(4,128)S(1)}, f32[2,8,4,4,1024]{4,3,2,1,0:T(4,128)}, u32[]{:S(2)}) copy-start(f32[2,8,4,4,1024]{4,3,2,1,0:T(4,128)} %shard_map.55) | copy-start | bytes 3145732
  79.4 0.7 slice-start
  80.3 0.7 copy-start.4

commit v13 on v11

--- a/solution.py
+++ b/solution.py
@@ -305,7 +305,7 @@
         b = jnp.where(rb == p, t0, jnp.where(rb == q, t1, b - c0 * t0 - c1 * t1))
         return m, b
 
-    x = lax.fori_loop(0, n // 2, step, (m, b), unroll=4)[1]
+    x = lax.fori_loop(0, n // 2, step, (m, b), unroll=True)[1]
     if o_ref.shape == b.shape:
         o_ref[...] = x.astype(o_ref.dtype)
     else:

time: 88.6 us -> 87.9 us (level)
  no operation moved by 1% of the time
where the time goes in v13:
time: 87.9 us; the launch traced here: 87 us
  Pallas kernels  66.5 us (76%)
  local copies, waits for them, and re-layouts  8.35 us (9%)
  matrix products  6.26 us (7%)
  other arithmetic  5 us (6%)
    pallas_call x5, Pallas kernels, exchange(): pl.pallas_call(functools.partial(_exchange_kernel, axis, other, size, str...  49.7 us
    pallas_call x2, Pallas kernels, spd_solve(): pl.pallas_call(_eliminate, out_shape=jax.ShapeDtypeStruct(shape, dtype or...  10 us
    pallas_call x1, Pallas kernels, with_halo(): pl.pallas_call(functools.partial(_halo_kernel, n), out_shape=(jax.ShapeDt...  6.81 us
    dot_general x1, matrix products, per_device(): lax.dot_general(factor, factor, (((1, 2), (1, 2)), ((), ())), precision=l...  3.3 us
    unnamed x14, local copies, waits for them, and re-layouts  2.77 us

profile of v13, /device:TPU:24, one launch (start us, length us, event | category | flops | bytes accessed | tf_op | source)
XLA Modules:
  0.0 87.0 jit_solution(6305951112242842001)
XLA Ops:
  0.7 0.7 copy-done.4
  1.4 0.8 copy.18
  2.2 0.7 multiply_bitcast_fusion.b_ref
  3.2 0.9 convolution_multiply_fusion.m_ref
  4.1 5.0 %shard_map.50 = bf16[64,64]{1,0:T(8,128)(2,1)} custom-call(f32[64,64]{1,0:T(8,128)} %convolution_multiply_fusion.m_ref, f32[64,64]{1,0:T(8,128)} %multiply_bitcast_fusion.b_ref), custom_call_target="tpu_custom_call" | custom-call | tf_op jit(solution)/shard_map/pallas_call | solution.py:317
  9.1 1.2 %fusion.3 = f32[2,8,4,4,1024]{4,2,3,1,0:T(4,128)S(1)} fusion(bf16[2,8,4,64,1]{3,2,4,1,0:T(4,128)(2,1)} %bitcast.49, bf16[64,4,1024,1,1]{2,1,0,4,3:T(4,128)(2,1)S(1)} %bitcast.43), kind=kOutput, calls=%fused_computation.6 | convolution fusion | flops 33554432 | bytes 1581056 | tf_op jit(solution)/shard_map/dot_general | solution.py:333
  10.3 1.7 %copy.21.x_ref = f32[2,8,4,4,1024]{4,3,2,1,0:T(4,128)} copy(f32[2,8,4,4,1024]{4,2,3,1,0:T(4,128)S(1)} %fusion.3) | data formatting | bytes 2097152 | tf_op jit(solution)/shard_map/dot_general | solution.py:333
  12.0 4.1 %shard_map.51.x_ref = f32[8,4,4,1024]{3,2,1,0:T(4,128)} custom-call(f32[2,8,4,4,1024]{4,3,2,1,0:T(4,128)} %copy.21.x_ref), custom_call_target="tpu_custom_call" | custom-call | tf_op jit(solution)/shard_map/pallas_call | solution.py:110
  16.1 13.9 %shard_map.52 = f32[4,4,1024]{2,1,0:T(4,128)} custom-call(f32[8,4,4,1024]{3,2,1,0:T(4,128)} %shard_map.51.x_ref), custom_call_target="tpu_custom_call" | custom-call | tf_op jit(solution)/shard_map/pallas_call | solution.py:110
  29.9 1.6 %fusion.52 = (f32[4,3,1024]{2,1,0:T(4,128)}, f32[4,3,1024]{2,1,0:T(4,128)}) fusion(f32[4,4,1024]{2,1,0:T(4,128)} %shard_map.52), kind=kLoop, calls=%fused_computation.90 | loop fusion | bytes 196608 | tf_op jit(solution)/shard_map/slice | solution.py:187
  31.5 6.8 %shard_map.53 = (f32[4,3,1024]{2,1,0:T(4,128)}, f32[4,3,1024]{2,1,0:T(4,128)}) custom-call(f32[4,3,1024]{2,1,0:T(4,128)} %get-tuple-element.13.head_ref, f32[4,3,1024]{2,1,0:T(4,128)} %get-tuple-element.12.tail_ref), custom_call_target="tpu_custom_call" | custom-call | tf_op jit(solution)/shard_map/pallas_call | solution.py:188
  38.3 1.0 %pad_maximum_fusion = (f32[4,10,1024]{2,1,0:T(8,128)S(1)}, f32[4,10,1024]{2,1,0:T(8,128)S(1)}) fusion(f32[4,3,1024]{2,1,0:T(4,128)} %get-tuple-element.5, f32[4,4,1024]{2,1,0:T(4,128)S(1)} %copy-done.2, f32[4,3,1024]{2,1,0:T(4,128)} %get-tuple-element.4), kind=kLoop, calls=%fused_computation.10 | loop fusion | flops 122880 | bytes 491520 | tf_op jit(solution)/shard_map/concatenate | solution.py:196
  40.1 0.8 fusion.40.x_ref
  40.9 11.1 %shard_map.54.x_ref = f32[8,4,4,1024]{3,2,1,0:T(4,128)} custom-call(f32[4,4,1024]{2,1,0:T(4,128)} %fusion.40.x_ref), custom_call_target="tpu_custom_call" | custom-call | tf_op jit(solution)/shard_map/pallas_call | solution.py:110
  52.0 3.3 %shard_map.55 = f32[2,8,4,4,1024]{4,3,2,1,0:T(4,128)} custom-call(f32[8,4,4,1024]{3,2,1,0:T(4,128)} %shard_map.54.x_ref), custom_call_target="tpu_custom_call" | custom-call | tf_op jit(solution)/shard_map/pallas_call | solution.py:110
  55.3 3.3 %convolution_bitcast_fusion.1 = f32[64,64]{0,1:T(8,128)S(1)} fusion(f32[64,4,1024]{2,1,0:T(4,128)} %bitcast.45), kind=kOutput, calls=%fused_computation.2 | convolution fusion | flops 100663296 | bytes 1064960 | tf_op jit(solution)/shard_map/dot_general | solution.py:347
  59.2 0.7 fusion.1
  60.1 0.7 concatenate.16.x_ref
  60.8 17.4 %shard_map.56 = f32[16,2144]{1,0:T(8,128)} custom-call(f32[2144]{0:T(1024)} %concatenate.16.x_ref), custom_call_target="tpu_custom_call" | custom-call | tf_op jit(solution)/shard_map/pallas_call | solution.py:110
  78.2 0.9 %reduce_sum.29 = f32[2144]{0:T(1024)S(1)} reduce(f32[16,2144]{1,0:T(8,128)} %shard_map.56, f32[]{:T(128)} %constant.56.clone.1), dimensions={0}, to_apply=%region_2.3 | reduce | flops 32160 | bytes 145796 | tf_op jit(solution)/shard_map/reduce_sum | solution.py:225
  79.5 0.7 maximum_multiply_fusion.m_ref
  80.3 0.7 copy.31.b_ref
  81.0 5.0 %shard_map.57 = f32[1,64]{1,0:T(1,128)} custom-call(f32[64,64]{1,0:T(8,128)} %maximum_multiply_fusion.m_ref, f32[64,1]{1,0:T(8,128)} %copy.31.b_ref), custom_call_target="tpu_custom_call" | custom-call | tf_op jit(solution)/shard_map/pallas_call | solution.py:317
  86.0 1.0 %copy.51 = f32[64,4,1024]{2,1,0:T(4,128)} copy(f32[64,4,1024]{2,1,0:T(4,128)S(1)} %bitcast.46) | data formatting | bytes 2097152
  (37 shorter events, 2.3 us)
Async XLA Ops:
  0.6 8.5 %copy-start = (bf16[1,64,4,1024]{3,2,1,0:T(4,128)(2,1)S(1)}, bf16[1,64,4,1024]{3,2,1,0:T(4,128)(2,1)}, u32[]{:S(2)}) copy-start(bf16[1,64,4,1024]{3,2,1,0:T(4,128)(2,1)} %param.3) | copy-start | bytes 1572868
  0.6 0.8 copy-start.4
  2.2 0.8 copy-start.3
  31.5 6.8 %copy-start.2 = (f32[4,4,1024]{2,1,0:T(4,128)S(1)}, f32[4,4,1024]{2,1,0:T(4,128)}, u32[]{:S(2)}) copy-start(f32[4,4,1024]{2,1,0:T(4,128)} %shard_map.52) | copy-start | bytes 196612
  55.3 3.7 %copy-start.1 = (f32[2,8,4,4,1024]{4,3,2,1,0:T(4,128)S(1)}, f32[2,8,4,4,1024]{4,3,2,1,0:T(4,128)}, u32[]{:S(2)}) copy-start(f32[2,8,4,4,1024]{4,3,2,1,0:T(4,128)} %shard_map.55) | copy-start | bytes 3145732

commit v14 on v13

--- a/solution.py
+++ b/solution.py
@@ -196,6 +196,139 @@
     return jnp.concatenate([below, cells, above], axis=1)
 
 
+def _scatter_halo_kernel(size, stride, n, width, x_ref, o_ref, below_ref, above_ref,
+                         got, head_buf, tail_buf, send_sem, recv_sem, own_sem, hsend, hrecv):
+    me = lax.axis_index("cuts")
+    cm = lax.axis_index("col")
+    pos = (me // stride) % size
+    base = me - pos * stride
+    has_left = (cm + n - 1) // n
+    has_right = 1 - cm // (n - 1)
+    left, right = (me, cm - has_left), (me, cm + has_right)
+
+    def where(peer_pos):
+        return (base + peer_pos * stride, cm)
+
+    barrier = pltpu.get_barrier_semaphore()
+    for d in range(1, size):
+        pl.semaphore_signal(
+            barrier, inc=1, device_id=where((pos + d) % size), device_id_type=MESH
+        )
+
+    @pl.when(cm > 0)
+    def _():
+        pl.semaphore_signal(barrier, inc=1, device_id=left, device_id_type=MESH)
+
+    @pl.when(cm < n - 1)
+    def _():
+        pl.semaphore_signal(barrier, inc=1, device_id=right, device_id_type=MESH)
+
+    pl.semaphore_wait(barrier, size - 1 + has_left + has_right)
+
+    @pl.when(cm == 0)
+    def _():
+        below_ref[...] = jnp.zeros_like(below_ref)
+
+    @pl.when(cm == n - 1)
+    def _():
+        above_ref[...] = jnp.zeros_like(above_ref)
+
+    own = pltpu.make_async_copy(x_ref.at[pos], got.at[pos], own_sem)
+    own.start()
+    copies = []
+    for d in range(1, size):
+        peer_pos = (pos + d) % size
+        copy = pltpu.make_async_remote_copy(
+            src_ref=x_ref.at[peer_pos], dst_ref=got.at[pos],
+            send_sem=send_sem.at[peer_pos], recv_sem=recv_sem.at[pos],
+            device_id=where(peer_pos), device_id_type=MESH,
+        )
+        copy.start()
+        copies.append(copy)
+    for copy in copies:
+        copy.wait_send()
+    for d in range(1, size):
+        source = (pos + size - d) % size
+        pltpu.make_async_remote_copy(
+            src_ref=x_ref.at[source], dst_ref=got.at[source],
+            send_sem=send_sem.at[source], recv_sem=recv_sem.at[source],
+            device_id=where(source), device_id_type=MESH,
+        ).wait_recv()
+    own.wait()
+    total = got[0]
+    for slot in range(1, size):
+        total = total + got[slot]
+    o_ref[...] = total
+    planes = total.shape[1]
+    head_buf[...] = total[:, :width]
+    tail_buf[...] = total[:, planes - width :]
+
+    def to_left():
+        return pltpu.make_async_remote_copy(
+            src_ref=head_buf, dst_ref=above_ref, send_sem=hsend.at[0],
+            recv_sem=hrecv.at[1], device_id=left, device_id_type=MESH,
+        )
+
+    def to_right():
+        return pltpu.make_async_remote_copy(
+            src_ref=tail_buf, dst_ref=below_ref, send_sem=hsend.at[1],
+            recv_sem=hrecv.at[0], device_id=right, device_id_type=MESH,
+        )
+
+    @pl.when(cm > 0)
+    def _():
+        to_left().start()
+
+    @pl.when(cm < n - 1)
+    def _():
+        to_right().start()
+
+    @pl.when(cm > 0)
+    def _():
+        to_left().wait_send()
+        pltpu.make_async_remote_copy(
+            src_ref=tail_buf, dst_ref=below_ref, send_sem=hsend.at[1],
+            recv_sem=hrecv.at[0], device_id=left, device_id_type=MESH,
+        ).wait_recv()
+
+    @pl.when(cm < n - 1)
+    def _():
+        to_right().wait_send()
+        pltpu.make_async_remote_copy(
+            src_ref=head_buf, dst_ref=above_ref, send_sem=hsend.at[0],
+            recv_sem=hrecv.at[1], device_id=right, device_id_type=MESH,
+        ).wait_recv()
+
+
+def scatter_with_halo(x, size, stride, width):
+    n = lax.axis_size("col")
+    block = x.shape[1:]
+    halo = (block[0], width, *block[2:])
+    vmem = pl.BlockSpec(memory_space=pltpu.VMEM)
+    portion, below, above = pl.pallas_call(
+        functools.partial(_scatter_halo_kernel, size, stride, n, width),
+        out_shape=(
+            jax.ShapeDtypeStruct(block, x.dtype),
+            jax.ShapeDtypeStruct(halo, x.dtype),
+            jax.ShapeDtypeStruct(halo, x.dtype),
+        ),
+        in_specs=[vmem],
+        out_specs=(vmem, vmem, vmem),
+        scratch_shapes=[
+            pltpu.VMEM(x.shape, x.dtype),
+            pltpu.VMEM(halo, x.dtype),
+            pltpu.VMEM(halo, x.dtype),
+            pltpu.SemaphoreType.DMA((size,)),
+            pltpu.SemaphoreType.DMA((size,)),
+            pltpu.SemaphoreType.DMA,
+            pltpu.SemaphoreType.DMA((2,)),
+            pltpu.SemaphoreType.DMA((2,)),
+        ],
+        compiler_params=pltpu.CompilerParams(collective_id=4, has_side_effects=True),
+    )(x)
+    return portion, jnp.concatenate([below, portion, above], axis=1)
+
+
 def split_up(shard, dim, devices):
     before, after = (shard.shape[:dim], shard.shape[dim + 1 :])
     return jnp.moveaxis(shard.reshape(*before, devices, -1, *after), dim, 0)
@@ -250,9 +383,8 @@
     return interior + strength * (6.0 * interior - neighbours)
 
 
-def smooth_once(source):
+def smooth_once(source, extended):
     planes = source.shape[1]
-    extended = with_halo(source, ITERS)
     first_plane = lax.axis_index("col") * planes - ITERS
     total_planes = planes * lax.axis_size("col")
     levels = first_plane + jnp.arange(planes + 2 * ITERS, dtype=jnp.int32)
@@ -272,10 +404,6 @@
     return solution + direction
 
 
-def smooth(source):
-    return smooth_once(source)
-
-
 def _eliminate(m_ref, b_ref, o_ref):
     m = m_ref[...]
     b = b_ref[...]
@@ -338,8 +466,8 @@
     paired = exchange(
         partial.reshape(cores, chips, -1, planes, cells), "cuts", 0, size=cores, summed=True
     )
-    portion = exchange(paired, "cuts", 4, size=chips, stride=cores, summed=True)
-    smoothed = smooth(portion.reshape(-1, planes, cells))
+    portion, extended = scatter_with_halo(paired, chips, cores, ITERS)
+    smoothed = smooth_once(portion, extended)
     half_factor = exchange(smoothed, "cuts", 1, whole=True, size=chips, stride=cores)
     factor = exchange(half_factor, "cuts", 5, whole=True, size=cores, space=pl.ANY)
     factor = factor.reshape(ranks, planes, cells)

time: 87.9 us -> 83.2 us (0.947)
  Pallas kernels: 66.5 us -> 63.6 us
  local copies, waits for them, and re-layouts: 8.35 us -> 6.76 us
    pallas_call x5 -> x4, Pallas kernels: 49.7 us -> 35.9 us  [exchange(): pl.pallas_call(functools.partial(_exchange_kernel, axis, other, size, str...]
    pallas_call x1, Pallas kernels: 6.81 us -> 17.7 us  [scatter_with_halo(): pl.pallas_call(functools.partial(_scatter_halo_kernel, size, stride, n, w...]
    slice x1 -> x0, local copies, waits for them, and re-layouts: 1.59 us -> none  [with_halo(): lax.slice_in_dim(cells, cells.shape[1] - width, cells.shape[1], axis=1)]
    unnamed x14 -> x12, local copies, waits for them, and re-layouts: 2.77 us -> 2.77 us
where the time goes in v14:
time: 83.2 us; the launch traced here: 82.5 us
  Pallas kernels  63.6 us (76%)
  local copies, waits for them, and re-layouts  6.76 us (8%)
  matrix products  6.26 us (8%)
  other arithmetic  5.02 us (6%)
    pallas_call x4, Pallas kernels, exchange(): pl.pallas_call(functools.partial(_exchange_kernel, axis, other, size, str...  35.9 us
    pallas_call x1, Pallas kernels, scatter_with_halo(): pl.pallas_call(functools.partial(_scatter_halo_kernel, size, stride, n, w...  17.7 us
    pallas_call x2, Pallas kernels, spd_solve(): pl.pallas_call(_eliminate, out_shape=jax.ShapeDtypeStruct(shape, dtype or...  10 us
    dot_general x1, matrix products, per_device(): lax.dot_general(factor, factor, (((1, 2), (1, 2)), ((), ())), precision=l...  3.3 us
    unnamed x12, local copies, waits for them, and re-layouts  2.77 us
    dot_general x1, local copies, waits for them, and re-layouts, per_device(): lax.dot_general(coefficients, data.reshape(-1, planes, cells), (((1,), (0...  1.68 us

profile of v14, /device:TPU:24, one launch (start us, length us, event | category | flops | bytes accessed | tf_op | source)
XLA Modules:
  0.0 82.5 jit_solution(5414381818277081835)
XLA Ops:
  0.7 0.7 copy-done.3
  1.4 0.8 %copy.18 = f32[64,64]{0,1:T(8,128)S(1)} copy(f32[64,64]{1,0:T(8,128)} %param.5) | data formatting | bytes 32768 | tf_op args[2]
  2.2 0.7 multiply_bitcast_fusion.b_ref
  3.0 0.2 fusion.54
  3.2 0.9 %convolution_multiply_fusion.m_ref = f32[64,64]{1,0:T(8,128)} fusion(f32[64,64]{1,0:T(8,128)S(1)} %fusion.54, f32[16,64]{1,0:T(8,128)S(1)} %copy-done.3), kind=kOutput, calls=%fused_computation.3 | convolution fusion | flops 790528 | bytes 36864 | tf_op jit(solution)/shard_map/dot_general | solution.py:453
  4.1 5.0 %shard_map.50 = bf16[64,64]{1,0:T(8,128)(2,1)} custom-call(f32[64,64]{1,0:T(8,128)} %convolution_multiply_fusion.m_ref, f32[64,64]{1,0:T(8,128)} %multiply_bitcast_fusion.b_ref), custom_call_target="tpu_custom_call" | custom-call | tf_op jit(solution)/shard_map/pallas_call | solution.py:445
  9.1 1.2 %fusion.3 = f32[2,8,4,4,1024]{4,2,3,1,0:T(4,128)S(1)} fusion(bf16[2,8,4,64,1]{3,2,4,1,0:T(4,128)(2,1)} %bitcast.49, bf16[64,4,1024,1,1]{2,1,0,4,3:T(4,128)(2,1)S(1)} %bitcast.43), kind=kOutput, calls=%fused_computation.6 | convolution fusion | flops 33554432 | bytes 1581056 | tf_op jit(solution)/shard_map/dot_general | solution.py:461
  10.3 1.7 %copy.21.x_ref = f32[2,8,4,4,1024]{4,3,2,1,0:T(4,128)} copy(f32[2,8,4,4,1024]{4,2,3,1,0:T(4,128)S(1)} %fusion.3) | data formatting | bytes 2097152 | tf_op jit(solution)/shard_map/dot_general | solution.py:461
  12.0 4.1 %shard_map.51.x_ref = f32[8,4,4,1024]{3,2,1,0:T(4,128)} custom-call(f32[2,8,4,4,1024]{4,3,2,1,0:T(4,128)} %copy.21.x_ref), custom_call_target="tpu_custom_call" | custom-call | tf_op jit(solution)/shard_map/pallas_call | solution.py:110
  16.1 17.7 %shard_map.52 = (f32[4,4,1024]{2,1,0:T(4,128)}, f32[4,3,1024]{2,1,0:T(4,128)}, f32[4,3,1024]{2,1,0:T(4,128)}) custom-call(f32[8,4,4,1024]{3,2,1,0:T(4,128)} %shard_map.51.x_ref), custom_call_target="tpu_custom_call" | custom-call | tf_op jit(solution)/shard_map/pallas_call | solution.py:308
  33.8 1.0 %pad_maximum_fusion = (f32[4,10,1024]{2,1,0:T(8,128)S(1)}, f32[4,10,1024]{2,1,0:T(8,128)S(1)}) fusion(f32[4,3,1024]{2,1,0:T(4,128)} %get-tuple-element.7, f32[4,4,1024]{2,1,0:T(4,128)} %get-tuple-element.6, f32[4,3,1024]{2,1,0:T(4,128)} %get-tuple-element.5), kind=kLoop, calls=%fused_computation.10 | loop fusion | flops 122880 | bytes 491520 | tf_op jit(solution)/shard_map/concatenate | solution.py:329
  35.5 0.8 %fusion.40.x_ref = f32[4,4,1024]{2,1,0:T(4,128)} fusion(f32[4,4,1024]{2,1,0:T(4,128)S(1)} %slice.174, f32[4,8,1024]{2,1,0:T(8,128)S(1)} %get-tuple-element.10, f32[4,10,1024]{2,1,0:T(8,128)S(1)} %get-tuple-element.13, f32[4,6,1024]{2,1,0:T(8,128)S(1)} %get-tuple-element.8, f32[4,6,1024]{2,1,0:T(8,128)S(1)} %get-tuple-element.9, ...), kind=kLoop, calls=%fused_computation.63 | loop fusion | flops 311296 | bytes 466960 | tf_op jit(solution)/shard_map/add | solution.py:404
  36.4 11.1 %shard_map.53.x_ref = f32[8,4,4,1024]{3,2,1,0:T(4,128)} custom-call(f32[4,4,1024]{2,1,0:T(4,128)} %fusion.40.x_ref), custom_call_target="tpu_custom_call" | custom-call | tf_op jit(solution)/shard_map/pallas_call | solution.py:110
  47.5 3.3 %shard_map.54 = f32[2,8,4,4,1024]{4,3,2,1,0:T(4,128)} custom-call(f32[8,4,4,1024]{3,2,1,0:T(4,128)} %shard_map.53.x_ref), custom_call_target="tpu_custom_call" | custom-call | tf_op jit(solution)/shard_map/pallas_call | solution.py:110
  50.8 3.3 %convolution_bitcast_fusion.1 = f32[64,64]{0,1:T(8,128)S(1)} fusion(f32[64,4,1024]{2,1,0:T(4,128)} %bitcast.45), kind=kOutput, calls=%fused_computation.2 | convolution fusion | flops 100663296 | bytes 1064960 | tf_op jit(solution)/shard_map/dot_general | solution.py:475
  54.5 0.2 convert_element_type.69
  54.7 0.7 fusion.1
  55.5 0.7 concatenate.16.x_ref
  56.2 17.5 %shard_map.55 = f32[16,2144]{1,0:T(8,128)} custom-call(f32[2144]{0:T(1024)} %concatenate.16.x_ref), custom_call_target="tpu_custom_call" | custom-call | tf_op jit(solution)/shard_map/pallas_call | solution.py:110
  73.7 0.9 %reduce_sum.29 = f32[2144]{0:T(1024)S(1)} reduce(f32[16,2144]{1,0:T(8,128)} %shard_map.55, f32[]{:T(128)} %constant.56.clone.1), dimensions={0}, to_apply=%region_2.3 | reduce | flops 32160 | bytes 145796 | tf_op jit(solution)/shard_map/reduce_sum | solution.py:358
  75.0 0.7 maximum_multiply_fusion.m_ref
  75.8 0.7 copy.31.b_ref
  76.5 5.0 %shard_map.56 = f32[1,64]{1,0:T(1,128)} custom-call(f32[64,64]{1,0:T(8,128)} %maximum_multiply_fusion.m_ref, f32[64,1]{1,0:T(8,128)} %copy.31.b_ref), custom_call_target="tpu_custom_call" | custom-call | tf_op jit(solution)/shard_map/pallas_call | solution.py:445
  81.5 1.0 %copy.51 = f32[64,4,1024]{2,1,0:T(4,128)} copy(f32[64,4,1024]{2,1,0:T(4,128)S(1)} %bitcast.46) | data formatting | bytes 2097152
  (33 shorter events, 1.8 us)
Async XLA Ops:
  0.6 8.5 %copy-start = (bf16[1,64,4,1024]{3,2,1,0:T(4,128)(2,1)S(1)}, bf16[1,64,4,1024]{3,2,1,0:T(4,128)(2,1)}, u32[]{:S(2)}) copy-start(bf16[1,64,4,1024]{3,2,1,0:T(4,128)(2,1)} %param.3) | copy-start | bytes 1572868
  0.6 0.8 copy-start.3
  2.2 0.8 copy-start.2
  50.7 3.7 %copy-start.1 = (f32[2,8,4,4,1024]{4,3,2,1,0:T(4,128)S(1)}, f32[2,8,4,4,1024]{4,3,2,1,0:T(4,128)}, u32[]{:S(2)}) copy-start(f32[2,8,4,4,1024]{4,3,2,1,0:T(4,128)} %shard_map.54) | copy-start | bytes 3145732

commit v15 on v14

--- a/solution.py
+++ b/solution.py
@@ -197,11 +197,14 @@
 
 
 def _scatter_halo_kernel(size, stride, n, width, x_ref, o_ref, below_ref, above_ref,
-                         got, head_buf, tail_buf, send_sem, recv_sem, own_sem, hsend, hrecv):
+                         got, head_buf, tail_buf, send_sem, recv_sem, own_sem, hsend, hrecv,
+                         pair_got, pair_buf, pair_sem):
     me = lax.axis_index("cuts")
     cm = lax.axis_index("col")
     pos = (me // stride) % size
     base = me - pos * stride
+    core = me % stride
+    partner = me + 1 - 2 * core
     has_left = (cm + n - 1) // n
     has_right = 1 - cm // (n - 1)
     left, right = (me, cm - has_left), (me, cm + has_right)
@@ -223,7 +226,17 @@
     def _():
         pl.semaphore_signal(barrier, inc=1, device_id=right, device_id_type=MESH)
 
-    pl.semaphore_wait(barrier, size - 1 + has_left + has_right)
+    pl.semaphore_signal(barrier, inc=1, device_id=(partner, cm), device_id_type=MESH)
+    pl.semaphore_wait(barrier, size + has_left + has_right)
+
+    pair = pltpu.make_async_remote_copy(
+        src_ref=x_ref.at[1 - core], dst_ref=pair_got, send_sem=pair_sem.at[0],
+        recv_sem=pair_sem.at[1], device_id=(partner, cm), device_id_type=MESH,
+    )
+    pair.start()
+    pair.wait_send()
+    pair.wait_recv()
+    pair_buf[...] = x_ref[core] + pair_got[...]
 
     @pl.when(cm == 0)
     def _():
@@ -233,13 +246,13 @@
     def _():
         above_ref[...] = jnp.zeros_like(above_ref)
 
-    own = pltpu.make_async_copy(x_ref.at[pos], got.at[pos], own_sem)
+    own = pltpu.make_async_copy(pair_buf.at[pos], got.at[pos], own_sem)
     own.start()
     copies = []
     for d in range(1, size):
         peer_pos = (pos + d) % size
         copy = pltpu.make_async_remote_copy(
-            src_ref=x_ref.at[peer_pos], dst_ref=got.at[pos],
+            src_ref=pair_buf.at[peer_pos], dst_ref=got.at[pos],
             send_sem=send_sem.at[peer_pos], recv_sem=recv_sem.at[pos],
             device_id=where(peer_pos), device_id_type=MESH,
         )
@@ -250,7 +263,7 @@
     for d in range(1, size):
         source = (pos + size - d) % size
         pltpu.make_async_remote_copy(
-            src_ref=x_ref.at[source], dst_ref=got.at[source],
+            src_ref=pair_buf.at[source], dst_ref=got.at[source],
             send_sem=send_sem.at[source], recv_sem=recv_sem.at[source],
             device_id=where(source), device_id_type=MESH,
         ).wait_recv()
@@ -302,7 +315,7 @@
 
 def scatter_with_halo(x, size, stride, width):
     n = lax.axis_size("col")
-    block = x.shape[1:]
+    block = x.shape[2:]
     halo = (block[0], width, *block[2:])
     vmem = pl.BlockSpec(memory_space=pltpu.VMEM)
     portion, below, above = pl.pallas_call(
@@ -315,13 +328,16 @@
         in_specs=[vmem],
         out_specs=(vmem, vmem, vmem),
         scratch_shapes=[
-            pltpu.VMEM(x.shape, x.dtype),
+            pltpu.VMEM(x.shape[1:], x.dtype),
             pltpu.VMEM(halo, x.dtype),
             pltpu.VMEM(halo, x.dtype),
             pltpu.SemaphoreType.DMA((size,)),
             pltpu.SemaphoreType.DMA((size,)),
             pltpu.SemaphoreType.DMA,
             pltpu.SemaphoreType.DMA((2,)),
+            pltpu.SemaphoreType.DMA((2,)),
+            pltpu.VMEM(x.shape[1:], x.dtype),
+            pltpu.VMEM(x.shape[1:], x.dtype),
             pltpu.SemaphoreType.DMA((2,)),
         ],
         compiler_params=pltpu.CompilerParams(collective_id=4, has_side_effects=True),
@@ -463,10 +479,9 @@
     )
     cores = 2
     chips = lax.axis_size("cuts") // cores
-    paired = exchange(
-        partial.reshape(cores, chips, -1, planes, cells), "cuts", 0, size=cores, summed=True
-    )
-    portion, extended = scatter_with_halo(paired, chips, cores, ITERS)
+    portion, extended = scatter_with_halo(
+        partial.reshape(cores, chips, -1, planes, cells), chips, cores, ITERS
+    )
     smoothed = smooth_once(portion, extended)
     half_factor = exchange(smoothed, "cuts", 1, whole=True, size=chips, stride=cores)
     factor = exchange(half_factor, "cuts", 5, whole=True, size=cores, space=pl.ANY)

time: 83.2 us -> 82 us (0.986)
  Pallas kernels: 63.6 us -> 62.3 us
    pallas_call x4 -> x3, Pallas kernels: 35.9 us -> 32 us  [exchange(): pl.pallas_call(functools.partial(_exchange_kernel, axis, other, size, str...]
    pallas_call x1, Pallas kernels: 17.7 us -> 20.4 us  [scatter_with_halo(): pl.pallas_call(functools.partial(_scatter_halo_kernel, size, stride, n, w...]
where the time goes in v15:
time: 82 us; the launch traced here: 81.2 us
  Pallas kernels  62.3 us (76%)
  local copies, waits for them, and re-layouts  6.76 us (8%)
  matrix products  6.26 us (8%)
  other arithmetic  5.02 us (6%)
    pallas_call x3, Pallas kernels, exchange(): pl.pallas_call(functools.partial(_exchange_kernel, axis, other, size, str...  32 us
    pallas_call x1, Pallas kernels, scatter_with_halo(): pl.pallas_call(functools.partial(_scatter_halo_kernel, size, stride, n, w...  20.4 us
    pallas_call x2, Pallas kernels, spd_solve(): pl.pallas_call(_eliminate, out_shape=jax.ShapeDtypeStruct(shape, dtype or...  10 us
    dot_general x1, matrix products, per_device(): lax.dot_general(factor, factor, (((1, 2), (1, 2)), ((), ())), precision=l...  3.3 us
    unnamed x12, local copies, waits for them, and re-layouts  2.77 us
    dot_general x1, local copies, waits for them, and re-layouts, per_device(): lax.dot_general(coefficients, data.reshape(-1, planes, cells), (((1,), (0...  1.68 us

profile of v15, /device:TPU:24, one launch (start us, length us, event | category | flops | bytes accessed | tf_op | source)
XLA Modules:
  0.0 81.2 jit_solution(11446046356727052736)
XLA Ops:
  0.7 0.7 copy-done.3
  1.4 0.8 %copy.18 = f32[64,64]{0,1:T(8,128)S(1)} copy(f32[64,64]{1,0:T(8,128)} %param.5) | data formatting | bytes 32768 | tf_op args[2]
  2.2 0.7 multiply_bitcast_fusion.b_ref
  3.0 0.2 fusion.54
  3.2 0.9 %convolution_multiply_fusion.m_ref = f32[64,64]{1,0:T(8,128)} fusion(f32[64,64]{1,0:T(8,128)S(1)} %fusion.54, f32[16,64]{1,0:T(8,128)S(1)} %copy-done.3), kind=kOutput, calls=%fused_computation.3 | convolution fusion | flops 790528 | bytes 36864 | tf_op jit(solution)/shard_map/dot_general | solution.py:469
  4.1 5.0 %shard_map.50 = bf16[64,64]{1,0:T(8,128)(2,1)} custom-call(f32[64,64]{1,0:T(8,128)} %convolution_multiply_fusion.m_ref, f32[64,64]{1,0:T(8,128)} %multiply_bitcast_fusion.b_ref), custom_call_target="tpu_custom_call" | custom-call | tf_op jit(solution)/shard_map/pallas_call | solution.py:461
  9.1 1.2 %fusion.3 = f32[2,8,4,4,1024]{4,2,3,1,0:T(4,128)S(1)} fusion(bf16[2,8,4,64,1]{3,2,4,1,0:T(4,128)(2,1)} %bitcast.49, bf16[64,4,1024,1,1]{2,1,0,4,3:T(4,128)(2,1)S(1)} %bitcast.43), kind=kOutput, calls=%fused_computation.6 | convolution fusion | flops 33554432 | bytes 1581056 | tf_op jit(solution)/shard_map/dot_general | solution.py:477
  10.3 1.7 %copy.21.x_ref = f32[2,8,4,4,1024]{4,3,2,1,0:T(4,128)} copy(f32[2,8,4,4,1024]{4,2,3,1,0:T(4,128)S(1)} %fusion.3) | data formatting | bytes 2097152 | tf_op jit(solution)/shard_map/dot_general | solution.py:477
  12.0 20.4 %shard_map.51 = (f32[4,4,1024]{2,1,0:T(4,128)}, f32[4,3,1024]{2,1,0:T(4,128)}, f32[4,3,1024]{2,1,0:T(4,128)}) custom-call(f32[2,8,4,4,1024]{4,3,2,1,0:T(4,128)} %copy.21.x_ref), custom_call_target="tpu_custom_call" | custom-call | tf_op jit(solution)/shard_map/pallas_call | solution.py:321
  32.4 1.0 %pad_maximum_fusion = (f32[4,10,1024]{2,1,0:T(8,128)S(1)}, f32[4,10,1024]{2,1,0:T(8,128)S(1)}) fusion(f32[4,3,1024]{2,1,0:T(4,128)} %get-tuple-element.7, f32[4,4,1024]{2,1,0:T(4,128)} %get-tuple-element.6, f32[4,3,1024]{2,1,0:T(4,128)} %get-tuple-element.5), kind=kLoop, calls=%fused_computation.10 | loop fusion | flops 122880 | bytes 491520 | tf_op jit(solution)/shard_map/concatenate | solution.py:345
  33.8 0.2 multiply_add_fusion
  34.1 0.8 %fusion.40.x_ref = f32[4,4,1024]{2,1,0:T(4,128)} fusion(f32[4,4,1024]{2,1,0:T(4,128)S(1)} %slice.174, f32[4,8,1024]{2,1,0:T(8,128)S(1)} %get-tuple-element.10, f32[4,10,1024]{2,1,0:T(8,128)S(1)} %get-tuple-element.13, f32[4,6,1024]{2,1,0:T(8,128)S(1)} %get-tuple-element.8, f32[4,6,1024]{2,1,0:T(8,128)S(1)} %get-tuple-element.9, ...), kind=kLoop, calls=%fused_computation.63 | loop fusion | flops 311296 | bytes 466960 | tf_op jit(solution)/shard_map/add | solution.py:420
  35.0 11.4 %shard_map.52.x_ref = f32[8,4,4,1024]{3,2,1,0:T(4,128)} custom-call(f32[4,4,1024]{2,1,0:T(4,128)} %fusion.40.x_ref), custom_call_target="tpu_custom_call" | custom-call | tf_op jit(solution)/shard_map/pallas_call | solution.py:110
  46.4 3.3 %shard_map.53 = f32[2,8,4,4,1024]{4,3,2,1,0:T(4,128)} custom-call(f32[8,4,4,1024]{3,2,1,0:T(4,128)} %shard_map.52.x_ref), custom_call_target="tpu_custom_call" | custom-call | tf_op jit(solution)/shard_map/pallas_call | solution.py:110
  49.7 3.3 %convolution_bitcast_fusion.1 = f32[64,64]{0,1:T(8,128)S(1)} fusion(f32[64,4,1024]{2,1,0:T(4,128)} %bitcast.45), kind=kOutput, calls=%fused_computation.2 | convolution fusion | flops 100663296 | bytes 1064960 | tf_op jit(solution)/shard_map/dot_general | solution.py:490
  53.4 0.2 convert_element_type.69
  53.6 0.7 fusion.1
  54.5 0.7 concatenate.16.x_ref
  55.1 17.3 %shard_map.54 = f32[16,2144]{1,0:T(8,128)} custom-call(f32[2144]{0:T(1024)} %concatenate.16.x_ref), custom_call_target="tpu_custom_call" | custom-call | tf_op jit(solution)/shard_map/pallas_call | solution.py:110
  72.4 0.9 %reduce_sum.29 = f32[2144]{0:T(1024)S(1)} reduce(f32[16,2144]{1,0:T(8,128)} %shard_map.54, f32[]{:T(128)} %constant.56.clone.1), dimensions={0}, to_apply=%region_2.3 | reduce | flops 32160 | bytes 145796 | tf_op jit(solution)/shard_map/reduce_sum | solution.py:374
  73.8 0.7 maximum_multiply_fusion.m_ref
  74.5 0.7 copy.31.b_ref
  75.2 5.0 %shard_map.55 = f32[1,64]{1,0:T(1,128)} custom-call(f32[64,64]{1,0:T(8,128)} %maximum_multiply_fusion.m_ref, f32[64,1]{1,0:T(8,128)} %copy.31.b_ref), custom_call_target="tpu_custom_call" | custom-call | tf_op jit(solution)/shard_map/pallas_call | solution.py:461
  80.2 1.0 %copy.51 = f32[64,4,1024]{2,1,0:T(4,128)} copy(f32[64,4,1024]{2,1,0:T(4,128)S(1)} %bitcast.46) | data formatting | bytes 2097152
  (32 shorter events, 1.6 us)
Async XLA Ops:
  0.6 8.5 %copy-start = (bf16[1,64,4,1024]{3,2,1,0:T(4,128)(2,1)S(1)}, bf16[1,64,4,1024]{3,2,1,0:T(4,128)(2,1)}, u32[]{:S(2)}) copy-start(bf16[1,64,4,1024]{3,2,1,0:T(4,128)(2,1)} %param.3) | copy-start | bytes 1572868
  0.6 0.8 copy-start.3
  2.2 0.8 copy-start.2
  49.7 3.7 %copy-start.1 = (f32[2,8,4,4,1024]{4,3,2,1,0:T(4,128)S(1)}, f32[2,8,4,4,1024]{4,3,2,1,0:T(4,128)}, u32[]{:S(2)}) copy-start(f32[2,8,4,4,1024]{4,3,2,1,0:T(4,128)} %shard_map.53) | copy-start | bytes 3145732

commit v16 on v15

--- a/solution.py
+++ b/solution.py
@@ -345,6 +345,78 @@
     return portion, jnp.concatenate([below, portion, above], axis=1)
 
 
+def _gather_kernel(size, stride, x_ref, o_ref, got, send_sem, recv_sem, own_sem, pair_sem):
+    me = lax.axis_index("cuts")
+    cm = lax.axis_index("col")
+    pos = (me // stride) % size
+    base = me - pos * stride
+    core = me % stride
+    partner = me + 1 - 2 * core
+
+    def where(peer_pos):
+        return (base + peer_pos * stride, cm)
+
+    barrier = pltpu.get_barrier_semaphore()
+    for d in range(1, size):
+        pl.semaphore_signal(
+            barrier, inc=1, device_id=where((pos + d) % size), device_id_type=MESH
+        )
+    pl.semaphore_signal(barrier, inc=1, device_id=(partner, cm), device_id_type=MESH)
+    pl.semaphore_wait(barrier, size)
+    own = pltpu.make_async_copy(x_ref, got.at[pos], own_sem.at[0])
+    own.start()
+    copies = []
+    for d in range(1, size):
+        peer_pos = (pos + d) % size
+        copy = pltpu.make_async_remote_copy(
+            src_ref=x_ref, dst_ref=got.at[pos],
+            send_sem=send_sem.at[peer_pos], recv_sem=recv_sem.at[pos],
+            device_id=where(peer_pos), device_id_type=MESH,
+        )
+        copy.start()
+        copies.append(copy)
+    for copy in copies:
+        copy.wait_send()
+    for d in range(1, size):
+        source = (pos + size - d) % size
+        pltpu.make_async_remote_copy(
+            src_ref=x_ref, dst_ref=got.at[source],
+            send_sem=send_sem.at[source], recv_sem=recv_sem.at[source],
+            device_id=where(source), device_id_type=MESH,
+        ).wait_recv()
+    own.wait()
+    mine = pltpu.make_async_copy(got, o_ref.at[core], own_sem.at[1])
+    mine.start()
+    pair = pltpu.make_async_remote_copy(
+        src_ref=got, dst_ref=o_ref.at[core], send_sem=pair_sem.at[0],
+        recv_sem=pair_sem.at[1], device_id=(partner, cm), device_id_type=MESH,
+    )
+    pair.start()
+    pair.wait_send()
+    pltpu.make_async_remote_copy(
+        src_ref=got, dst_ref=o_ref.at[1 - core], send_sem=pair_sem.at[0],
+        recv_sem=pair_sem.at[1], device_id=(partner, cm), device_id_type=MESH,
+    ).wait_recv()
+    mine.wait()
+
+
+def gather_in_two(x, size, stride):
+    return pl.pallas_call(
+        functools.partial(_gather_kernel, size, stride),
+        out_shape=jax.ShapeDtypeStruct((stride, size, *x.shape), x.dtype),
+        in_specs=[pl.BlockSpec(memory_space=pltpu.VMEM)],
+        out_specs=pl.BlockSpec(memory_space=pl.ANY),
+        scratch_shapes=[
+            pltpu.VMEM((size, *x.shape), x.dtype),
+            pltpu.SemaphoreType.DMA((size,)),
+            pltpu.SemaphoreType.DMA((size,)),
+            pltpu.SemaphoreType.DMA((2,)),
+            pltpu.SemaphoreType.DMA((2,)),
+        ],
+        compiler_params=pltpu.CompilerParams(collective_id=1, has_side_effects=True),
+    )(x)
+
+
 def split_up(shard, dim, devices):
     before, after = (shard.shape[:dim], shard.shape[dim + 1 :])
     return jnp.moveaxis(shard.reshape(*before, devices, -1, *after), dim, 0)
@@ -483,8 +555,7 @@
         partial.reshape(cores, chips, -1, planes, cells), chips, cores, ITERS
     )
     smoothed = smooth_once(portion, extended)
-    half_factor = exchange(smoothed, "cuts", 1, whole=True, size=chips, stride=cores)
-    factor = exchange(half_factor, "cuts", 5, whole=True, size=cores, space=pl.ANY)
+    factor = gather_in_two(smoothed, chips, cores)
     factor = factor.reshape(ranks, planes, cells)
     factor_half = factor.astype(jnp.bfloat16)
     factor_gram = lax.dot_general(

time: 82 us -> 79.9 us (0.974)
  Pallas kernels: 62.3 us -> 60.4 us
    pallas_call x3 -> x1, Pallas kernels: 32 us -> 17.8 us  [exchange(): pl.pallas_call(functools.partial(_exchange_kernel, axis, other, size, str...]
    pallas_call x0 -> x1, Pallas kernels: none -> 12.3 us  [gather_in_two(): pl.pallas_call(functools.partial(_gather_kernel, size, stride), out_shape...]
where the time goes in v16:
time: 79.9 us; the launch traced here: 79.3 us
  Pallas kernels  60.4 us (76%)
  local copies, waits for them, and re-layouts  6.76 us (8%)
  matrix products  6.26 us (8%)
  other arithmetic  5.02 us (6%)
  between operations  0.81 us (1%)
    pallas_call x1, Pallas kernels, scatter_with_halo(): pl.pallas_call(functools.partial(_scatter_halo_kernel, size, stride, n, w...  20.4 us
    pallas_call x1, Pallas kernels, exchange(): pl.pallas_call(functools.partial(_exchange_kernel, axis, other, size, str...  17.8 us
    pallas_call x1, Pallas kernels, gather_in_two(): pl.pallas_call(functools.partial(_gather_kernel, size, stride), out_shape...  12.3 us
    pallas_call x2, Pallas kernels, spd_solve(): pl.pallas_call(_eliminate, out_shape=jax.ShapeDtypeStruct(shape, dtype or...  10 us
    dot_general x1, matrix products, per_device(): lax.dot_general(factor, factor, (((1, 2), (1, 2)), ((), ())), precision=l...  3.3 us
    unnamed x12, local copies, waits for them, and re-layouts  2.77 us
    dot_general x1, local copies, waits for them, and re-layouts, per_device(): lax.dot_general(coefficients, data.reshape(-1, planes, cells), (((1,), (0...  1.68 us

profile of v16, /device:TPU:24, one launch (start us, length us, event | category | flops | bytes accessed | tf_op | source)
XLA Modules:
  0.0 79.3 jit_solution(16754933133880831217)
XLA Ops:
  0.7 0.7 copy-done.3
  1.4 0.8 %copy.18 = f32[64,64]{0,1:T(8,128)S(1)} copy(f32[64,64]{1,0:T(8,128)} %param.5) | data formatting | bytes 32768 | tf_op args[2]
  2.2 0.7 multiply_bitcast_fusion.b_ref
  3.0 0.2 fusion.54
  3.2 0.9 %convolution_multiply_fusion.m_ref = f32[64,64]{1,0:T(8,128)} fusion(f32[64,64]{1,0:T(8,128)S(1)} %fusion.54, f32[16,64]{1,0:T(8,128)S(1)} %copy-done.3), kind=kOutput, calls=%fused_computation.3 | convolution fusion | flops 790528 | bytes 36864 | tf_op jit(solution)/shard_map/dot_general | solution.py:541
  4.1 5.0 %shard_map.50 = bf16[64,64]{1,0:T(8,128)(2,1)} custom-call(f32[64,64]{1,0:T(8,128)} %convolution_multiply_fusion.m_ref, f32[64,64]{1,0:T(8,128)} %multiply_bitcast_fusion.b_ref), custom_call_target="tpu_custom_call" | custom-call | tf_op jit(solution)/shard_map/pallas_call | solution.py:533
  9.1 1.2 %fusion.3 = f32[2,8,4,4,1024]{4,2,3,1,0:T(4,128)S(1)} fusion(bf16[2,8,4,64,1]{3,2,4,1,0:T(4,128)(2,1)} %bitcast.49, bf16[64,4,1024,1,1]{2,1,0,4,3:T(4,128)(2,1)S(1)} %bitcast.43), kind=kOutput, calls=%fused_computation.6 | convolution fusion | flops 33554432 | bytes 1581056 | tf_op jit(solution)/shard_map/dot_general | solution.py:549
  10.3 1.7 %copy.21.x_ref = f32[2,8,4,4,1024]{4,3,2,1,0:T(4,128)} copy(f32[2,8,4,4,1024]{4,2,3,1,0:T(4,128)S(1)} %fusion.3) | data formatting | bytes 2097152 | tf_op jit(solution)/shard_map/dot_general | solution.py:549
  12.0 20.4 %shard_map.51 = (f32[4,4,1024]{2,1,0:T(4,128)}, f32[4,3,1024]{2,1,0:T(4,128)}, f32[4,3,1024]{2,1,0:T(4,128)}) custom-call(f32[2,8,4,4,1024]{4,3,2,1,0:T(4,128)} %copy.21.x_ref), custom_call_target="tpu_custom_call" | custom-call | tf_op jit(solution)/shard_map/pallas_call | solution.py:321
  32.4 1.0 %pad_maximum_fusion = (f32[4,10,1024]{2,1,0:T(8,128)S(1)}, f32[4,10,1024]{2,1,0:T(8,128)S(1)}) fusion(f32[4,3,1024]{2,1,0:T(4,128)} %get-tuple-element.7, f32[4,4,1024]{2,1,0:T(4,128)} %get-tuple-element.6, f32[4,3,1024]{2,1,0:T(4,128)} %get-tuple-element.5), kind=kLoop, calls=%fused_computation.10 | loop fusion | flops 122880 | bytes 491520 | tf_op jit(solution)/shard_map/concatenate | solution.py:345
  33.5 0.2 multiply_add_fusion.1
  33.8 0.2 multiply_add_fusion
  34.1 0.8 %fusion.40.x_ref = f32[4,4,1024]{2,1,0:T(4,128)} fusion(f32[4,4,1024]{2,1,0:T(4,128)S(1)} %slice.174, f32[4,8,1024]{2,1,0:T(8,128)S(1)} %get-tuple-element.10, f32[4,10,1024]{2,1,0:T(8,128)S(1)} %get-tuple-element.13, f32[4,6,1024]{2,1,0:T(8,128)S(1)} %get-tuple-element.8, f32[4,6,1024]{2,1,0:T(8,128)S(1)} %get-tuple-element.9, ...), kind=kLoop, calls=%fused_computation.63 | loop fusion | flops 311296 | bytes 466960 | tf_op jit(solution)/shard_map/add | solution.py:492
  35.0 12.3 %shard_map.52 = f32[2,8,4,4,1024]{4,3,2,1,0:T(4,128)} custom-call(f32[4,4,1024]{2,1,0:T(4,128)} %fusion.40.x_ref), custom_call_target="tpu_custom_call" | custom-call | tf_op jit(solution)/shard_map/pallas_call | solution.py:404
  47.3 3.3 %convolution_bitcast_fusion.1 = f32[64,64]{0,1:T(8,128)S(1)} fusion(f32[64,4,1024]{2,1,0:T(4,128)} %bitcast.45), kind=kOutput, calls=%fused_computation.2 | convolution fusion | flops 100663296 | bytes 1064960 | tf_op jit(solution)/shard_map/dot_general | solution.py:561
  51.0 0.2 convert_element_type.69
  51.3 0.7 fusion.1
  52.1 0.7 concatenate.16.x_ref
  52.8 17.8 %shard_map.53 = f32[16,2144]{1,0:T(8,128)} custom-call(f32[2144]{0:T(1024)} %concatenate.16.x_ref), custom_call_target="tpu_custom_call" | custom-call | tf_op jit(solution)/shard_map/pallas_call | solution.py:110
  70.5 0.9 %reduce_sum.29 = f32[2144]{0:T(1024)S(1)} reduce(f32[16,2144]{1,0:T(8,128)} %shard_map.53, f32[]{:T(128)} %constant.56.clone.1), dimensions={0}, to_apply=%region_2.3 | reduce | flops 32160 | bytes 145796 | tf_op jit(solution)/shard_map/reduce_sum | solution.py:446
  71.8 0.7 maximum_multiply_fusion.m_ref
  72.6 0.7 copy.31.b_ref
  73.3 5.0 %shard_map.54 = f32[1,64]{1,0:T(1,128)} custom-call(f32[64,64]{1,0:T(8,128)} %maximum_multiply_fusion.m_ref, f32[64,1]{1,0:T(8,128)} %copy.31.b_ref), custom_call_target="tpu_custom_call" | custom-call | tf_op jit(solution)/shard_map/pallas_call | solution.py:533
  78.3 1.0 %copy.51 = f32[64,4,1024]{2,1,0:T(4,128)} copy(f32[64,4,1024]{2,1,0:T(4,128)S(1)} %bitcast.46) | data formatting | bytes 2097152
  (31 shorter events, 1.4 us)
Async XLA Ops:
  0.6 8.5 %copy-start = (bf16[1,64,4,1024]{3,2,1,0:T(4,128)(2,1)S(1)}, bf16[1,64,4,1024]{3,2,1,0:T(4,128)(2,1)}, u32[]{:S(2)}) copy-start(bf16[1,64,4,1024]{3,2,1,0:T(4,128)(2,1)} %param.3) | copy-start | bytes 1572868
  0.6 0.8 copy-start.3
  2.2 0.8 copy-start.2
  47.3 3.7 %copy-start.1 = (f32[2,8,4,4,1024]{4,3,2,1,0:T(4,128)S(1)}, f32[2,8,4,4,1024]{4,3,2,1,0:T(4,128)}, u32[]{:S(2)}) copy-start(f32[2,8,4,4,1024]{4,3,2,1,0:T(4,128)} %shard_map.52) | copy-start | bytes 3145732

commit v17 on v16

--- a/solution.py
+++ b/solution.py
@@ -492,9 +492,7 @@
     return solution + direction
 
 
-def _eliminate(m_ref, b_ref, o_ref):
-    m = m_ref[...]
-    b = b_ref[...]
+def _gauss_jordan(m, b):
     n = m.shape[0]
     ri = lax.broadcasted_iota(jnp.int32, m.shape, 0)
     ci = lax.broadcasted_iota(jnp.int32, m.shape, 1)
@@ -521,18 +519,35 @@
         b = jnp.where(rb == p, t0, jnp.where(rb == q, t1, b - c0 * t0 - c1 * t1))
         return m, b
 
-    x = lax.fori_loop(0, n // 2, step, (m, b), unroll=True)[1]
-    if o_ref.shape == b.shape:
-        o_ref[...] = x.astype(o_ref.dtype)
-    else:
-        o_ref[...] = jnp.sum(jnp.where(ri == ci, x, 0.0), axis=0, keepdims=True)
+    return lax.fori_loop(0, n // 2, step, (m, b), unroll=True)[1]
+
+
+def _eliminate(m_ref, b_ref, o_ref):
+    o_ref[...] = _gauss_jordan(m_ref[...], b_ref[...]).astype(o_ref.dtype)
+
+
+def _final_solve(g_ref, t_ref, o_ref):
+    g = g_ref[...]
+    n = g.shape[0]
+    t = t_ref[...]
+    ri = lax.broadcasted_iota(jnp.int32, g.shape, 0)
+    ci = lax.broadcasted_iota(jnp.int32, g.shape, 1)
+    m = g * t[:n]
+    b = jnp.sum(jnp.where(ri == ci, t[n : n + 1], 0.0), axis=1, keepdims=True)
+    x = _gauss_jordan(m, b)
+    o_ref[...] = jnp.sum(jnp.where(ri == ci, x, 0.0), axis=0, keepdims=True)
 
 
 def spd_solve(m, b, dtype=None):
-    shape = (1, b.shape[0]) if b.shape[1] == 1 else b.shape
     return pl.pallas_call(
-        _eliminate, out_shape=jax.ShapeDtypeStruct(shape, dtype or b.dtype)
+        _eliminate, out_shape=jax.ShapeDtypeStruct(b.shape, dtype or b.dtype)
     )(m, b)
+
+
+def final_solve(mix_gram, total):
+    return pl.pallas_call(
+        _final_solve, out_shape=jax.ShapeDtypeStruct((1, mix_gram.shape[0]), jnp.float32)
+    )(mix_gram, total)
 
 
 def per_device(data, weights, mixing):
@@ -565,20 +580,9 @@
         data, factor_half, (((2, 3), (1, 2)), ((), ())), preferred_element_type=jnp.float32
     )
     targets = jnp.sum(mixing[None, :, :] * products, axis=1)
-    half = ranks // 2
-    row = lax.broadcasted_iota(jnp.int32, (half, half), 0)
-    col = lax.broadcasted_iota(jnp.int32, (half, half), 1)
-    top, off, low = (factor_gram[:half, :half], factor_gram[:half, half:], factor_gram[half:, half:])
-    folded = jnp.where(row >= col, top, low)
-    folded, off, low_diag, targets = packed_total(
-        (folded, off, jnp.sum(jnp.where(row == col, low, 0.0), axis=1), targets), "col"
-    )
-    top = jnp.where(row >= col, folded, folded.T)
-    low = jnp.where(row < col, folded, jnp.where(row > col, folded.T, low_diag[:, None]))
-    factor_gram = jnp.concatenate(
-        [jnp.concatenate([top, off], axis=1), jnp.concatenate([off.T, low], axis=1)], axis=0
-    )
-    updated = spd_solve(mix_gram * factor_gram, targets.T)
+    payload = jnp.concatenate([factor_gram, targets], axis=0)
+    total = exchange(payload, "col", 2, whole=True, summed=True)
+    updated = final_solve(mix_gram, total)
     return (factor, updated)
 
 

time: 79.9 us -> 85 us (1.064)
  the two profiles are of different devices: /device:TPU:24 before, /device:TPU:30 now
where the time goes in v17:
time: 85 us; the launch traced here: 84.4 us
  Pallas kernels  68.7 us (81%)
  local copies, waits for them, and re-layouts  5.13 us (6%)
  other arithmetic  5.01 us (6%)
  matrix products  4.66 us (5%)
    pallas_call x1, Pallas kernels, exchange(): pl.pallas_call(functools.partial(_exchange_kernel, axis, other, size, str...  23.2 us
    pallas_call x1, Pallas kernels, scatter_with_halo(): pl.pallas_call(functools.partial(_scatter_halo_kernel, size, stride, n, w...  22.2 us
    pallas_call x1, Pallas kernels, gather_in_two(): pl.pallas_call(functools.partial(_gather_kernel, size, stride), out_shape...  13.4 us
    pallas_call x1, Pallas kernels, spd_solve(): pl.pallas_call(_eliminate, out_shape=jax.ShapeDtypeStruct(b.shape, dtype...  5.01 us
    pallas_call x1, Pallas kernels, final_solve(): pl.pallas_call(_final_solve, out_shape=jax.ShapeDtypeStruct((1, mix_gram....  4.92 us
    unnamed x12, local copies, waits for them, and re-layouts  3.19 us
    dot_general x1, matrix products, per_device(): lax.dot_general(factor, factor, (((1, 2), (1, 2)), ((), ())), precision=l...  1.71 us

profile of v17, /device:TPU:30, one launch (start us, length us, event | category | flops | bytes accessed | tf_op | source)
XLA Modules:
  0.0 84.4 jit_solution(17205007142677340825)
XLA Ops:
  0.7 0.7 copy-done.4
  1.4 0.8 copy.5
  2.2 0.7 multiply_bitcast_fusion.b_ref
  2.9 0.1 copy-done.2
  3.0 0.2 fusion.50.g_ref
  3.3 0.9 %convolution_multiply_fusion.m_ref = f32[64,64]{1,0:T(8,128)} fusion(f32[64,64]{1,0:T(8,128)S(1)} %fusion.50.g_ref, f32[16,64]{1,0:T(8,128)S(1)} %copy-done.4), kind=kOutput, calls=%fused_computation.3 | convolution fusion | flops 790528 | bytes 36864 | tf_op jit(solution)/shard_map/dot_general | solution.py:556
  4.1 5.0 %shard_map.50 = bf16[64,64]{1,0:T(8,128)(2,1)} custom-call(f32[64,64]{1,0:T(8,128)} %convolution_multiply_fusion.m_ref, f32[64,64]{1,0:T(8,128)} %multiply_bitcast_fusion.b_ref), custom_call_target="tpu_custom_call" | custom-call | tf_op jit(solution)/shard_map/pallas_call | solution.py:542
  9.1 1.2 %fusion.3 = f32[2,8,4,4,1024]{4,2,3,1,0:T(4,128)S(1)} fusion(bf16[2,8,4,64,1]{3,2,4,1,0:T(4,128)(2,1)} %bitcast.41, bf16[64,4,1024,1,1]{2,1,0,4,3:T(4,128)(2,1)S(1)} %bitcast.36), kind=kOutput, calls=%fused_computation.6 | convolution fusion | flops 33554432 | bytes 1581056 | tf_op jit(solution)/shard_map/dot_general | solution.py:564
  10.3 1.7 %copy.8.x_ref = f32[2,8,4,4,1024]{4,3,2,1,0:T(4,128)} copy(f32[2,8,4,4,1024]{4,2,3,1,0:T(4,128)S(1)} %fusion.3) | data formatting | bytes 2097152 | tf_op jit(solution)/shard_map/dot_general | solution.py:564
  12.0 22.2 %shard_map.51 = (f32[4,4,1024]{2,1,0:T(4,128)}, f32[4,3,1024]{2,1,0:T(4,128)}, f32[4,3,1024]{2,1,0:T(4,128)}) custom-call(f32[2,8,4,4,1024]{4,3,2,1,0:T(4,128)} %copy.8.x_ref), custom_call_target="tpu_custom_call" | custom-call | tf_op jit(solution)/shard_map/pallas_call | solution.py:321
  34.3 1.0 %pad_maximum_fusion = (f32[4,10,1024]{2,1,0:T(8,128)S(1)}, f32[4,10,1024]{2,1,0:T(8,128)S(1)}) fusion(f32[4,3,1024]{2,1,0:T(4,128)} %get-tuple-element.7, f32[4,4,1024]{2,1,0:T(4,128)} %get-tuple-element.6, f32[4,3,1024]{2,1,0:T(4,128)} %get-tuple-element.5), kind=kLoop, calls=%fused_computation.10 | loop fusion | flops 122880 | bytes 491520 | tf_op jit(solution)/shard_map/concatenate | solution.py:345
  35.4 0.2 multiply_add_fusion.1
  35.7 0.2 multiply_add_fusion
  35.9 0.1 slice_bitcast_fusion
  36.0 0.8 %fusion.40.x_ref = f32[4,4,1024]{2,1,0:T(4,128)} fusion(f32[4,4,1024]{2,1,0:T(4,128)S(1)} %slice.130, f32[4,8,1024]{2,1,0:T(8,128)S(1)} %get-tuple-element.10, f32[4,10,1024]{2,1,0:T(8,128)S(1)} %get-tuple-element.13, f32[4,6,1024]{2,1,0:T(8,128)S(1)} %get-tuple-element.8, f32[4,6,1024]{2,1,0:T(8,128)S(1)} %get-tuple-element.9, f32[4]{0:T(128)S(1)} %slice_bitcast_fusion, ...), kind=kLoop, calls=%fused_computation.63 | loop fusion | flops 311296 | bytes 466960 | tf_op jit(solution)/shard_map/add | solution.py:492
  36.9 13.4 %shard_map.52 = f32[2,8,4,4,1024]{4,3,2,1,0:T(4,128)} custom-call(f32[4,4,1024]{2,1,0:T(4,128)} %fusion.40.x_ref), custom_call_target="tpu_custom_call" | custom-call | tf_op jit(solution)/shard_map/pallas_call | solution.py:404
  50.3 1.4 %convert_element_type.69 = bf16[2,8,4,4,1024]{4,3,2,1,0:T(4,128)(2,1)S(1)} convert(f32[2,8,4,4,1024]{4,3,2,1,0:T(4,128)} %shard_map.52) | non-fusion elementwise | flops 262144 | bytes 1572864 | tf_op jit(solution)/shard_map/convert_element_type | solution.py:575
  51.7 0.7 fusion.1
  52.4 0.5 copy-done.1
  53.0 1.7 %convolution_bitcast_fusion.1 = f32[64,64]{1,0:T(8,128)S(1)} fusion(f32[64,4,1024]{2,1,0:T(4,128)S(1)} %bitcast.38), kind=kOutput, calls=%fused_computation.2 | convolution fusion | flops 100663296 | bytes 1064960 | tf_op jit(solution)/shard_map/dot_general | solution.py:576
  54.7 0.6 pad_maximum_fusion.1.x_ref
  55.3 23.2 %shard_map.53.t_ref = f32[65,64]{1,0:T(8,128)} custom-call(f32[65,64]{1,0:T(8,128)} %pad_maximum_fusion.1.x_ref), custom_call_target="tpu_custom_call" | custom-call | tf_op jit(solution)/shard_map/pallas_call | solution.py:110
  78.5 4.9 %shard_map.54 = f32[1,64]{1,0:T(1,128)} custom-call(f32[64,64]{1,0:T(8,128)} %copy-done.3, f32[65,64]{1,0:T(8,128)} %shard_map.53.t_ref), custom_call_target="tpu_custom_call" | custom-call | tf_op jit(solution)/shard_map/pallas_call | solution.py:548
  83.4 1.0 %copy.33 = f32[64,4,1024]{2,1,0:T(4,128)} copy(f32[64,4,1024]{2,1,0:T(4,128)S(1)} %bitcast.39) | data formatting | bytes 2097152
  (15 shorter events, 0.2 us)
Async XLA Ops:
  0.6 8.5 %copy-start = (bf16[1,64,4,1024]{3,2,1,0:T(4,128)(2,1)S(1)}, bf16[1,64,4,1024]{3,2,1,0:T(4,128)(2,1)}, u32[]{:S(2)}) copy-start(bf16[1,64,4,1024]{3,2,1,0:T(4,128)(2,1)} %param.3) | copy-start | bytes 1572868
  0.6 0.8 copy-start.4
  2.2 0.8 copy-start.2
  3.2 0.9 %copy-start.3 = (f32[64,64]{1,0:T(8,128)}, f32[64,64]{1,0:T(8,128)S(1)}, u32[]{:S(2)}) copy-start(f32[64,64]{1,0:T(8,128)S(1)} %fusion.50.g_ref) | copy-start | bytes 49156
  51.7 1.2 %copy-start.1 = (f32[2,8,4,4,1024]{4,3,2,1,0:T(4,128)S(1)}, f32[2,8,4,4,1024]{4,3,2,1,0:T(4,128)}, u32[]{:S(2)}) copy-start(f32[2,8,4,4,1024]{4,3,2,1,0:T(4,128)} %shard_map.52) | copy-start | bytes 3145732

commit v18 on v16

--- a/solution.py
+++ b/solution.py
@@ -448,7 +448,10 @@
 
 def packed_total(arrays, axis):
     line, at, done = (jnp.concatenate([a.reshape(-1) for a in arrays]), 0, [])
-    running = taken_together(line, axis)
+    lanes = 128
+    rows = -(-line.size // lanes)
+    block = jnp.pad(line, (0, rows * lanes - line.size)).reshape(rows, lanes)
+    running = taken_together(block, axis).reshape(-1)
     for a in arrays:
         done.append(running[at : at + a.size].reshape(a.shape))
         at += a.size

time: 79.9 us -> 80 us (level)
  no operation moved by 1% of the time
where the time goes in v18:
time: 80 us; the launch traced here: 79.3 us
  Pallas kernels  60.5 us (76%)
  local copies, waits for them, and re-layouts  6.78 us (8%)
  matrix products  6.26 us (8%)
  other arithmetic  5.04 us (6%)
  between operations  0.81 us (1%)
    pallas_call x1, Pallas kernels, scatter_with_halo(): pl.pallas_call(functools.partial(_scatter_halo_kernel, size, stride, n, w...  20.4 us
    pallas_call x1, Pallas kernels, exchange(): pl.pallas_call(functools.partial(_exchange_kernel, axis, other, size, str...  17.8 us
    pallas_call x1, Pallas kernels, gather_in_two(): pl.pallas_call(functools.partial(_gather_kernel, size, stride), out_shape...  12.3 us
    pallas_call x2, Pallas kernels, spd_solve(): pl.pallas_call(_eliminate, out_shape=jax.ShapeDtypeStruct(shape, dtype or...  10 us
    dot_general x1, matrix products, per_device(): lax.dot_general(factor, factor, (((1, 2), (1, 2)), ((), ())), precision=l...  3.3 us
    unnamed x12, local copies, waits for them, and re-layouts  2.77 us
    dot_general x1, local copies, waits for them, and re-layouts, per_device(): lax.dot_general(coefficients, data.reshape(-1, planes, cells), (((1,), (0...  1.68 us

profile of v18, /device:TPU:24, one launch (start us, length us, event | category | flops | bytes accessed | tf_op | source)
XLA Modules:
  0.0 79.3 jit_solution(6707461863990160414)
XLA Ops:
  0.7 0.7 copy-done.3
  1.4 0.8 %copy.18 = f32[64,64]{0,1:T(8,128)S(1)} copy(f32[64,64]{1,0:T(8,128)} %param.5) | data formatting | bytes 32768 | tf_op args[2]
  2.2 0.7 multiply_bitcast_fusion.b_ref
  3.0 0.2 fusion.54
  3.2 0.9 %convolution_multiply_fusion.m_ref = f32[64,64]{1,0:T(8,128)} fusion(f32[64,64]{1,0:T(8,128)S(1)} %fusion.54, f32[16,64]{1,0:T(8,128)S(1)} %copy-done.3), kind=kOutput, calls=%fused_computation.3 | convolution fusion | flops 790528 | bytes 36864 | tf_op jit(solution)/shard_map/dot_general | solution.py:544
  4.1 5.0 %shard_map.50 = bf16[64,64]{1,0:T(8,128)(2,1)} custom-call(f32[64,64]{1,0:T(8,128)} %convolution_multiply_fusion.m_ref, f32[64,64]{1,0:T(8,128)} %multiply_bitcast_fusion.b_ref), custom_call_target="tpu_custom_call" | custom-call | tf_op jit(solution)/shard_map/pallas_call | solution.py:536
  9.1 1.2 %fusion.3 = f32[2,8,4,4,1024]{4,2,3,1,0:T(4,128)S(1)} fusion(bf16[2,8,4,64,1]{3,2,4,1,0:T(4,128)(2,1)} %bitcast.52, bf16[64,4,1024,1,1]{2,1,0,4,3:T(4,128)(2,1)S(1)} %bitcast.46), kind=kOutput, calls=%fused_computation.6 | convolution fusion | flops 33554432 | bytes 1581056 | tf_op jit(solution)/shard_map/dot_general | solution.py:552
  10.3 1.7 %copy.21.x_ref = f32[2,8,4,4,1024]{4,3,2,1,0:T(4,128)} copy(f32[2,8,4,4,1024]{4,2,3,1,0:T(4,128)S(1)} %fusion.3) | data formatting | bytes 2097152 | tf_op jit(solution)/shard_map/dot_general | solution.py:552
  12.0 20.4 %shard_map.51 = (f32[4,4,1024]{2,1,0:T(4,128)}, f32[4,3,1024]{2,1,0:T(4,128)}, f32[4,3,1024]{2,1,0:T(4,128)}) custom-call(f32[2,8,4,4,1024]{4,3,2,1,0:T(4,128)} %copy.21.x_ref), custom_call_target="tpu_custom_call" | custom-call | tf_op jit(solution)/shard_map/pallas_call | solution.py:321
  32.4 1.0 %pad_maximum_fusion = (f32[4,10,1024]{2,1,0:T(8,128)S(1)}, f32[4,10,1024]{2,1,0:T(8,128)S(1)}) fusion(f32[4,3,1024]{2,1,0:T(4,128)} %get-tuple-element.7, f32[4,4,1024]{2,1,0:T(4,128)} %get-tuple-element.6, f32[4,3,1024]{2,1,0:T(4,128)} %get-tuple-element.5), kind=kLoop, calls=%fused_computation.10 | loop fusion | flops 122880 | bytes 491520 | tf_op jit(solution)/shard_map/concatenate | solution.py:345
  33.5 0.2 multiply_add_fusion.1
  33.8 0.2 multiply_add_fusion
  34.1 0.8 %fusion.40.x_ref = f32[4,4,1024]{2,1,0:T(4,128)} fusion(f32[4,4,1024]{2,1,0:T(4,128)S(1)} %slice.160, f32[4,8,1024]{2,1,0:T(8,128)S(1)} %get-tuple-element.10, f32[4,10,1024]{2,1,0:T(8,128)S(1)} %get-tuple-element.13, f32[4,6,1024]{2,1,0:T(8,128)S(1)} %get-tuple-element.8, f32[4,6,1024]{2,1,0:T(8,128)S(1)} %get-tuple-element.9, ...), kind=kLoop, calls=%fused_computation.63 | loop fusion | flops 311296 | bytes 466960 | tf_op jit(solution)/shard_map/add | solution.py:495
  35.0 12.3 %shard_map.52 = f32[2,8,4,4,1024]{4,3,2,1,0:T(4,128)} custom-call(f32[4,4,1024]{2,1,0:T(4,128)} %fusion.40.x_ref), custom_call_target="tpu_custom_call" | custom-call | tf_op jit(solution)/shard_map/pallas_call | solution.py:404
  47.3 3.3 %convolution_bitcast_fusion.1 = f32[64,64]{0,1:T(8,128)S(1)} fusion(f32[64,4,1024]{2,1,0:T(4,128)} %bitcast.48), kind=kOutput, calls=%fused_computation.2 | convolution fusion | flops 100663296 | bytes 1064960 | tf_op jit(solution)/shard_map/dot_general | solution.py:564
  51.0 0.2 convert_element_type.71
  51.3 0.7 fusion.1
  52.1 0.6 pad_bitcast_fusion.x_ref
  52.8 17.8 %shard_map.53 = f32[16,17,128]{2,1,0:T(8,128)} custom-call(f32[17,128]{1,0:T(8,128)} %pad_bitcast_fusion.x_ref), custom_call_target="tpu_custom_call" | custom-call | tf_op jit(solution)/shard_map/pallas_call | solution.py:110
  70.6 1.0 %reduce_sum.29 = f32[17,128]{1,0:T(8,128)S(1)} reduce(f32[16,17,128]{2,1,0:T(8,128)} %shard_map.53, f32[]{:T(128)} %constant.56.clone.1), dimensions={0}, to_apply=%region_2.3 | reduce | flops 32640 | bytes 147972 | tf_op jit(solution)/shard_map/reduce_sum | solution.py:446
  71.9 0.7 maximum_multiply_fusion.m_ref
  72.7 0.7 copy.31.b_ref
  73.4 5.0 %shard_map.54 = f32[1,64]{1,0:T(1,128)} custom-call(f32[64,64]{1,0:T(8,128)} %maximum_multiply_fusion.m_ref, f32[64,1]{1,0:T(8,128)} %copy.31.b_ref), custom_call_target="tpu_custom_call" | custom-call | tf_op jit(solution)/shard_map/pallas_call | solution.py:536
  78.4 1.0 %copy.51 = f32[64,4,1024]{2,1,0:T(4,128)} copy(f32[64,4,1024]{2,1,0:T(4,128)S(1)} %bitcast.49) | data formatting | bytes 2097152
  (32 shorter events, 1.4 us)
Async XLA Ops:
  0.6 8.5 %copy-start = (bf16[1,64,4,1024]{3,2,1,0:T(4,128)(2,1)S(1)}, bf16[1,64,4,1024]{3,2,1,0:T(4,128)(2,1)}, u32[]{:S(2)}) copy-start(bf16[1,64,4,1024]{3,2,1,0:T(4,128)(2,1)} %param.3) | copy-start | bytes 1572868
  0.6 0.8 copy-start.3
  2.2 0.8 copy-start.2
  47.3 3.7 %copy-start.1 = (f32[2,8,4,4,1024]{4,3,2,1,0:T(4,128)S(1)}, f32[2,8,4,4,1024]{4,3,2,1,0:T(4,128)}, u32[]{:S(2)}) copy-start(f32[2,8,4,4,1024]{4,3,2,1,0:T(4,128)} %shard_map.52) | copy-start | bytes 3145732

commit v19 on v18

--- a/solution.py
+++ b/solution.py
@@ -417,6 +417,88 @@
     )(x)
 
 
+def _split_sum_kernel(n, rows, x_ref, o_ref, other_ref, got, half_buf, send_sem, recv_sem,
+                      own_sem, pair_sem):
+    me = lax.axis_index("col")
+    cuts = lax.axis_index("cuts")
+    partner = cuts + 1 - 2 * (cuts % 2)
+
+    def where(peer):
+        return (cuts, peer)
+
+    barrier = pltpu.get_barrier_semaphore()
+    for d in range(1, n):
+        pl.semaphore_signal(barrier, inc=1, device_id=where((me + d) % n), device_id_type=MESH)
+    pl.semaphore_signal(barrier, inc=1, device_id=(partner, me), device_id_type=MESH)
+    pl.semaphore_wait(barrier, n)
+    own = pltpu.make_async_copy(x_ref, got.at[me], own_sem)
+    own.start()
+    copies = []
+    for d in range(1, n):
+        peer = (me + d) % n
+        copy = pltpu.make_async_remote_copy(
+            src_ref=x_ref, dst_ref=got.at[me], send_sem=send_sem.at[peer],
+            recv_sem=recv_sem.at[me], device_id=where(peer), device_id_type=MESH,
+        )
+        copy.start()
+        copies.append(copy)
+    for copy in copies:
+        copy.wait_send()
+    for d in range(1, n):
+        source = (me + n - d) % n
+        pltpu.make_async_remote_copy(
+            src_ref=x_ref, dst_ref=got.at[source], send_sem=send_sem.at[source],
+            recv_sem=recv_sem.at[source], device_id=where(source), device_id_type=MESH,
+        ).wait_recv()
+    own.wait()
+    total = got[0]
+    for slot in range(1, n):
+        total = total + got[slot]
+    o_ref[...] = total
+    half_buf[...] = total[:rows]
+    pair = pltpu.make_async_remote_copy(
+        src_ref=half_buf, dst_ref=other_ref, send_sem=pair_sem.at[0],
+        recv_sem=pair_sem.at[1], device_id=(partner, me), device_id_type=MESH,
+    )
+    pair.start()
+    pair.wait_send()
+    pair.wait_recv()
+
+
+def split_total(line, targets):
+    n = lax.axis_size("col")
+    lanes = 128
+    rows = -(-line.size // (2 * lanes))
+    core = lax.axis_index("cuts") % 2
+    halves = jnp.pad(line, (0, 2 * rows * lanes - line.size)).reshape(2, rows, lanes)
+    tail = jnp.pad(targets.reshape(-1), (0, lanes - targets.size)).reshape(1, lanes)
+    block = jnp.concatenate([lax.dynamic_index_in_dim(halves, core, 0, False), tail], axis=0)
+    vmem = pl.BlockSpec(memory_space=pltpu.VMEM)
+    total, other = pl.pallas_call(
+        functools.partial(_split_sum_kernel, n, rows),
+        out_shape=(
+            jax.ShapeDtypeStruct(block.shape, block.dtype),
+            jax.ShapeDtypeStruct((rows, lanes), block.dtype),
+        ),
+        in_specs=[vmem],
+        out_specs=(vmem, vmem),
+        scratch_shapes=[
+            pltpu.VMEM((n, *block.shape), block.dtype),
+            pltpu.VMEM((rows, lanes), block.dtype),
+            pltpu.SemaphoreType.DMA((n,)),
+            pltpu.SemaphoreType.DMA((n,)),
+            pltpu.SemaphoreType.DMA,
+            pltpu.SemaphoreType.DMA((2,)),
+        ],
+        compiler_params=pltpu.CompilerParams(collective_id=2, has_side_effects=True),
+    )(block)
+    mine = total[:rows]
+    first = jnp.where(core == 0, mine, other)
+    second = jnp.where(core == 0, other, mine)
+    whole = jnp.concatenate([first, second], axis=0).reshape(-1)[: line.size]
+    return whole, total[rows, : targets.size].reshape(targets.shape)
+
+
 def split_up(shard, dim, devices):
     before, after = (shard.shape[:dim], shard.shape[dim + 1 :])
     return jnp.moveaxis(shard.reshape(*before, devices, -1, *after), dim, 0)
@@ -573,9 +655,13 @@
     col = lax.broadcasted_iota(jnp.int32, (half, half), 1)
     top, off, low = (factor_gram[:half, :half], factor_gram[:half, half:], factor_gram[half:, half:])
     folded = jnp.where(row >= col, top, low)
-    folded, off, low_diag, targets = packed_total(
-        (folded, off, jnp.sum(jnp.where(row == col, low, 0.0), axis=1), targets), "col"
-    )
+    low_diag = jnp.sum(jnp.where(row == col, low, 0.0), axis=1)
+    line, targets = split_total(
+        jnp.concatenate([folded.reshape(-1), off.reshape(-1), low_diag]), targets
+    )
+    folded = line[: half * half].reshape(half, half)
+    off = line[half * half : 2 * half * half].reshape(half, half)
+    low_diag = line[2 * half * half :]
     top = jnp.where(row >= col, folded, folded.T)
     low = jnp.where(row < col, folded, jnp.where(row > col, folded.T, low_diag[:, None]))
     factor_gram = jnp.concatenate(

time: 80 us -> 81.6 us (1.020)
  the two profiles are of different devices: /device:TPU:24 before, /device:TPU:1 now
where the time goes in v19:
time: 81.6 us; the launch traced here: 80.9 us
  Pallas kernels  61.7 us (76%)
  local copies, waits for them, and re-layouts  6.72 us (8%)
  matrix products  6.26 us (8%)
  other arithmetic  5.44 us (7%)
  between operations  0.86 us (1%)
    pallas_call x1, Pallas kernels, scatter_with_halo(): pl.pallas_call(functools.partial(_scatter_halo_kernel, size, stride, n, w...  19.9 us
    pallas_call x1, Pallas kernels, split_total(): pl.pallas_call(functools.partial(_split_sum_kernel, n, rows), out_shape=(...  17.2 us
    pallas_call x1, Pallas kernels, gather_in_two(): pl.pallas_call(functools.partial(_gather_kernel, size, stride), out_shape...  14.5 us
    pallas_call x2, Pallas kernels, spd_solve(): pl.pallas_call(_eliminate, out_shape=jax.ShapeDtypeStruct(shape, dtype or...  10 us
    dot_general x1, matrix products, per_device(): lax.dot_general(factor, factor, (((1, 2), (1, 2)), ((), ())), precision=l...  3.3 us
    unnamed x12, local copies, waits for them, and re-layouts  2.77 us
    dot_general x1, local copies, waits for them, and re-layouts, per_device(): lax.dot_general(coefficients, data.reshape(-1, planes, cells), (((1,), (0...  1.68 us

profile of v19, /device:TPU:1, one launch (start us, length us, event | category | flops | bytes accessed | tf_op | source)
XLA Modules:
  0.0 80.9 jit_solution(7802218147166519735)
XLA Ops:
  0.7 0.7 copy-done.3
  1.4 0.8 %copy.18 = f32[64,64]{0,1:T(8,128)S(1)} copy(f32[64,64]{1,0:T(8,128)} %param.5) | data formatting | bytes 32768 | tf_op args[2]
  2.2 0.7 multiply_bitcast_fusion.b_ref
  3.0 0.2 fusion.55
  3.2 0.9 %convolution_multiply_fusion.m_ref = f32[64,64]{1,0:T(8,128)} fusion(f32[64,64]{1,0:T(8,128)S(1)} %fusion.55, f32[16,64]{1,0:T(8,128)S(1)} %copy-done.3), kind=kOutput, calls=%fused_computation.3 | convolution fusion | flops 790528 | bytes 36864 | tf_op jit(solution)/shard_map/dot_general | solution.py:626
  4.1 5.0 %shard_map.50 = bf16[64,64]{1,0:T(8,128)(2,1)} custom-call(f32[64,64]{1,0:T(8,128)} %convolution_multiply_fusion.m_ref, f32[64,64]{1,0:T(8,128)} %multiply_bitcast_fusion.b_ref), custom_call_target="tpu_custom_call" | custom-call | tf_op jit(solution)/shard_map/pallas_call | solution.py:618
  9.1 1.2 %fusion.3 = f32[2,8,4,4,1024]{4,2,3,1,0:T(4,128)S(1)} fusion(bf16[2,8,4,64,1]{3,2,4,1,0:T(4,128)(2,1)} %bitcast.55, bf16[64,4,1024,1,1]{2,1,0,4,3:T(4,128)(2,1)S(1)} %bitcast.49), kind=kOutput, calls=%fused_computation.6 | convolution fusion | flops 33554432 | bytes 1581056 | tf_op jit(solution)/shard_map/dot_general | solution.py:634
  10.3 1.7 %copy.21.x_ref = f32[2,8,4,4,1024]{4,3,2,1,0:T(4,128)} copy(f32[2,8,4,4,1024]{4,2,3,1,0:T(4,128)S(1)} %fusion.3) | data formatting | bytes 2097152 | tf_op jit(solution)/shard_map/dot_general | solution.py:634
  12.0 19.9 %shard_map.51 = (f32[4,4,1024]{2,1,0:T(4,128)}, f32[4,3,1024]{2,1,0:T(4,128)}, f32[4,3,1024]{2,1,0:T(4,128)}) custom-call(f32[2,8,4,4,1024]{4,3,2,1,0:T(4,128)} %copy.21.x_ref), custom_call_target="tpu_custom_call" | custom-call | tf_op jit(solution)/shard_map/pallas_call | solution.py:321
  31.9 1.0 %pad_maximum_fusion = (f32[4,10,1024]{2,1,0:T(8,128)S(1)}, f32[4,10,1024]{2,1,0:T(8,128)S(1)}) fusion(f32[4,3,1024]{2,1,0:T(4,128)} %get-tuple-element.9, f32[4,4,1024]{2,1,0:T(4,128)} %get-tuple-element.8, f32[4,3,1024]{2,1,0:T(4,128)} %get-tuple-element.7), kind=kLoop, calls=%fused_computation.10 | loop fusion | flops 122880 | bytes 491520 | tf_op jit(solution)/shard_map/concatenate | solution.py:345
  33.4 0.2 multiply_add_fusion
  33.7 0.8 %fusion.40.x_ref = f32[4,4,1024]{2,1,0:T(4,128)} fusion(f32[4,4,1024]{2,1,0:T(4,128)S(1)} %slice.177, f32[4,8,1024]{2,1,0:T(8,128)S(1)} %get-tuple-element.14, f32[4,10,1024]{2,1,0:T(8,128)S(1)} %get-tuple-element.17, f32[4,6,1024]{2,1,0:T(8,128)S(1)} %get-tuple-element.12, f32[4,6,1024]{2,1,0:T(8,128)S(1)} %get-tuple-element.13, ...), kind=kLoop, calls=%fused_computation.63 | loop fusion | flops 311296 | bytes 466960 | tf_op jit(solution)/shard_map/add | solution.py:577
  34.6 14.5 %shard_map.52 = f32[2,8,4,4,1024]{4,3,2,1,0:T(4,128)} custom-call(f32[4,4,1024]{2,1,0:T(4,128)} %fusion.40.x_ref), custom_call_target="tpu_custom_call" | custom-call | tf_op jit(solution)/shard_map/pallas_call | solution.py:404
  49.1 3.3 %convolution_bitcast_fusion.1 = f32[64,64]{0,1:T(8,128)S(1)} fusion(f32[64,4,1024]{2,1,0:T(4,128)} %bitcast.51), kind=kOutput, calls=%fused_computation.2 | convolution fusion | flops 100663296 | bytes 1064960 | tf_op jit(solution)/shard_map/dot_general | solution.py:646
  53.0 0.2 convert_element_type.73
  53.3 0.7 fusion.1
  53.9 0.6 pad_maximum_fusion.2.x_ref
  54.6 17.2 %shard_map.53 = (f32[10,128]{1,0:T(8,128)}, f32[9,128]{1,0:T(8,128)}) custom-call(f32[10,128]{1,0:T(8,128)} %pad_maximum_fusion.2.x_ref), custom_call_target="tpu_custom_call" | custom-call | tf_op jit(solution)/shard_map/pallas_call | solution.py:477
  71.8 0.7 slice_select_fusion
  72.9 0.7 maximum_multiply_fusion.m_ref
  73.6 0.7 slice_bitcast_fusion
  74.3 0.7 copy.31.b_ref
  75.0 5.0 %shard_map.54 = f32[1,64]{1,0:T(1,128)} custom-call(f32[64,64]{1,0:T(8,128)} %maximum_multiply_fusion.m_ref, f32[64,1]{1,0:T(8,128)} %copy.31.b_ref), custom_call_target="tpu_custom_call" | custom-call | tf_op jit(solution)/shard_map/pallas_call | solution.py:618
  80.0 1.0 %copy.51 = f32[64,4,1024]{2,1,0:T(4,128)} copy(f32[64,4,1024]{2,1,0:T(4,128)S(1)} %bitcast.52) | data formatting | bytes 2097152
  (36 shorter events, 1.6 us)
Async XLA Ops:
  0.6 8.5 %copy-start = (bf16[1,64,4,1024]{3,2,1,0:T(4,128)(2,1)S(1)}, bf16[1,64,4,1024]{3,2,1,0:T(4,128)(2,1)}, u32[]{:S(2)}) copy-start(bf16[1,64,4,1024]{3,2,1,0:T(4,128)(2,1)} %param.3) | copy-start | bytes 1572868
  0.6 0.8 copy-start.3
  2.2 0.8 copy-start.2
  49.1 3.9 %copy-start.1 = (f32[2,8,4,4,1024]{4,3,2,1,0:T(4,128)S(1)}, f32[2,8,4,4,1024]{4,3,2,1,0:T(4,128)}, u32[]{:S(2)}) copy-start(f32[2,8,4,4,1024]{4,3,2,1,0:T(4,128)} %shard_map.52) | copy-start | bytes 3145732

commit v20 on v18

--- a/solution.py
+++ b/solution.py
@@ -54,17 +54,21 @@
     def part(peer_pos):
         return x_ref if whole else x_ref.at[peer_pos]
 
+    if axis == "col" and size == 16:
+        hops = lambda z, x: 2 * min(z, 4 - z) + min(x, 4 - x)
+        order = sorted(((z, x) for z in range(4) for x in range(4) if z or x),
+                       key=lambda o: -hops(*o))
+        peers = [((pos // 4 + z) % 4) * 4 + (pos % 4 + x) % 4 for z, x in order]
+    else:
+        peers = [(pos + d) % size for d in range(1, size)]
     barrier = pltpu.get_barrier_semaphore()
-    for d in range(1, size):
-        pl.semaphore_signal(
-            barrier, inc=1, device_id=where((pos + d) % size), device_id_type=MESH
-        )
+    for peer_pos in peers:
+        pl.semaphore_signal(barrier, inc=1, device_id=where(peer_pos), device_id_type=MESH)
     pl.semaphore_wait(barrier, size - 1)
     own = pltpu.make_async_copy(part(pos), got.at[pos], own_sem)
     own.start()
     copies = []
-    for d in range(1, size):
-        peer_pos = (pos + d) % size
+    for peer_pos in peers:
         copy = pltpu.make_async_remote_copy(
             src_ref=part(peer_pos),
             dst_ref=got.at[pos],

time: 80 us -> 80.8 us (1.010)
  no operation moved by 1% of the time
where the time goes in v20:
time: 80.8 us; the launch traced here: 79.7 us
  Pallas kernels  60.8 us (75%)
  local copies, waits for them, and re-layouts  6.78 us (8%)
  matrix products  6.26 us (8%)
  other arithmetic  5.04 us (6%)
  between operations  0.81 us (1%)
    pallas_call x1, Pallas kernels, scatter_with_halo(): pl.pallas_call(functools.partial(_scatter_halo_kernel, size, stride, n, w...  20.4 us
    pallas_call x1, Pallas kernels, exchange(): pl.pallas_call(functools.partial(_exchange_kernel, axis, other, size, str...  18.1 us
    pallas_call x1, Pallas kernels, gather_in_two(): pl.pallas_call(functools.partial(_gather_kernel, size, stride), out_shape...  12.3 us
    pallas_call x2, Pallas kernels, spd_solve(): pl.pallas_call(_eliminate, out_shape=jax.ShapeDtypeStruct(shape, dtype or...  10 us
    dot_general x1, matrix products, per_device(): lax.dot_general(factor, factor, (((1, 2), (1, 2)), ((), ())), precision=l...  3.3 us
    unnamed x12, local copies, waits for them, and re-layouts  2.77 us
    dot_general x1, local copies, waits for them, and re-layouts, per_device(): lax.dot_general(coefficients, data.reshape(-1, planes, cells), (((1,), (0...  1.68 us

profile of v20, /device:TPU:24, one launch (start us, length us, event | category | flops | bytes accessed | tf_op | source)
XLA Modules:
  0.0 79.7 jit_solution(4292510736853744353)
XLA Ops:
  0.7 0.7 copy-done.3
  1.4 0.8 %copy.18 = f32[64,64]{0,1:T(8,128)S(1)} copy(f32[64,64]{1,0:T(8,128)} %param.5) | data formatting | bytes 32768 | tf_op args[2]
  2.2 0.7 multiply_bitcast_fusion.b_ref
  3.0 0.2 fusion.54
  3.2 0.9 %convolution_multiply_fusion.m_ref = f32[64,64]{1,0:T(8,128)} fusion(f32[64,64]{1,0:T(8,128)S(1)} %fusion.54, f32[16,64]{1,0:T(8,128)S(1)} %copy-done.3), kind=kOutput, calls=%fused_computation.3 | convolution fusion | flops 790528 | bytes 36864 | tf_op jit(solution)/shard_map/dot_general | solution.py:548
  4.1 5.0 %shard_map.50 = bf16[64,64]{1,0:T(8,128)(2,1)} custom-call(f32[64,64]{1,0:T(8,128)} %convolution_multiply_fusion.m_ref, f32[64,64]{1,0:T(8,128)} %multiply_bitcast_fusion.b_ref), custom_call_target="tpu_custom_call" | custom-call | tf_op jit(solution)/shard_map/pallas_call | solution.py:540
  9.1 1.2 %fusion.3 = f32[2,8,4,4,1024]{4,2,3,1,0:T(4,128)S(1)} fusion(bf16[2,8,4,64,1]{3,2,4,1,0:T(4,128)(2,1)} %bitcast.52, bf16[64,4,1024,1,1]{2,1,0,4,3:T(4,128)(2,1)S(1)} %bitcast.46), kind=kOutput, calls=%fused_computation.6 | convolution fusion | flops 33554432 | bytes 1581056 | tf_op jit(solution)/shard_map/dot_general | solution.py:556
  10.3 1.7 %copy.21.x_ref = f32[2,8,4,4,1024]{4,3,2,1,0:T(4,128)} copy(f32[2,8,4,4,1024]{4,2,3,1,0:T(4,128)S(1)} %fusion.3) | data formatting | bytes 2097152 | tf_op jit(solution)/shard_map/dot_general | solution.py:556
  12.0 20.4 %shard_map.51 = (f32[4,4,1024]{2,1,0:T(4,128)}, f32[4,3,1024]{2,1,0:T(4,128)}, f32[4,3,1024]{2,1,0:T(4,128)}) custom-call(f32[2,8,4,4,1024]{4,3,2,1,0:T(4,128)} %copy.21.x_ref), custom_call_target="tpu_custom_call" | custom-call | tf_op jit(solution)/shard_map/pallas_call | solution.py:325
  32.4 1.0 %pad_maximum_fusion = (f32[4,10,1024]{2,1,0:T(8,128)S(1)}, f32[4,10,1024]{2,1,0:T(8,128)S(1)}) fusion(f32[4,3,1024]{2,1,0:T(4,128)} %get-tuple-element.7, f32[4,4,1024]{2,1,0:T(4,128)} %get-tuple-element.6, f32[4,3,1024]{2,1,0:T(4,128)} %get-tuple-element.5), kind=kLoop, calls=%fused_computation.10 | loop fusion | flops 122880 | bytes 491520 | tf_op jit(solution)/shard_map/concatenate | solution.py:349
  33.5 0.2 multiply_add_fusion.1
  33.8 0.2 multiply_add_fusion
  34.1 0.8 %fusion.40.x_ref = f32[4,4,1024]{2,1,0:T(4,128)} fusion(f32[4,4,1024]{2,1,0:T(4,128)S(1)} %slice.160, f32[4,8,1024]{2,1,0:T(8,128)S(1)} %get-tuple-element.10, f32[4,10,1024]{2,1,0:T(8,128)S(1)} %get-tuple-element.13, f32[4,6,1024]{2,1,0:T(8,128)S(1)} %get-tuple-element.8, f32[4,6,1024]{2,1,0:T(8,128)S(1)} %get-tuple-element.9, ...), kind=kLoop, calls=%fused_computation.63 | loop fusion | flops 311296 | bytes 466960 | tf_op jit(solution)/shard_map/add | solution.py:499
  35.0 12.3 %shard_map.52 = f32[2,8,4,4,1024]{4,3,2,1,0:T(4,128)} custom-call(f32[4,4,1024]{2,1,0:T(4,128)} %fusion.40.x_ref), custom_call_target="tpu_custom_call" | custom-call | tf_op jit(solution)/shard_map/pallas_call | solution.py:408
  47.3 3.3 %convolution_bitcast_fusion.1 = f32[64,64]{0,1:T(8,128)S(1)} fusion(f32[64,4,1024]{2,1,0:T(4,128)} %bitcast.48), kind=kOutput, calls=%fused_computation.2 | convolution fusion | flops 100663296 | bytes 1064960 | tf_op jit(solution)/shard_map/dot_general | solution.py:568
  51.0 0.2 convert_element_type.71
  51.3 0.7 fusion.1
  52.1 0.6 pad_bitcast_fusion.x_ref
  52.8 18.1 %shard_map.53 = f32[16,17,128]{2,1,0:T(8,128)} custom-call(f32[17,128]{1,0:T(8,128)} %pad_bitcast_fusion.x_ref), custom_call_target="tpu_custom_call" | custom-call | tf_op jit(solution)/shard_map/pallas_call | solution.py:114
  70.9 1.0 %reduce_sum.29 = f32[17,128]{1,0:T(8,128)S(1)} reduce(f32[16,17,128]{2,1,0:T(8,128)} %shard_map.53, f32[]{:T(128)} %constant.56.clone.1), dimensions={0}, to_apply=%region_2.3 | reduce | flops 32640 | bytes 147972 | tf_op jit(solution)/shard_map/reduce_sum | solution.py:450
  72.2 0.7 maximum_multiply_fusion.m_ref
  73.0 0.7 copy.31.b_ref
  73.7 5.0 %shard_map.54 = f32[1,64]{1,0:T(1,128)} custom-call(f32[64,64]{1,0:T(8,128)} %maximum_multiply_fusion.m_ref, f32[64,1]{1,0:T(8,128)} %copy.31.b_ref), custom_call_target="tpu_custom_call" | custom-call | tf_op jit(solution)/shard_map/pallas_call | solution.py:540
  78.7 1.0 %copy.51 = f32[64,4,1024]{2,1,0:T(4,128)} copy(f32[64,4,1024]{2,1,0:T(4,128)S(1)} %bitcast.49) | data formatting | bytes 2097152
  (32 shorter events, 1.4 us)
Async XLA Ops:
  0.6 8.5 %copy-start = (bf16[1,64,4,1024]{3,2,1,0:T(4,128)(2,1)S(1)}, bf16[1,64,4,1024]{3,2,1,0:T(4,128)(2,1)}, u32[]{:S(2)}) copy-start(bf16[1,64,4,1024]{3,2,1,0:T(4,128)(2,1)} %param.3) | copy-start | bytes 1572868
  0.6 0.8 copy-start.3
  2.2 0.8 copy-start.2
  47.3 3.7 %copy-start.1 = (f32[2,8,4,4,1024]{4,3,2,1,0:T(4,128)S(1)}, f32[2,8,4,4,1024]{4,3,2,1,0:T(4,128)}, u32[]{:S(2)}) copy-start(f32[2,8,4,4,1024]{4,3,2,1,0:T(4,128)} %shard_map.52) | copy-start | bytes 3145732

commit v21 on v18

--- a/solution.py
+++ b/solution.py
@@ -540,8 +540,8 @@
 
 def per_device(data, weights, mixing):
     local_scans, ranks, planes, cells = data.shape
-    mix_gram = jnp.dot(mixing.T, mixing, precision=highest)
-    weight_gram = jnp.dot(weights.T, weights, precision=highest)
+    mix_gram = jnp.dot(mixing.T, mixing, precision=lax.Precision.HIGH)
+    weight_gram = jnp.dot(weights.T, weights, precision=lax.Precision.HIGH)
     own_weights = lax.dynamic_slice_in_dim(
         weights, lax.axis_index("cuts") * local_scans, local_scans, 0
     )

time: 80 us -> 79.9 us (level)
  no operation moved by 1% of the time
where the time goes in v21:
time: 79.9 us; the launch traced here: 79.3 us
  Pallas kernels  60.5 us (76%)
  local copies, waits for them, and re-layouts  6.78 us (8%)
  matrix products  6.22 us (8%)
  other arithmetic  5.04 us (6%)
  between operations  0.81 us (1%)
    pallas_call x1, Pallas kernels, scatter_with_halo(): pl.pallas_call(functools.partial(_scatter_halo_kernel, size, stride, n, w...  20.4 us
    pallas_call x1, Pallas kernels, exchange(): pl.pallas_call(functools.partial(_exchange_kernel, axis, other, size, str...  17.8 us
    pallas_call x1, Pallas kernels, gather_in_two(): pl.pallas_call(functools.partial(_gather_kernel, size, stride), out_shape...  12.3 us
    pallas_call x2, Pallas kernels, spd_solve(): pl.pallas_call(_eliminate, out_shape=jax.ShapeDtypeStruct(shape, dtype or...  10 us
    dot_general x1, matrix products, per_device(): lax.dot_general(factor, factor, (((1, 2), (1, 2)), ((), ())), precision=l...  3.3 us
    unnamed x12, local copies, waits for them, and re-layouts  2.77 us
    dot_general x1, local copies, waits for them, and re-layouts, per_device(): lax.dot_general(coefficients, data.reshape(-1, planes, cells), (((1,), (0...  1.68 us

profile of v21, /device:TPU:24, one launch (start us, length us, event | category | flops | bytes accessed | tf_op | source)
XLA Modules:
  0.0 79.3 jit_solution(16184766989784560195)
XLA Ops:
  0.7 0.7 copy-done.3
  1.4 0.8 %copy.18 = f32[64,64]{0,1:T(8,128)S(1)} copy(f32[64,64]{1,0:T(8,128)} %param.5) | data formatting | bytes 32768 | tf_op args[2]
  2.2 0.7 multiply_bitcast_fusion.b_ref
  3.0 0.2 fusion.54
  3.2 0.8 %convolution_multiply_fusion.m_ref = f32[64,64]{1,0:T(8,128)} fusion(f32[64,64]{1,0:T(8,128)S(1)} %fusion.54, f32[16,64]{1,0:T(8,128)S(1)} %copy-done.3), kind=kOutput, calls=%fused_computation.3 | convolution fusion | flops 397312 | bytes 36864 | tf_op jit(solution)/shard_map/dot_general | solution.py:544
  4.1 5.0 %shard_map.50 = bf16[64,64]{1,0:T(8,128)(2,1)} custom-call(f32[64,64]{1,0:T(8,128)} %convolution_multiply_fusion.m_ref, f32[64,64]{1,0:T(8,128)} %multiply_bitcast_fusion.b_ref), custom_call_target="tpu_custom_call" | custom-call | tf_op jit(solution)/shard_map/pallas_call | solution.py:536
  9.1 1.2 %fusion.3 = f32[2,8,4,4,1024]{4,2,3,1,0:T(4,128)S(1)} fusion(bf16[2,8,4,64,1]{3,2,4,1,0:T(4,128)(2,1)} %bitcast.52, bf16[64,4,1024,1,1]{2,1,0,4,3:T(4,128)(2,1)S(1)} %bitcast.46), kind=kOutput, calls=%fused_computation.6 | convolution fusion | flops 33554432 | bytes 1581056 | tf_op jit(solution)/shard_map/dot_general | solution.py:552
  10.3 1.7 %copy.21.x_ref = f32[2,8,4,4,1024]{4,3,2,1,0:T(4,128)} copy(f32[2,8,4,4,1024]{4,2,3,1,0:T(4,128)S(1)} %fusion.3) | data formatting | bytes 2097152 | tf_op jit(solution)/shard_map/dot_general | solution.py:552
  12.0 20.4 %shard_map.51 = (f32[4,4,1024]{2,1,0:T(4,128)}, f32[4,3,1024]{2,1,0:T(4,128)}, f32[4,3,1024]{2,1,0:T(4,128)}) custom-call(f32[2,8,4,4,1024]{4,3,2,1,0:T(4,128)} %copy.21.x_ref), custom_call_target="tpu_custom_call" | custom-call | tf_op jit(solution)/shard_map/pallas_call | solution.py:321
  32.3 1.0 %pad_maximum_fusion = (f32[4,10,1024]{2,1,0:T(8,128)S(1)}, f32[4,10,1024]{2,1,0:T(8,128)S(1)}) fusion(f32[4,3,1024]{2,1,0:T(4,128)} %get-tuple-element.7, f32[4,4,1024]{2,1,0:T(4,128)} %get-tuple-element.6, f32[4,3,1024]{2,1,0:T(4,128)} %get-tuple-element.5), kind=kLoop, calls=%fused_computation.10 | loop fusion | flops 122880 | bytes 491520 | tf_op jit(solution)/shard_map/concatenate | solution.py:345
  33.5 0.2 multiply_add_fusion.1
  33.8 0.2 multiply_add_fusion
  34.1 0.8 %fusion.40.x_ref = f32[4,4,1024]{2,1,0:T(4,128)} fusion(f32[4,4,1024]{2,1,0:T(4,128)S(1)} %slice.160, f32[4,8,1024]{2,1,0:T(8,128)S(1)} %get-tuple-element.10, f32[4,10,1024]{2,1,0:T(8,128)S(1)} %get-tuple-element.13, f32[4,6,1024]{2,1,0:T(8,128)S(1)} %get-tuple-element.8, f32[4,6,1024]{2,1,0:T(8,128)S(1)} %get-tuple-element.9, ...), kind=kLoop, calls=%fused_computation.63 | loop fusion | flops 311296 | bytes 466960 | tf_op jit(solution)/shard_map/add | solution.py:495
  34.9 12.3 %shard_map.52 = f32[2,8,4,4,1024]{4,3,2,1,0:T(4,128)} custom-call(f32[4,4,1024]{2,1,0:T(4,128)} %fusion.40.x_ref), custom_call_target="tpu_custom_call" | custom-call | tf_op jit(solution)/shard_map/pallas_call | solution.py:404
  47.3 3.3 %convolution_bitcast_fusion.1 = f32[64,64]{0,1:T(8,128)S(1)} fusion(f32[64,4,1024]{2,1,0:T(4,128)} %bitcast.48), kind=kOutput, calls=%fused_computation.2 | convolution fusion | flops 100663296 | bytes 1064960 | tf_op jit(solution)/shard_map/dot_general | solution.py:564
  51.0 0.2 convert_element_type.71
  51.2 0.7 fusion.1
  52.1 0.6 pad_bitcast_fusion.x_ref
  52.7 17.8 %shard_map.53 = f32[16,17,128]{2,1,0:T(8,128)} custom-call(f32[17,128]{1,0:T(8,128)} %pad_bitcast_fusion.x_ref), custom_call_target="tpu_custom_call" | custom-call | tf_op jit(solution)/shard_map/pallas_call | solution.py:110
  70.5 1.0 %reduce_sum.29 = f32[17,128]{1,0:T(8,128)S(1)} reduce(f32[16,17,128]{2,1,0:T(8,128)} %shard_map.53, f32[]{:T(128)} %constant.56.clone.1), dimensions={0}, to_apply=%region_2.3 | reduce | flops 32640 | bytes 147972 | tf_op jit(solution)/shard_map/reduce_sum | solution.py:446
  71.8 0.7 maximum_multiply_fusion.m_ref
  72.6 0.7 copy.31.b_ref
  73.3 5.0 %shard_map.54 = f32[1,64]{1,0:T(1,128)} custom-call(f32[64,64]{1,0:T(8,128)} %maximum_multiply_fusion.m_ref, f32[64,1]{1,0:T(8,128)} %copy.31.b_ref), custom_call_target="tpu_custom_call" | custom-call | tf_op jit(solution)/shard_map/pallas_call | solution.py:536
  78.3 1.0 %copy.51 = f32[64,4,1024]{2,1,0:T(4,128)} copy(f32[64,4,1024]{2,1,0:T(4,128)S(1)} %bitcast.49) | data formatting | bytes 2097152
  (32 shorter events, 1.4 us)
Async XLA Ops:
  0.6 8.4 %copy-start = (bf16[1,64,4,1024]{3,2,1,0:T(4,128)(2,1)S(1)}, bf16[1,64,4,1024]{3,2,1,0:T(4,128)(2,1)}, u32[]{:S(2)}) copy-start(bf16[1,64,4,1024]{3,2,1,0:T(4,128)(2,1)} %param.3) | copy-start | bytes 1572868
  0.6 0.8 copy-start.3
  2.2 0.8 copy-start.2
  47.2 3.7 %copy-start.1 = (f32[2,8,4,4,1024]{4,3,2,1,0:T(4,128)S(1)}, f32[2,8,4,4,1024]{4,3,2,1,0:T(4,128)}, u32[]{:S(2)}) copy-start(f32[2,8,4,4,1024]{4,3,2,1,0:T(4,128)} %shard_map.52) | copy-start | bytes 3145732

commit v22 on v18

--- a/solution.py
+++ b/solution.py
@@ -501,6 +501,8 @@
     n = m.shape[0]
     ri = lax.broadcasted_iota(jnp.int32, m.shape, 0)
     ci = lax.broadcasted_iota(jnp.int32, m.shape, 1)
+    if b.shape[0] == 1:
+        b = jnp.sum(jnp.where(ri == ci, b, 0.0), axis=1, keepdims=True)
     rb = lax.broadcasted_iota(jnp.int32, b.shape, 0)
 
     def pick_row(x, rows, p):
@@ -532,7 +534,7 @@
 
 
 def spd_solve(m, b, dtype=None):
-    shape = (1, b.shape[0]) if b.shape[1] == 1 else b.shape
+    shape = b.shape if b.shape[0] == 1 else b.shape
     return pl.pallas_call(
         _eliminate, out_shape=jax.ShapeDtypeStruct(shape, dtype or b.dtype)
     )(m, b)
@@ -581,7 +583,7 @@
     factor_gram = jnp.concatenate(
         [jnp.concatenate([top, off], axis=1), jnp.concatenate([off.T, low], axis=1)], axis=0
     )
-    updated = spd_solve(mix_gram * factor_gram, targets.T)
+    updated = spd_solve(mix_gram * factor_gram, targets)
     return (factor, updated)
 
 

time: 80 us -> 79.7 us (level)
  no operation moved by 1% of the time
where the time goes in v22:
time: 79.7 us; the launch traced here: 79 us
  Pallas kernels  60.3 us (76%)
  local copies, waits for them, and re-layouts  6.59 us (8%)
  matrix products  6.26 us (8%)
  other arithmetic  5.04 us (6%)
  between operations  0.81 us (1%)
    pallas_call x1, Pallas kernels, scatter_with_halo(): pl.pallas_call(functools.partial(_scatter_halo_kernel, size, stride, n, w...  20.4 us
    pallas_call x1, Pallas kernels, exchange(): pl.pallas_call(functools.partial(_exchange_kernel, axis, other, size, str...  17.8 us
    pallas_call x1, Pallas kernels, gather_in_two(): pl.pallas_call(functools.partial(_gather_kernel, size, stride), out_shape...  12.3 us
    pallas_call x2, Pallas kernels, spd_solve(): pl.pallas_call(_eliminate, out_shape=jax.ShapeDtypeStruct(shape, dtype or...  9.9 us
    dot_general x1, matrix products, per_device(): lax.dot_general(factor, factor, (((1, 2), (1, 2)), ((), ())), precision=l...  3.3 us
    unnamed x12, local copies, waits for them, and re-layouts  2.77 us
    dot_general x1, local copies, waits for them, and re-layouts, per_device(): lax.dot_general(coefficients, data.reshape(-1, planes, cells), (((1,), (0...  1.68 us

profile of v22, /device:TPU:24, one launch (start us, length us, event | category | flops | bytes accessed | tf_op | source)
XLA Modules:
  0.0 79.0 jit_solution(3634155350889773411)
XLA Ops:
  0.7 0.7 copy-done.3
  1.4 0.8 %copy.17 = f32[64,64]{0,1:T(8,128)S(1)} copy(f32[64,64]{1,0:T(8,128)} %param.5) | data formatting | bytes 32768 | tf_op args[2]
  2.2 0.7 multiply_bitcast_fusion.b_ref
  3.0 0.2 fusion.54
  3.2 0.9 %convolution_multiply_fusion.m_ref = f32[64,64]{1,0:T(8,128)} fusion(f32[64,64]{1,0:T(8,128)S(1)} %fusion.54, f32[16,64]{1,0:T(8,128)S(1)} %copy-done.3), kind=kOutput, calls=%fused_computation.3 | convolution fusion | flops 790528 | bytes 36864 | tf_op jit(solution)/shard_map/dot_general | solution.py:546
  4.1 5.0 %shard_map.50 = bf16[64,64]{1,0:T(8,128)(2,1)} custom-call(f32[64,64]{1,0:T(8,128)} %convolution_multiply_fusion.m_ref, f32[64,64]{1,0:T(8,128)} %multiply_bitcast_fusion.b_ref), custom_call_target="tpu_custom_call" | custom-call | tf_op jit(solution)/shard_map/pallas_call | solution.py:538
  9.1 1.2 %fusion.3 = f32[2,8,4,4,1024]{4,2,3,1,0:T(4,128)S(1)} fusion(bf16[2,8,4,64,1]{3,2,4,1,0:T(4,128)(2,1)} %bitcast.52, bf16[64,4,1024,1,1]{2,1,0,4,3:T(4,128)(2,1)S(1)} %bitcast.46), kind=kOutput, calls=%fused_computation.6 | convolution fusion | flops 33554432 | bytes 1581056 | tf_op jit(solution)/shard_map/dot_general | solution.py:554
  10.3 1.7 %copy.20.x_ref = f32[2,8,4,4,1024]{4,3,2,1,0:T(4,128)} copy(f32[2,8,4,4,1024]{4,2,3,1,0:T(4,128)S(1)} %fusion.3) | data formatting | bytes 2097152 | tf_op jit(solution)/shard_map/dot_general | solution.py:554
  12.0 20.4 %shard_map.51 = (f32[4,4,1024]{2,1,0:T(4,128)}, f32[4,3,1024]{2,1,0:T(4,128)}, f32[4,3,1024]{2,1,0:T(4,128)}) custom-call(f32[2,8,4,4,1024]{4,3,2,1,0:T(4,128)} %copy.20.x_ref), custom_call_target="tpu_custom_call" | custom-call | tf_op jit(solution)/shard_map/pallas_call | solution.py:321
  32.4 1.0 %pad_maximum_fusion = (f32[4,10,1024]{2,1,0:T(8,128)S(1)}, f32[4,10,1024]{2,1,0:T(8,128)S(1)}) fusion(f32[4,3,1024]{2,1,0:T(4,128)} %get-tuple-element.7, f32[4,4,1024]{2,1,0:T(4,128)} %get-tuple-element.6, f32[4,3,1024]{2,1,0:T(4,128)} %get-tuple-element.5), kind=kLoop, calls=%fused_computation.10 | loop fusion | flops 122880 | bytes 491520 | tf_op jit(solution)/shard_map/concatenate | solution.py:345
  33.5 0.2 multiply_add_fusion.1
  33.8 0.2 multiply_add_fusion
  34.1 0.8 %fusion.40.x_ref = f32[4,4,1024]{2,1,0:T(4,128)} fusion(f32[4,4,1024]{2,1,0:T(4,128)S(1)} %slice.160, f32[4,8,1024]{2,1,0:T(8,128)S(1)} %get-tuple-element.10, f32[4,10,1024]{2,1,0:T(8,128)S(1)} %get-tuple-element.13, f32[4,6,1024]{2,1,0:T(8,128)S(1)} %get-tuple-element.8, f32[4,6,1024]{2,1,0:T(8,128)S(1)} %get-tuple-element.9, ...), kind=kLoop, calls=%fused_computation.63 | loop fusion | flops 311296 | bytes 466960 | tf_op jit(solution)/shard_map/add | solution.py:495
  35.0 12.3 %shard_map.52 = f32[2,8,4,4,1024]{4,3,2,1,0:T(4,128)} custom-call(f32[4,4,1024]{2,1,0:T(4,128)} %fusion.40.x_ref), custom_call_target="tpu_custom_call" | custom-call | tf_op jit(solution)/shard_map/pallas_call | solution.py:404
  47.3 3.3 %convolution_bitcast_fusion.1 = f32[64,64]{0,1:T(8,128)S(1)} fusion(f32[64,4,1024]{2,1,0:T(4,128)} %bitcast.48), kind=kOutput, calls=%fused_computation.2 | convolution fusion | flops 100663296 | bytes 1064960 | tf_op jit(solution)/shard_map/dot_general | solution.py:566
  51.0 0.2 convert_element_type.71
  51.3 0.7 fusion.1
  52.1 0.6 pad_bitcast_fusion.x_ref
  52.8 17.8 %shard_map.53 = f32[16,17,128]{2,1,0:T(8,128)} custom-call(f32[17,128]{1,0:T(8,128)} %pad_bitcast_fusion.x_ref), custom_call_target="tpu_custom_call" | custom-call | tf_op jit(solution)/shard_map/pallas_call | solution.py:110
  70.6 1.0 %reduce_sum.29 = f32[17,128]{1,0:T(8,128)S(1)} reduce(f32[16,17,128]{2,1,0:T(8,128)} %shard_map.53, f32[]{:T(128)} %constant.56.clone.1), dimensions={0}, to_apply=%region_2.3 | reduce | flops 32640 | bytes 147972 | tf_op jit(solution)/shard_map/reduce_sum | solution.py:446
  71.9 0.7 maximum_multiply_fusion.m_ref
  72.6 0.6 slice_bitcast_fusion.b_ref
  73.2 4.9 %shard_map.54 = f32[1,64]{1,0:T(1,128)} custom-call(f32[64,64]{1,0:T(8,128)} %maximum_multiply_fusion.m_ref, f32[1,64]{1,0:T(1,128)} %slice_bitcast_fusion.b_ref), custom_call_target="tpu_custom_call" | custom-call | tf_op jit(solution)/shard_map/pallas_call | solution.py:538
  78.1 1.0 %copy.49 = f32[64,4,1024]{2,1,0:T(4,128)} copy(f32[64,4,1024]{2,1,0:T(4,128)S(1)} %bitcast.49) | data formatting | bytes 2097152
  (31 shorter events, 1.4 us)
Async XLA Ops:
  0.6 8.5 %copy-start = (bf16[1,64,4,1024]{3,2,1,0:T(4,128)(2,1)S(1)}, bf16[1,64,4,1024]{3,2,1,0:T(4,128)(2,1)}, u32[]{:S(2)}) copy-start(bf16[1,64,4,1024]{3,2,1,0:T(4,128)(2,1)} %param.3) | copy-start | bytes 1572868
  0.6 0.8 copy-start.3
  2.2 0.8 copy-start.2
  47.3 3.7 %copy-start.1 = (f32[2,8,4,4,1024]{4,3,2,1,0:T(4,128)S(1)}, f32[2,8,4,4,1024]{4,3,2,1,0:T(4,128)}, u32[]{:S(2)}) copy-start(f32[2,8,4,4,1024]{4,3,2,1,0:T(4,128)} %shard_map.52) | copy-start | bytes 3145732
